TPU v7x, 32 devices: a whole 2x2x4 slice. The times are simulated.
32 devices in a mesh: role: 4 (over y, core), tile: 8 (over z, x).
Axes of the slice: x: 2, y: 2, z: 4, core: 2. Of those that a mesh axis runs over, the one named last changes fastest.
Arguments:
- velocity: float32 [3, 32, 512, 128], P(None, 'role', 'tile'), may hold values from -5 to 5
- params: float32 [819200], replicated, may hold values from -0.36 to 0.36
- first_moment: float32 [819200], P(('role', 'tile')), may hold values from -1.8 to 1.8
- second_moment: float32 [819200], P(('role', 'tile')), may hold values from 0.02 to 2
- patch_index: int32 [65536], P(('role', 'tile')), may hold values from 0 to 1023
- patch_count: int32 [32], P(('role', 'tile')), may hold values from 1 to 2048, 16384 in all
Outputs:
- velocity_out: float32 [3, 32, 512, 128], P(None, 'role', 'tile')
- sgs_force: float32 [3, 32, 512, 128], P(None, 'role', 'tile')
- params_out: float32 [819200], replicated
- first_out: float32 [819200], P(('role', 'tile'))
- second_out: float32 [819200], P(('role', 'tile'))
Inputs may be any that keep to these rules, and one draw needn't show every extreme that they name: `patch_index`: only the first patch_count entries of a device's list are used. `patch_count`: the counts of all devices sum to 16384; the largest is 2048.
All inputs are finite; a program needn't handle non-finite values.
Results may differ from a plain program's by a relative error of at most 0.0091.
Values may be sent and summed in bfloat16 or wider, within the bound.
No kernel may reach another device: no remote copies, remote signals or barrier semaphores. Data moves between devices by JAX's collectives and lax.ppermute only.
A program may use at most 128 MiB of HBM per device.

v0:
```python
import functools

import jax
import jax.numpy as jnp
import numpy as np
from jax import lax
from jax.experimental import pallas as pl
from jax.experimental.pallas import tpu as pltpu
from jax.sharding import PartitionSpec as P

FEAT = 192
TGT = 384
HID = 512
ADAM_STEP = 100
STEP_DT = 0.1
VISCOSITY = 0.1
SGS_SCALE = 1.5
BETA_ONE = 0.9
BETA_TWO = 0.999
LEARN_RATE = 0.001
EPSILON = 1e-08
PAIRS = ((0, 0), (1, 1), (2, 2), (0, 1), (0, 2), (1, 2))
COMPONENT = ((0, 3, 4), (3, 1, 5), (4, 5, 2))

CX, CY, CZ = 8, 64, 128
NPATCH = 1024
ROWS = 6400
W1_AT = 768
W2_AT = W1_AT + 2048
WO_AT = W2_AT + 2048
BOTH = ("role", "tile")
F32, BF16 = jnp.float32, jnp.bfloat16
VMEM_LIMIT = 56 * 1024 * 1024


def row_matrix():
    matrix = np.zeros((256, 256), np.float32)
    for dx in range(4):
        for j in range(4):
            for pyl in range(4):
                for dy in range(4):
                    matrix[pyl * 64 + j * 16 + dx * 4 + dy, dx * 64 + j * 16 + pyl * 4 + dy] = 1
    return matrix


def lane_matrix():
    matrix = np.zeros((512, 512), np.float32)
    for pyl in range(4):
        for pz in range(32):
            for dz in range(4):
                matrix[pyl * 128 + pz * 4 + dz, dz * 128 + pyl * 32 + pz] = 1
    return matrix


def feature_matrix():
    matrix = np.zeros((128, 128), np.float32)
    for c in range(2):
        for off in range(16):
            for dz in range(4):
                matrix[c * 64 + off * 4 + dz, c * 64 + dz * 16 + off] = 1
    return matrix


def dot(a, b):
    return jnp.dot(a, b, preferred_element_type=F32)


def dot_tn(a, b):
    return lax.dot_general(a, b, (((0,), (0,)), ((), ())), preferred_element_type=F32)


def dot_nt(a, b):
    return lax.dot_general(a, b, (((1,), (1,)), ((), ())), preferred_element_type=F32)


def permute_features(feature_mat, x, channels):
    pieces = []
    at = 0
    while at < channels * 64:
        size = min(128, channels * 64 - at)
        pieces.append(dot(feature_mat[:size, :size], x[at : at + size]).astype(BF16))
        at += size
    return jnp.concatenate(pieces, axis=0)


def cells_to_patches(blocks, row_mat, lane_mat, feature_mat, channels):
    moved = dot(row_mat, jnp.concatenate(blocks, axis=1)).astype(BF16)
    rows = []
    for i in range(2 * channels):
        part = moved[:, i * 128 : (i + 1) * 128]
        rows.append(jnp.concatenate([part[p * 64 : (p + 1) * 64] for p in range(4)], axis=1))
    spread = dot(jnp.concatenate(rows, axis=0), lane_mat).astype(BF16)
    bands = []
    for c in range(channels):
        for dz in range(4):
            bands.append(
                jnp.concatenate(
                    [
                        spread[((c * 2 + px) * 4 + j) * 16 : ((c * 2 + px) * 4 + j) * 16 + 16, dz * 128 : dz * 128 + 128]
                        for px in range(2)
                        for j in range(4)
                    ],
                    axis=1,
                )
            )
    return permute_features(feature_mat, jnp.concatenate(bands, axis=0), channels)


def patches_to_cells(x, row_mat, lane_mat, feature_mat, channels):
    pieces = []
    for at in range(0, channels * 64, 128):
        pieces.append(dot_tn(feature_mat, x[at : at + 128]).astype(BF16))
    x = jnp.concatenate(pieces, axis=0)
    rows = []
    for c in range(channels):
        for px in range(2):
            for j in range(4):
                lanes = (px * 4 + j) * 128
                rows.append(
                    jnp.concatenate(
                        [x[c * 64 + dz * 16 : c * 64 + dz * 16 + 16, lanes : lanes + 128] for dz in range(4)], axis=1
                    )
                )
    spread = dot_nt(jnp.concatenate(rows, axis=0), lane_mat).astype(BF16)
    columns = []
    for i in range(2 * channels):
        part = spread[i * 64 : (i + 1) * 64]
        columns.append(jnp.concatenate([part[:, p * 128 : (p + 1) * 128] for p in range(4)], axis=0))
    moved = dot_tn(row_mat, jnp.concatenate(columns, axis=1))
    return [moved[:, i * 128 : (i + 1) * 128] for i in range(2 * channels)]


def load_weights(p_ref, w0, w1, w2, wo):
    for k in range(4):
        lanes = slice(k * 128, (k + 1) * 128)
        w0[:, lanes] = p_ref[pl.ds(k, FEAT, stride=4), :].astype(BF16)
        w1[:, lanes] = p_ref[pl.ds(W1_AT + k, HID, stride=4), :].astype(BF16)
        w2[:, lanes] = p_ref[pl.ds(W2_AT + k, HID, stride=4), :].astype(BF16)
    for k in range(3):
        wo[:, k * 128 : (k + 1) * 128] = p_ref[pl.ds(WO_AT + k, HID, stride=3), :].astype(BF16)


def velocity_blocks(v_ref):
    return [
        v_ref[c, px * 4 : px * 4 + 4].reshape(256, 128).astype(BF16) for c in range(3) for px in range(2)
    ]


def forward_kernel(v_ref, p_ref, row_ref, lane_ref, feat_ref, x_out, a_out, d_out, pred_out, w0, w1, w2, wo):
    load_weights(p_ref, w0, w1, w2, wo)
    x = cells_to_patches(velocity_blocks(v_ref), row_ref[...], lane_ref[...], feat_ref[...], 3)
    x_out[...] = x
    hidden = x
    for layer, w in enumerate((w0, w1, w2)):
        z = dot_tn(w[...], hidden)
        s = 0.5 * jnp.tanh(0.5 * z) + 0.5
        a = z * s
        d_out[layer] = s + a * (1.0 - s)
        hidden = a.astype(BF16)
        a_out[layer] = hidden
    pred_out[...] = dot_tn(wo[...], hidden)


def fill_padded(pad, v_ref, xlo_ref, xhi_ref, ylo_ref, yhi_ref):
    pad[:, 2:10, 8:72, :] = v_ref[...]
    pad[:, 0:2, 8:72, :] = xlo_ref[...]
    pad[:, 10:12, 8:72, :] = xhi_ref[...]
    pad[:, :, 6:8, :] = ylo_ref[...]
    pad[:, :, 72:74, :] = yhi_ref[...]


def box(field_sum):
    along = field_sum[:, 0:64] + field_sum[:, 1:65] + field_sum[:, 2:66]
    return (along + roll_z(along, 1) + roll_z(along, CZ - 1)) * (1.0 / 27.0)


def roll_z(x, by):
    return pltpu.roll(x, by, x.ndim - 1)


def stress_blocks(pad):
    out = [None] * 12
    for px in range(2):
        first = 1 + px * 4
        planes = [[pad[c, first + i, 7:73, :] for i in range(6)] for c in range(3)]
        smooth = []
        for c in range(3):
            sums = jnp.stack([planes[c][i] + planes[c][i + 1] + planes[c][i + 2] for i in range(4)])
            smooth.append(box(sums))
        for k, (a, b) in enumerate(PAIRS):
            prod = [planes[a][i] * planes[b][i] for i in range(6)]
            sums = jnp.stack([prod[i] + prod[i + 1] + prod[i + 2] for i in range(4)])
            value = box(sums) - smooth[a] * smooth[b]
            out[k * 2 + px] = value.astype(BF16).reshape(256, 128)
    return out


def multiplicity(index_ref, count_ref):
    index = index_ref[...]
    selected = index.shape[1]
    live = lax.broadcasted_iota(jnp.int32, (16, selected), 1) < count_ref[0]
    high = lax.broadcasted_iota(jnp.int32, (16, selected), 0) == (index >> 7)
    left = jnp.where(high & live, 1.0, 0.0).astype(BF16)
    low = lax.broadcasted_iota(jnp.int32, (128, selected), 0) == (index & 127)
    right = jnp.where(low, 1.0, 0.0).astype(BF16)
    return dot_nt(left, right)


def backward_kernel(row_scale, rows, in_order, order_ref, count_ref, index_ref, v_ref, xlo_ref, xhi_ref, ylo_ref, yhi_ref, p_ref, row_ref, lane_ref,
                    feat_ref, x_ref, a_ref, d_ref, pred_ref, *rest):
    if in_order:
        send_out, keep_out, pad, w0, w1, w2, wo, grads = rest
    else:
        grads, pad, w0, w1, w2, wo = rest
    load_weights(p_ref, w0, w1, w2, wo)
    weight = multiplicity(index_ref, count_ref) * row_scale
    weight = jnp.concatenate([weight[q : q + 1] for q in range(8)], axis=1)
    fill_padded(pad, v_ref, xlo_ref, xhi_ref, ylo_ref, yhi_ref)
    target = cells_to_patches(stress_blocks(pad), row_ref[...], lane_ref[...], feat_ref[...], 6)
    error = ((pred_ref[...] - target.astype(F32)) * weight).astype(BF16)
    grad = dot_nt(a_ref[2], error)
    for k in range(3):
        grads[pl.ds(WO_AT + k, HID, stride=3), :] = grad[:, k * 128 : (k + 1) * 128]
    up = dot(wo[...], error)
    for layer, at, size, w in ((2, W2_AT, HID, w2), (1, W1_AT, HID, w1), (0, 0, FEAT, None)):
        slope = (up * d_ref[layer]).astype(BF16)
        left = a_ref[layer - 1] if layer else x_ref[...]
        grad = dot_nt(left, slope)
        for k in range(4):
            grads[pl.ds(at + k, size, stride=4), :] = grad[:, k * 128 : (k + 1) * 128]
        if layer:
            up = dot(w[...], slope)
    if in_order:
        half = keep_out.shape[0]

        def place(i, carry):
            here = pl.multiple_of(order_ref[i + half] * rows, 8)
            send_out[i] = grads[pl.ds(here, rows), :].astype(BF16)
            here = pl.multiple_of(order_ref[i] * rows, 8)
            keep_out[i] = grads[pl.ds(here, rows), :]
            return carry

        lax.fori_loop(0, half, place, 0)


def substep(now, after_x, before_x, after_y, before_y):
    after_z = [roll_z(f, CZ - 1) for f in now]
    before_z = [roll_z(f, 1) for f in now]
    out = []
    for c in range(3):
        transport = now[0] * (0.5 * (after_x[c] - before_x[c]))
        transport = transport + now[1] * (0.5 * (after_y[c] - before_y[c]))
        transport = transport + now[2] * (0.5 * (after_z[c] - before_z[c]))
        laplace = after_x[c] + before_x[c] + after_y[c] + before_y[c] + after_z[c] + before_z[c] - 6.0 * now[c]
        out.append(now[c] + STEP_DT * (VISCOSITY * laplace - transport))
    return out


def flow_kernel(v_ref, xlo_ref, xhi_ref, ylo_ref, yhi_ref, row_ref, lane_ref, feat_ref, flow_out, x_out, pad, mid):
    fill_padded(pad, v_ref, xlo_ref, xhi_ref, ylo_ref, yhi_ref)
    for src, dst, first, count, low, high in ((pad, mid, 1, 10, 7, 73), (mid, flow_out, 2, 8, 8, 72)):
        for i in range(first, first + count):
            now = [src[c, i, low:high, :] for c in range(3)]
            after_x = [src[c, i + 1, low:high, :] for c in range(3)]
            before_x = [src[c, i - 1, low:high, :] for c in range(3)]
            after_y = [src[c, i, low + 1 : high + 1, :] for c in range(3)]
            before_y = [src[c, i, low - 1 : high - 1, :] for c in range(3)]
            new = substep(now, after_x, before_x, after_y, before_y)
            for c in range(3):
                if dst is mid:
                    mid[c, i, low:high, :] = new[c]
                else:
                    flow_out[c, i - 2] = new[c]
    x_out[...] = cells_to_patches(velocity_blocks(flow_out), row_ref[...], lane_ref[...], feat_ref[...], 3)


def model_kernel(rows, in_order, order_ref, p_ref, own_ref, other_ref, x_ref, row_ref, lane_ref, feat_ref, p_out, s_out, xfirst, xlast, yfirst, ylast, w0, w1, w2, wo):
    half = own_ref.shape[0]
    if in_order:

        def place(i, carry):
            here = pl.ds(pl.multiple_of(order_ref[i] * rows, 8), rows)
            p_out[here, :] = p_ref[here, :] - own_ref[i].astype(F32)
            here = pl.ds(pl.multiple_of(order_ref[i + half] * rows, 8), rows)
            p_out[here, :] = p_ref[here, :] - other_ref[i].astype(F32)
            return carry

        lax.fori_loop(0, half, place, 0)
    else:
        p_out[...] = p_ref[...] - own_ref[...].astype(F32)
    load_weights(p_out, w0, w1, w2, wo)
    hidden = x_ref[...]
    for w in (w0, w1, w2):
        z = dot_tn(w[...], hidden)
        hidden = (z * (0.5 * jnp.tanh(0.5 * z) + 0.5)).astype(BF16)
    modelled = dot_tn(wo[...], hidden).astype(BF16)
    blocks = patches_to_cells(modelled, row_ref[...], lane_ref[...], feat_ref[...], 6)
    for k in range(6):
        for px in range(2):
            s_out[k, px * 4 : px * 4 + 4] = blocks[k * 2 + px].reshape(4, 64, 128)
    for n, k in enumerate((0, 3, 4)):
        xfirst[n] = s_out[k, 0].astype(BF16)
        xlast[n] = s_out[k, CX - 1].astype(BF16)
    for n, k in enumerate((3, 1, 5)):
        yfirst[n] = s_out[k, :, 0, :].astype(BF16)
        ylast[n] = s_out[k, :, CY - 1, :].astype(BF16)


def force_kernel(s_ref, flow_ref, xlo_ref, xhi_ref, ylo_ref, yhi_ref, v_out, force_out, pad):
    pad[:, :, 8:72, :] = jnp.stack([s_ref[k] for k in (3, 1, 5)])
    pad[:, :, 7, :] = ylo_ref[...].astype(F32)
    pad[:, :, 72, :] = yhi_ref[...].astype(F32)
    for i in range(3):
        kx, kz = COMPONENT[i][0], COMPONENT[i][2]
        for x in range(CX):
            after = s_ref[kx, x + 1] if x < CX - 1 else xhi_ref[i].astype(F32)
            before = s_ref[kx, x - 1] if x else xlo_ref[i].astype(F32)
            total = 0.5 * (after - before)
            total = total + 0.5 * (pad[i, x, 9:73, :] - pad[i, x, 7:71, :])
            centre = s_ref[kz, x]
            total = total + 0.5 * (roll_z(centre, CZ - 1) - roll_z(centre, 1))
            force = -SGS_SCALE * total
            force_out[i, x] = force
            v_out[i, x] = flow_ref[i, x] + force


def call(kernel, outs, args, scratch, scalars=0, flops=0, name=None):
    vm = pl.BlockSpec(memory_space=pltpu.VMEM)
    sm = pl.BlockSpec(memory_space=pltpu.SMEM)
    size = sum(a.size * a.dtype.itemsize for a in args) + sum(int(np.prod(s)) * np.dtype(t).itemsize for s, t in outs)
    return pl.pallas_call(
        kernel,
        out_shape=[jax.ShapeDtypeStruct(s, t) for s, t in outs],
        in_specs=[sm] * scalars + [vm] * (len(args) - scalars),
        out_specs=[vm] * len(outs),
        scratch_shapes=[pltpu.VMEM(s, t) for s, t in scratch],
        compiler_params=pltpu.CompilerParams(vmem_limit_bytes=VMEM_LIMIT),
        cost_estimate=pl.CostEstimate(flops=flops, transcendentals=0, bytes_accessed=size),
        name=name,
    )(*args)


WEIGHTS = [((FEAT, HID), BF16), ((HID, HID), BF16), ((HID, HID), BF16), ((HID, TGT), BF16)]
PADDED = ((3, 12, 80, 128), F32)


def bits(size):
    return [1 << i for i in range(size.bit_length() - 1)]


def stage_masks(n_role, n_tile):
    role = [n_tile * b for b in bits(n_role)]
    tile = bits(n_tile)
    rest = tile[:1] + role[1:] + tile[1:]
    other = rest[1::-1] + rest[2:]
    return role[:1] + rest, role[:1] + other


def shifts(axis):
    size = lax.axis_size(axis)
    up = [(i, (i + 1) % size) for i in range(size)]
    return up, [(j, i) for i, j in up]


def local(velocity, params, first_moment, second_moment, patch_index, patch_count):
    n_role, n_tile = lax.axis_size("role"), lax.axis_size("tile")
    devices = n_role * n_tile
    own_rank = lax.axis_index(BOTH)
    rows = ROWS // devices
    in_order = rows % 8 == 0
    masks = stage_masks(n_role, n_tile)
    steps = len(masks[0])
    core_of = [(d // n_tile) & 1 for d in range(devices)]

    def exchange(x, step):
        pairs = [(d, d ^ masks[core_of[d]][step]) for d in range(devices)]
        return lax.ppermute(x, BOTH, pairs)

    def offsets(core):
        return [
            functools.reduce(lambda a, b: a ^ b, [masks[core][i] if (j >> (steps - 1 - i)) & 1 else 0 for i in range(steps)])
            for j in range(devices)
        ]

    half = devices // 2
    both = [offsets(0), offsets(1)]
    table = np.array([both[c][:half] + both[1 - c][half:] for c in range(2)], np.int32)
    order = own_rank ^ jnp.where((own_rank // n_tile) % 2 == 0, table[0], table[1])

    row_mat, lane_mat, feat_mat = (jnp.asarray(m, BF16) for m in (row_matrix(), lane_matrix(), feature_matrix()))
    mats = [row_mat, lane_mat, feat_mat]
    p2 = params.reshape(ROWS, 128)
    selected = patch_index.shape[0]
    row_scale = 1.0 / (selected // 4)

    up, down = shifts("role")
    xlo = lax.ppermute(velocity[:, CX - 2 :], "role", up)
    xhi = lax.ppermute(velocity[:, :2], "role", down)
    x, act, slope, pred = call(
        forward_kernel,
        [((FEAT, NPATCH), BF16), ((3, HID, NPATCH), BF16), ((3, HID, NPATCH), F32), ((TGT, NPATCH), F32)],
        [velocity, p2] + mats,
        WEIGHTS,
        flops=2 * 819200 * NPATCH,
        name="forward",
    )
    up, down = shifts("tile")
    last = jnp.concatenate([xlo[:, :, CY - 2 :], velocity[:, :, CY - 2 :], xhi[:, :, CY - 2 :]], axis=1)
    first = jnp.concatenate([xlo[:, :, :2], velocity[:, :, :2], xhi[:, :, :2]], axis=1)
    ylo = lax.ppermute(last, "tile", up)
    yhi = lax.ppermute(first, "tile", down)
    halos = [xlo, xhi, ylo, yhi]

    grad_outs = [((half, rows, 128), BF16), ((half, rows, 128), F32)] if in_order else [((ROWS, 128), F32)]
    grads = call(
        functools.partial(backward_kernel, row_scale, rows, in_order),
        grad_outs,
        [order, patch_count, patch_index.reshape(1, selected), velocity] + halos + [p2] + mats + [x, act, slope, pred],
        [PADDED] + WEIGHTS + ([((ROWS, 128), F32)] if in_order else []),
        scalars=2,
        flops=4 * 819200 * NPATCH,
        name="backward",
    )
    if in_order:
        send, keep = grads
    else:
        placed = grads[0].reshape(devices, rows, 128)[order]
        send, keep = placed[half:].astype(BF16), placed[:half]

    got = exchange(send, 0)
    flow, x_new = call(
        flow_kernel,
        [((3, CX, CY, CZ), F32), ((FEAT, NPATCH), BF16)],
        [velocity] + halos + mats,
        [PADDED, PADDED],
        flops=1 << 30,
        name="flow",
    )
    size = half
    for step in range(1, steps):
        size //= 2
        send = (keep[size:] + got[size:].astype(F32)).astype(BF16)
        keep = keep[:size] + got[:size].astype(F32)
        got = exchange(send, step)
    grad = (keep + got.astype(F32)).reshape(-1)
    first_out = BETA_ONE * first_moment + (1.0 - BETA_ONE) * grad
    second_out = BETA_TWO * second_moment + (1.0 - BETA_TWO) * grad * grad
    fix_first = 1.0 - BETA_ONE**ADAM_STEP
    fix_second = 1.0 - BETA_TWO**ADAM_STEP
    update = LEARN_RATE * (first_out / fix_first) / (jnp.sqrt(second_out / fix_second) + EPSILON)
    held = update.astype(BF16).reshape(1, rows, 128)
    for step in range(steps - 1, 0, -1):
        held = jnp.concatenate([held, exchange(held, step)], axis=0)
    other = exchange(held, 0)
    if not in_order:
        slots = jnp.zeros((devices,), jnp.int32).at[order].set(jnp.arange(devices, dtype=jnp.int32))
        held = other = jnp.concatenate([held, other], axis=0)[slots].reshape(ROWS, 128)

    p_new, stress, xfirst, xlast, yfirst, ylast = call(
        functools.partial(model_kernel, rows, in_order),
        [((ROWS, 128), F32), ((6, CX, CY, CZ), F32)] + [((3, CY, CZ), BF16)] * 2 + [((3, CX, CZ), BF16)] * 2,
        [order, p2, held, other, x_new] + mats,
        WEIGHTS,
        scalars=1,
        flops=2 * 819200 * NPATCH,
        name="model",
    )
    up, down = shifts("role")
    sxlo = lax.ppermute(xlast, "role", up)
    sxhi = lax.ppermute(xfirst, "role", down)
    up, down = shifts("tile")
    sylo = lax.ppermute(ylast, "tile", up)
    syhi = lax.ppermute(yfirst, "tile", down)
    velocity_out, sgs_force = call(
        force_kernel,
        [((3, CX, CY, CZ), F32)] * 2,
        [stress, flow, sxlo, sxhi, sylo, syhi],
        [((3, CX, 80, CZ), F32)],
        name="force",
    )
    return (velocity_out, sgs_force, p_new.reshape(-1), first_out, second_out)


def solution(mesh):
    placed = (
        P(None, "role", "tile", None),
        P(),
        P(BOTH),
        P(BOTH),
        P(BOTH),
        P(BOTH),
    )
    return jax.shard_map(
        local,
        mesh=mesh,
        in_specs=placed,
        out_specs=(
            P(None, "role", "tile", None),
            P(None, "role", "tile", None),
            P(),
            P(BOTH),
            P(BOTH),
        ),
        check_vma=False,
    )
```

profile of v0, /device:TPU:0, one launch (start us, length us, event | category | flops | bytes accessed | tf_op | source)
XLA Modules:
  0.0 119.5 jit_solution(3680906006885866806)
XLA Ops:
  2.2 2.0 %collective-permute-start.1 = (f32[3,2,64,128]{3,2,1,0:T(8,128)S(1)}, f32[3,2,64,128]{3,2,1,0:T(8,128)S(1)}, u32[]{:S(2)}, u32[]{:S(2)}) collective-permute-start(f32[3,2,64,128]{3,2,1,0:T(8,128)S(1)} %get-tuple-element.47), channel_id=1, source_target_pairs={{8,0},{16,8},{24,16},{0,24},{9,1},{17,9},{25,17},{1,25},{10,2},{18... | collective-permute-start | bytes 589832 | tf_op jit(solution)/shard_map/ppermute | solution.py:398
  7.5 1.9 %collective-permute-done.1.xhi_ref = f32[3,2,64,128]{3,2,1,0:T(8,128)S(1)} collective-permute-done((f32[3,2,64,128]{3,2,1,0:T(8,128)S(1)}, f32[3,2,64,128]{3,2,1,0:T(8,128)S(1)}, u32[]{:S(2)}, u32[]{:S(2)}) %collective-permute-start.1) | collective-permute-done | bytes 196640 | tf_op jit(solution)/shard_map/ppermute | solution.py:398
  9.5 4.6 %collective-permute-start.3 = (f32[3,12,2,128]{3,2,1,0:T(2,128)S(1)}, f32[3,12,2,128]{3,2,1,0:T(2,128)S(1)}, u32[]{:S(2)}, u32[]{:S(2)}) collective-permute-start(f32[3,12,2,128]{3,2,1,0:T(2,128)S(1)} %pad_maximum_fusion.4), channel_id=1, source_target_pairs={{1,0},{2,1},{3,2},{4,3},{5,4},{6,5},{7,6},{0,7},{9,8},{10,9},{11,1... | collective-permute-start | bytes 110600 | tf_op jit(solution)/shard_map/ppermute | solution.py:411
  14.1 9.8 %forward.1 = (bf16[192,1024]{1,0:T(8,128)(2,1)}, bf16[3,512,1024]{2,1,0:T(8,128)(2,1)}, f32[3,512,1024]{2,1,0:T(8,128)}, f32[384,1024]{1,0:T(8,128)}) custom-call(f32[3,8,64,128]{3,2,1,0:T(8,128)} %v_ref.5, f32[6400,128]{1,0:T(8,128)} %bitcast.14, bf16[256,256]{1,0:T(8,128)(2,1)} %constant.66.clone.row_ref, bf16[512,512]{1,0:T(8,128)(2,1)} %constant.67.clone.lane_ref, ...), custom_call_target="tpu_custom_call" | custom-call | flops 1677721600 | bytes 16154624 | tf_op jit(solution)/shard_map/forward/pallas_call | solution.py:331
  25.2 13.5 %backward.1 = (bf16[16,200,128]{2,1,0:T(8,128)(2,1)}, f32[16,200,128]{2,1,0:T(8,128)}) custom-call(s32[32]{0:T(128)} %fusion.7.order_ref, s32[1]{0:T(128)S(6)} %copy.20.count_ref, s32[1,2048]{1,0:T(1,128)} %bitcast.17, f32[3,8,64,128]{3,2,1,0:T(8,128)} %v_ref.5, f32[3,2,64,128]{3,2,1,0:T(8,128)} %copy-done, f32[3,2,64,128]{3,2,1,0:T(8,128)} %copy-done.1, ...), custom_call_target="tpu_custom_call" | custom-call | flops 3355443200 | bytes 19087492 | tf_op jit(solution)/shard_map/backward/pallas_call | solution.py:331
  39.3 2.2 %collective-permute-done.4 = bf16[16,200,128]{2,1,0:T(8,128)(2,1)S(1)} collective-permute-done((bf16[16,200,128]{2,1,0:T(8,128)(2,1)}, bf16[16,200,128]{2,1,0:T(8,128)(2,1)S(1)}, u32[]{:S(2)}, u32[]{:S(2)}) %collective-permute-start.4) | collective-permute-done | bytes 819232 | tf_op jit(solution)/shard_map/ppermute | solution.py:377
  41.5 1.6 %add_convert_fusion = (bf16[8,200,128]{2,1,0:T(8,128)(2,1)S(1)}, f32[8,200,128]{2,1,0:T(8,128)S(1)}) fusion(f32[16,200,128]{2,1,0:T(8,128)} %get-tuple-element.25, bf16[16,200,128]{2,1,0:T(8,128)(2,1)S(1)} %collective-permute-done.4), kind=kLoop, calls=%fused_computation | loop fusion | flops 1024000 | bytes 3686400 | tf_op jit(solution)/shard_map/convert_element_type | solution.py:442
  43.2 7.9 %collective-permute-done.5 = bf16[8,200,128]{2,1,0:T(8,128)(2,1)S(1)} collective-permute-done((bf16[8,200,128]{2,1,0:T(8,128)(2,1)S(1)}, bf16[8,200,128]{2,1,0:T(8,128)(2,1)S(1)}, u32[]{:S(2)}, u32[]{:S(2)}) %collective-permute-start.5) | collective-permute-done | bytes 409632 | tf_op jit(solution)/shard_map/ppermute | solution.py:377
  51.2 1.7 %collective-permute-start.6 = (bf16[4,200,128]{2,1,0:T(8,128)(2,1)S(1)}, bf16[4,200,128]{2,1,0:T(8,128)(2,1)S(1)}, u32[]{:S(2)}, u32[]{:S(2)}) collective-permute-start(bf16[4,200,128]{2,1,0:T(8,128)(2,1)S(1)} %get-tuple-element.43), channel_id=1, source_target_pairs={{0,16},{1,17},{2,18},{3,19},{4,20},{5,21},{6,22},{7,23},{8,9},{9,8... | collective-permute-start | bytes 614408 | tf_op jit(solution)/shard_map/ppermute | solution.py:377
  52.9 4.2 %collective-permute-done.6 = bf16[4,200,128]{2,1,0:T(8,128)(2,1)S(1)} collective-permute-done((bf16[4,200,128]{2,1,0:T(8,128)(2,1)S(1)}, bf16[4,200,128]{2,1,0:T(8,128)(2,1)S(1)}, u32[]{:S(2)}, u32[]{:S(2)}) %collective-permute-start.6) | collective-permute-done | bytes 204832 | tf_op jit(solution)/shard_map/ppermute | solution.py:377
  57.1 4.6 %collective-permute-done.7 = bf16[2,200,128]{2,1,0:T(8,128)(2,1)S(1)} collective-permute-done((bf16[2,200,128]{2,1,0:T(8,128)(2,1)S(1)}, bf16[2,200,128]{2,1,0:T(8,128)(2,1)S(1)}, u32[]{:S(2)}, u32[]{:S(2)}) %collective-permute-start.7) | collective-permute-done | bytes 102432 | tf_op jit(solution)/shard_map/ppermute | solution.py:377
  61.8 1.7 %collective-permute-start.8 = (bf16[1,200,128]{2,1,0:T(8,128)(2,1)S(1)}, bf16[1,200,128]{2,1,0:T(8,128)(2,1)S(1)}, u32[]{:S(2)}, u32[]{:S(2)}) collective-permute-start(bf16[1,200,128]{2,1,0:T(8,128)(2,1)S(1)} %fusion.3), channel_id=1, source_target_pairs={{0,4},{1,5},{2,6},{3,7},{4,0},{5,1},{6,2},{7,3},{8,12},{9,13},{10,... | collective-permute-start | bytes 153608 | tf_op jit(solution)/shard_map/ppermute | solution.py:377
  63.5 3.9 %collective-permute-done.8 = bf16[1,200,128]{2,1,0:T(8,128)(2,1)S(1)} collective-permute-done((bf16[1,200,128]{2,1,0:T(8,128)(2,1)S(1)}, bf16[1,200,128]{2,1,0:T(8,128)(2,1)S(1)}, u32[]{:S(2)}, u32[]{:S(2)}) %collective-permute-start.8) | collective-permute-done | bytes 51232 | tf_op jit(solution)/shard_map/ppermute | solution.py:377
  69.3 4.3 %collective-permute-done.9 = bf16[1,200,128]{2,1,0:T(8,128)(2,1)S(1)} collective-permute-done((bf16[1,200,128]{2,1,0:T(8,128)(2,1)S(1)}, bf16[1,200,128]{2,1,0:T(8,128)(2,1)S(1)}, u32[]{:S(2)}, u32[]{:S(2)}) %collective-permute-start.9) | collective-permute-done | bytes 51232 | tf_op jit(solution)/shard_map/ppermute | solution.py:377
  74.1 4.2 %collective-permute-done.10 = bf16[2,200,128]{2,1,0:T(8,128)(2,1)S(1)} collective-permute-done((bf16[2,200,128]{2,1,0:T(8,128)(2,1)S(1)}, bf16[2,200,128]{2,1,0:T(8,128)(2,1)S(1)}, u32[]{:S(2)}, u32[]{:S(2)}) %collective-permute-start.10) | collective-permute-done | bytes 102432 | tf_op jit(solution)/shard_map/ppermute | solution.py:377
  78.4 1.7 %collective-permute-start.11 = (bf16[4,200,128]{2,1,0:T(8,128)(2,1)S(1)}, bf16[4,200,128]{2,1,0:T(8,128)(2,1)S(1)}, u32[]{:S(2)}, u32[]{:S(2)}) collective-permute-start(bf16[4,200,128]{2,1,0:T(8,128)(2,1)S(1)} %pad_maximum_fusion.1), channel_id=1, source_target_pairs={{0,16},{1,17},{2,18},{3,19},{4,20},{5,21},{6,22},{7,23},{8,9},{9,8... | collective-permute-start | bytes 614408 | tf_op jit(solution)/shard_map/ppermute | solution.py:377
  80.1 5.7 %collective-permute-done.11 = bf16[4,200,128]{2,1,0:T(8,128)(2,1)S(1)} collective-permute-done((bf16[4,200,128]{2,1,0:T(8,128)(2,1)S(1)}, bf16[4,200,128]{2,1,0:T(8,128)(2,1)S(1)}, u32[]{:S(2)}, u32[]{:S(2)}) %collective-permute-start.11) | collective-permute-done | bytes 204832 | tf_op jit(solution)/shard_map/ppermute | solution.py:377
  87.0 6.9 %collective-permute-done.12 = bf16[8,200,128]{2,1,0:T(8,128)(2,1)S(1)} collective-permute-done((bf16[8,200,128]{2,1,0:T(8,128)(2,1)S(1)}, bf16[8,200,128]{2,1,0:T(8,128)(2,1)S(1)}, u32[]{:S(2)}, u32[]{:S(2)}) %collective-permute-start.12) | collective-permute-done | bytes 409632 | tf_op jit(solution)/shard_map/ppermute | solution.py:377
  94.1 4.6 %flow.1 = (f32[3,8,64,128]{3,2,1,0:T(8,128)}, bf16[192,1024]{1,0:T(8,128)(2,1)}) custom-call(f32[3,8,64,128]{3,2,1,0:T(8,128)} %v_ref.5, f32[3,2,64,128]{3,2,1,0:T(8,128)} %copy-done, f32[3,2,64,128]{3,2,1,0:T(8,128)} %copy-done.1, f32[3,12,2,128]{3,2,1,0:T(2,128)} %copy-done.7, f32[3,12,2,128]{3,2,1,0:T(2,128)} %copy-done.6, ...), custom_call_target="tpu_custom_call" | custom-call | flops 1073741824 | bytes 3121152 | tf_op jit(solution)/shard_map/flow/pallas_call | solution.py:331
  99.6 7.7 %model.1 = (f32[6400,128]{1,0:T(8,128)}, f32[6,8,64,128]{3,2,1,0:T(8,128)}, bf16[3,64,128]{2,1,0:T(8,128)(2,1)}, bf16[3,64,128]{2,1,0:T(8,128)(2,1)}, bf16[3,8,1...) custom-call(s32[32]{0:T(128)} %fusion.7.order_ref, f32[6400,128]{1,0:T(8,128)} %bitcast.16, ...), custom_call_target="tpu_custom_call" | custom-call | flops 1677721600 | bytes 10956928 | tf_op jit(solution)/shard_map/model/pallas_call | solution.py:331
  107.6 1.5 %collective-permute-start.15 = (bf16[3,64,128]{2,1,0:T(8,128)(2,1)}, bf16[3,64,128]{2,1,0:T(8,128)(2,1)S(1)}, u32[]{:S(2)}, u32[]{:S(2)}) collective-permute-start(bf16[3,64,128]{2,1,0:T(8,128)(2,1)} %get-tuple-element.31), channel_id=1, source_target_pairs={{8,0},{16,8},{24,16},{0,24},{9,1},{17,9},{25,17},{1,25},{10,2},{18... | collective-permute-start | bytes 147464 | tf_op jit(solution)/shard_map/ppermute | solution.py:470
  110.0 3.8 %collective-permute-start.17 = (bf16[3,8,128]{2,1,0:T(8,128)(2,1)}, bf16[3,8,128]{2,1,0:T(8,128)(2,1)S(1)}, u32[]{:S(2)}, u32[]{:S(2)}) collective-permute-start(bf16[3,8,128]{2,1,0:T(8,128)(2,1)} %get-tuple-element.33), channel_id=1, source_target_pairs={{1,0},{2,1},{3,2},{4,3},{5,4},{6,5},{7,6},{0,7},{9,8},{10,9},{11,1... | collective-permute-start | bytes 18440 | tf_op jit(solution)/shard_map/ppermute | solution.py:473
  113.8 1.8 %collective-permute-done.16.ylo_ref = bf16[3,8,128]{2,1,0:T(8,128)(2,1)S(1)} collective-permute-done((bf16[3,8,128]{2,1,0:T(8,128)(2,1)}, bf16[3,8,128]{2,1,0:T(8,128)(2,1)S(1)}, u32[]{:S(2)}, u32[]{:S(2)}) %collective-permute-start.16) | collective-permute-done | bytes 6176 | tf_op jit(solution)/shard_map/ppermute | solution.py:472
  116.2 3.3 %force.1 = (f32[3,8,64,128]{3,2,1,0:T(8,128)}, f32[3,8,64,128]{3,2,1,0:T(8,128)}) custom-call(f32[6,8,64,128]{3,2,1,0:T(8,128)} %get-tuple-element.28.s_ref, f32[3,8,64,128]{3,2,1,0:T(8,128)} %get-tuple-element.29.flow_ref, bf16[3,64,128]{2,1,0:T(8,128)(2,1)} %copy-done.4, bf16[3,64,128]{2,1,0:T(8,128)(2,1)} %copy-done.5, bf16[3,8,128]{2,1,0:T(8,128)(2,1)} %copy-done.8, ...), custom_call_target="tpu_custom_call" | custom-call | bytes 4042752 | tf_op jit(solution)/shard_map/force/pallas_call | solution.py:331
  (60 shorter events, 12.7 us)
Async XLA Ops:
  1.7 5.8 %collective-permute-start = (f32[3,2,64,128]{3,2,1,0:T(8,128)S(1)}, f32[3,2,64,128]{3,2,1,0:T(8,128)S(1)}, u32[]{:S(2)}, u32[]{:S(2)}) collective-permute-start(f32[3,2,64,128]{3,2,1,0:T(8,128)S(1)} %get-tuple-element.48), channel_id=1, source_target_pairs={{0,8},{8,16},{16,24},{24,0},{1,9},{9,17},{17,25},{25,1},{2,10},{10... | collective-permute-start | bytes 589832 | tf_op jit(solution)/shard_map/ppermute | solution.py:397
  2.2 7.2 %collective-permute-start.1 = (f32[3,2,64,128]{3,2,1,0:T(8,128)S(1)}, f32[3,2,64,128]{3,2,1,0:T(8,128)S(1)}, u32[]{:S(2)}, u32[]{:S(2)}) collective-permute-start(f32[3,2,64,128]{3,2,1,0:T(8,128)S(1)} %get-tuple-element.47), channel_id=1, source_target_pairs={{8,0},{16,8},{24,16},{0,24},{9,1},{17,9},{25,17},{1,25},{10,2},{18... | collective-permute-start | bytes 589832 | tf_op jit(solution)/shard_map/ppermute | solution.py:398
  7.5 16.4 %copy-start = (f32[3,2,64,128]{3,2,1,0:T(8,128)}, f32[3,2,64,128]{3,2,1,0:T(8,128)S(1)}, u32[]{:S(2)}) copy-start(f32[3,2,64,128]{3,2,1,0:T(8,128)S(1)} %collective-permute-done.xlo_ref) | copy-start | bytes 589828
  9.4 14.5 %copy-start.1 = (f32[3,2,64,128]{3,2,1,0:T(8,128)}, f32[3,2,64,128]{3,2,1,0:T(8,128)S(1)}, u32[]{:S(2)}) copy-start(f32[3,2,64,128]{3,2,1,0:T(8,128)S(1)} %collective-permute-done.1.xhi_ref) | copy-start | bytes 589828
  9.5 15.1 %collective-permute-start.3 = (f32[3,12,2,128]{3,2,1,0:T(2,128)S(1)}, f32[3,12,2,128]{3,2,1,0:T(2,128)S(1)}, u32[]{:S(2)}, u32[]{:S(2)}) collective-permute-start(f32[3,12,2,128]{3,2,1,0:T(2,128)S(1)} %pad_maximum_fusion.4), channel_id=1, source_target_pairs={{1,0},{2,1},{3,2},{4,3},{5,4},{6,5},{7,6},{0,7},{9,8},{10,9},{11,1... | collective-permute-start | bytes 110600 | tf_op jit(solution)/shard_map/ppermute | solution.py:411
  14.1 10.6 %collective-permute-start.2 = (f32[3,12,2,128]{3,2,1,0:T(2,128)S(1)}, f32[3,12,2,128]{3,2,1,0:T(2,128)S(1)}, u32[]{:S(2)}, u32[]{:S(2)}) collective-permute-start(f32[3,12,2,128]{3,2,1,0:T(2,128)S(1)} %pad_maximum_fusion.3), channel_id=1, source_target_pairs={{0,1},{1,2},{2,3},{3,4},{4,5},{5,6},{6,7},{7,0},{8,9},{9,10},{10,1... | collective-permute-start | bytes 110600 | tf_op jit(solution)/shard_map/ppermute | solution.py:410
  38.8 2.7 %collective-permute-start.4 = (bf16[16,200,128]{2,1,0:T(8,128)(2,1)}, bf16[16,200,128]{2,1,0:T(8,128)(2,1)S(1)}, u32[]{:S(2)}, u32[]{:S(2)}) collective-permute-start(bf16[16,200,128]{2,1,0:T(8,128)(2,1)} %get-tuple-element.26), channel_id=1, source_target_pairs={{0,8},{1,9},{2,10},{3,11},{4,12},{5,13},{6,14},{7,15},{8,0},{9,1},... | collective-permute-start | bytes 2457608 | tf_op jit(solution)/shard_map/ppermute | solution.py:377
  41.5 26.0 %copy-start.2 = (f32[25600]{0:T(1024)S(1)}, f32[25600]{0:T(1024)}, u32[]{:S(2)}) copy-start(f32[25600]{0:T(1024)} %param.13) | copy-start | bytes 307204
  41.5 26.0 %copy-start.3 = (f32[25600]{0:T(1024)S(1)}, f32[25600]{0:T(1024)}, u32[]{:S(2)}) copy-start(f32[25600]{0:T(1024)} %param.14) | copy-start | bytes 307204
  43.1 8.0 %collective-permute-start.5 = (bf16[8,200,128]{2,1,0:T(8,128)(2,1)S(1)}, bf16[8,200,128]{2,1,0:T(8,128)(2,1)S(1)}, u32[]{:S(2)}, u32[]{:S(2)}) collective-permute-start(bf16[8,200,128]{2,1,0:T(8,128)(2,1)S(1)} %get-tuple-element.41), channel_id=1, source_target_pairs={{0,1},{1,0},{2,3},{3,2},{4,5},{5,4},{6,7},{7,6},{8,24},{9,25},{10,... | collective-permute-start | bytes 1228808 | tf_op jit(solution)/shard_map/ppermute | solution.py:377
  51.2 5.8 %collective-permute-start.6 = (bf16[4,200,128]{2,1,0:T(8,128)(2,1)S(1)}, bf16[4,200,128]{2,1,0:T(8,128)(2,1)S(1)}, u32[]{:S(2)}, u32[]{:S(2)}) collective-permute-start(bf16[4,200,128]{2,1,0:T(8,128)(2,1)S(1)} %get-tuple-element.43), channel_id=1, source_target_pairs={{0,16},{1,17},{2,18},{3,19},{4,20},{5,21},{6,22},{7,23},{8,9},{9,8... | collective-permute-start | bytes 614408 | tf_op jit(solution)/shard_map/ppermute | solution.py:377
  57.1 4.7 %collective-permute-start.7 = (bf16[2,200,128]{2,1,0:T(8,128)(2,1)S(1)}, bf16[2,200,128]{2,1,0:T(8,128)(2,1)S(1)}, u32[]{:S(2)}, u32[]{:S(2)}) collective-permute-start(bf16[2,200,128]{2,1,0:T(8,128)(2,1)S(1)} %get-tuple-element.49), channel_id=1, source_target_pairs={{0,2},{1,3},{2,0},{3,1},{4,6},{5,7},{6,4},{7,5},{8,10},{9,11},{10,... | collective-permute-start | bytes 307208 | tf_op jit(solution)/shard_map/ppermute | solution.py:377
  61.8 5.6 %collective-permute-start.8 = (bf16[1,200,128]{2,1,0:T(8,128)(2,1)S(1)}, bf16[1,200,128]{2,1,0:T(8,128)(2,1)S(1)}, u32[]{:S(2)}, u32[]{:S(2)}) collective-permute-start(bf16[1,200,128]{2,1,0:T(8,128)(2,1)S(1)} %fusion.3), channel_id=1, source_target_pairs={{0,4},{1,5},{2,6},{3,7},{4,0},{5,1},{6,2},{7,3},{8,12},{9,13},{10,... | collective-permute-start | bytes 153608 | tf_op jit(solution)/shard_map/ppermute | solution.py:377
  68.2 5.4 %collective-permute-start.9 = (bf16[1,200,128]{2,1,0:T(8,128)(2,1)S(1)}, bf16[1,200,128]{2,1,0:T(8,128)(2,1)S(1)}, u32[]{:S(2)}, u32[]{:S(2)}) collective-permute-start(bf16[1,200,128]{2,1,0:T(8,128)(2,1)S(1)} %get-tuple-element.38), channel_id=1, source_target_pairs={{0,4},{1,5},{2,6},{3,7},{4,0},{5,1},{6,2},{7,3},{8,12},{9,13},{10,... | collective-permute-start | bytes 153608 | tf_op jit(solution)/shard_map/ppermute | solution.py:377
  73.6 4.7 %collective-permute-start.10 = (bf16[2,200,128]{2,1,0:T(8,128)(2,1)S(1)}, bf16[2,200,128]{2,1,0:T(8,128)(2,1)S(1)}, u32[]{:S(2)}, u32[]{:S(2)}) collective-permute-start(bf16[2,200,128]{2,1,0:T(8,128)(2,1)S(1)} %pad_maximum_fusion.2), channel_id=1, source_target_pairs={{0,2},{1,3},{2,0},{3,1},{4,6},{5,7},{6,4},{7,5},{8,10},{9,11},{10,... | collective-permute-start | bytes 307208 | tf_op jit(solution)/shard_map/ppermute | solution.py:377
  78.4 7.5 %collective-permute-start.11 = (bf16[4,200,128]{2,1,0:T(8,128)(2,1)S(1)}, bf16[4,200,128]{2,1,0:T(8,128)(2,1)S(1)}, u32[]{:S(2)}, u32[]{:S(2)}) collective-permute-start(bf16[4,200,128]{2,1,0:T(8,128)(2,1)S(1)} %pad_maximum_fusion.1), channel_id=1, source_target_pairs={{0,16},{1,17},{2,18},{3,19},{4,20},{5,21},{6,22},{7,23},{8,9},{9,8... | collective-permute-start | bytes 614408 | tf_op jit(solution)/shard_map/ppermute | solution.py:377
  85.9 8.0 %collective-permute-start.12 = (bf16[8,200,128]{2,1,0:T(8,128)(2,1)S(1)}, bf16[8,200,128]{2,1,0:T(8,128)(2,1)S(1)}, u32[]{:S(2)}, u32[]{:S(2)}) collective-permute-start(bf16[8,200,128]{2,1,0:T(8,128)(2,1)S(1)} %pad_maximum_fusion), channel_id=1, source_target_pairs={{0,1},{1,0},{2,3},{3,2},{4,5},{5,4},{6,7},{7,6},{8,24},{9,25},{10,... | collective-permute-start | bytes 1228808 | tf_op jit(solution)/shard_map/ppermute | solution.py:377
  94.0 4.7 %copy-start.10 = (bf16[16,200,128]{2,1,0:T(8,128)(2,1)}, bf16[16,200,128]{2,1,0:T(8,128)(2,1)S(1)}, u32[]{:S(2)}) copy-start(bf16[16,200,128]{2,1,0:T(8,128)(2,1)S(1)} %constant_dynamic-update-slice_fusion.own_ref) | copy-start | bytes 2457604
  94.0 4.7 %collective-permute-start.13 = (bf16[16,200,128]{2,1,0:T(8,128)(2,1)S(1)}, bf16[16,200,128]{2,1,0:T(8,128)(2,1)S(1)}, u32[]{:S(2)}, u32[]{:S(2)}) collective-permute-start(bf16[16,200,128]{2,1,0:T(8,128)(2,1)S(1)} %constant_dynamic-update-slice_fusion.own_ref), channel_id=1, source_target_pairs={{0,8},{1,9},{2,10},{3,11},{4,12},{5,13},{6,14},{7,15},{8,0},{9,1},... | collective-permute-start | bytes 2457608 | tf_op jit(solution)/shard_map/ppermute | solution.py:377
  98.7 0.9 copy-start.11
  107.3 8.3 %collective-permute-start.14 = (bf16[3,64,128]{2,1,0:T(8,128)(2,1)}, bf16[3,64,128]{2,1,0:T(8,128)(2,1)S(1)}, u32[]{:S(2)}, u32[]{:S(2)}) collective-permute-start(bf16[3,64,128]{2,1,0:T(8,128)(2,1)} %get-tuple-element.30), channel_id=1, source_target_pairs={{0,8},{8,16},{16,24},{24,0},{1,9},{9,17},{17,25},{25,1},{2,10},{10... | collective-permute-start | bytes 147464 | tf_op jit(solution)/shard_map/ppermute | solution.py:469
  107.6 8.0 %collective-permute-start.15 = (bf16[3,64,128]{2,1,0:T(8,128)(2,1)}, bf16[3,64,128]{2,1,0:T(8,128)(2,1)S(1)}, u32[]{:S(2)}, u32[]{:S(2)}) collective-permute-start(bf16[3,64,128]{2,1,0:T(8,128)(2,1)} %get-tuple-element.31), channel_id=1, source_target_pairs={{8,0},{16,8},{24,16},{0,24},{9,1},{17,9},{25,17},{1,25},{10,2},{18... | collective-permute-start | bytes 147464 | tf_op jit(solution)/shard_map/ppermute | solution.py:470
  109.1 6.5 %collective-permute-start.16 = (bf16[3,8,128]{2,1,0:T(8,128)(2,1)}, bf16[3,8,128]{2,1,0:T(8,128)(2,1)S(1)}, u32[]{:S(2)}, u32[]{:S(2)}) collective-permute-start(bf16[3,8,128]{2,1,0:T(8,128)(2,1)} %get-tuple-element.32), channel_id=1, source_target_pairs={{0,1},{1,2},{2,3},{3,4},{4,5},{5,6},{6,7},{7,0},{8,9},{9,10},{10,1... | collective-permute-start | bytes 18440 | tf_op jit(solution)/shard_map/ppermute | solution.py:472
  110.0 5.6 %collective-permute-start.17 = (bf16[3,8,128]{2,1,0:T(8,128)(2,1)}, bf16[3,8,128]{2,1,0:T(8,128)(2,1)S(1)}, u32[]{:S(2)}, u32[]{:S(2)}) collective-permute-start(bf16[3,8,128]{2,1,0:T(8,128)(2,1)} %get-tuple-element.33), channel_id=1, source_target_pairs={{1,0},{2,1},{3,2},{4,3},{5,4},{6,5},{7,6},{0,7},{9,8},{10,9},{11,1... | collective-permute-start | bytes 18440 | tf_op jit(solution)/shard_map/ppermute | solution.py:473
  (6 other events, 3.6 us)
where the time goes:
time: 120 us
  waiting for transfers between devices  48.9 us (41%)
  Pallas kernels  38.9 us (32%)
  starting transfers between devices  22.1 us (18%)
  local copies, waits for them, and re-layouts  4.27 us (4%)
  other arithmetic  3.81 us (3%)
  between operations  1.49 us (1%)
    ppermute x10, waiting for transfers between devices, exchange(): return lax.ppermute(x, BOTH, pairs)  44.1 us
    pallas_call x5, Pallas kernels, call(): pl.pallas_call(kernel, out_shape=[jax.ShapeDtypeStruct(s, t) for s, t in...  38.9 us
    ppermute x10, starting transfers between devices, exchange(): return lax.ppermute(x, BOTH, pairs)  8.43 us
    ppermute x1, starting transfers between devices, local(): yhi = lax.ppermute(first, 'tile', down)  4.58 us
    ppermute x1, starting transfers between devices, local(): syhi = lax.ppermute(yfirst, 'tile', down)  3.82 us
  transfers between devices with their start and end apart: 18, of which 12 were waited for; matrix products, arithmetic and copies ran while one was open for 2% of the time, Pallas kernels for 12%

commit v1 on v0

--- a/solution.py
+++ b/solution.py
@@ -30,7 +30,7 @@
 WO_AT = W2_AT + 2048
 BOTH = ("role", "tile")
 F32, BF16 = jnp.float32, jnp.bfloat16
-VMEM_LIMIT = 56 * 1024 * 1024
+VMEM_LIMIT = 24 * 1024 * 1024
 
 
 def row_matrix():
@@ -146,18 +146,26 @@
     ]
 
 
-def forward_kernel(v_ref, p_ref, row_ref, lane_ref, feat_ref, x_out, a_out, d_out, pred_out, w0, w1, w2, wo):
+def layer(w, hidden, a_out, d_out):
+    z = dot_tn(w[...], hidden)
+    s = 0.5 * jnp.tanh(0.5 * z) + 0.5
+    a = z * s
+    d_out[...] = s + a * (1.0 - s)
+    hidden = a.astype(BF16)
+    a_out[...] = hidden
+    return hidden
+
+
+def forward_first_kernel(v_ref, p_ref, row_ref, lane_ref, feat_ref, x_out, a_out, d_out, w0, w1, w2, wo):
     load_weights(p_ref, w0, w1, w2, wo)
     x = cells_to_patches(velocity_blocks(v_ref), row_ref[...], lane_ref[...], feat_ref[...], 3)
     x_out[...] = x
-    hidden = x
-    for layer, w in enumerate((w0, w1, w2)):
-        z = dot_tn(w[...], hidden)
-        s = 0.5 * jnp.tanh(0.5 * z) + 0.5
-        a = z * s
-        d_out[layer] = s + a * (1.0 - s)
-        hidden = a.astype(BF16)
-        a_out[layer] = hidden
+    layer(w0, x, a_out, d_out)
+
+
+def forward_rest_kernel(a1_ref, w1, w2, wo, a2_out, d2_out, a3_out, d3_out, pred_out):
+    hidden = layer(w1, a1_ref[...], a2_out, d2_out)
+    hidden = layer(w2, hidden, a3_out, d3_out)
     pred_out[...] = dot_tn(wo[...], hidden)
 
 
@@ -206,29 +214,28 @@
     return dot_nt(left, right)
 
 
-def backward_kernel(row_scale, rows, in_order, order_ref, count_ref, index_ref, v_ref, xlo_ref, xhi_ref, ylo_ref, yhi_ref, p_ref, row_ref, lane_ref,
-                    feat_ref, x_ref, a_ref, d_ref, pred_ref, *rest):
+def backward_kernel(row_scale, rows, in_order, order_ref, count_ref, index_ref, v_ref, xlo_ref, xhi_ref, ylo_ref, yhi_ref, row_ref, lane_ref,
+                    feat_ref, w1, w2, wo, x_ref, a1_ref, a2_ref, a3_ref, d1_ref, d2_ref, d3_ref, pred_ref, *rest):
     if in_order:
-        send_out, keep_out, pad, w0, w1, w2, wo, grads = rest
+        send_out, keep_out, pad, grads = rest
     else:
-        grads, pad, w0, w1, w2, wo = rest
-    load_weights(p_ref, w0, w1, w2, wo)
+        grads, pad = rest
     weight = multiplicity(index_ref, count_ref) * row_scale
     weight = jnp.concatenate([weight[q : q + 1] for q in range(8)], axis=1)
     fill_padded(pad, v_ref, xlo_ref, xhi_ref, ylo_ref, yhi_ref)
     target = cells_to_patches(stress_blocks(pad), row_ref[...], lane_ref[...], feat_ref[...], 6)
     error = ((pred_ref[...] - target.astype(F32)) * weight).astype(BF16)
-    grad = dot_nt(a_ref[2], error)
+    grad = dot_nt(a3_ref[...], error)
     for k in range(3):
         grads[pl.ds(WO_AT + k, HID, stride=3), :] = grad[:, k * 128 : (k + 1) * 128]
     up = dot(wo[...], error)
-    for layer, at, size, w in ((2, W2_AT, HID, w2), (1, W1_AT, HID, w1), (0, 0, FEAT, None)):
-        slope = (up * d_ref[layer]).astype(BF16)
-        left = a_ref[layer - 1] if layer else x_ref[...]
-        grad = dot_nt(left, slope)
+    for d_ref, left_ref, at, w in ((d3_ref, a2_ref, W2_AT, w2), (d2_ref, a1_ref, W1_AT, w1), (d1_ref, x_ref, 0, None)):
+        slope = (up * d_ref[...]).astype(BF16)
+        grad = dot_nt(left_ref[...], slope)
+        size = left_ref.shape[0]
         for k in range(4):
             grads[pl.ds(at + k, size, stride=4), :] = grad[:, k * 128 : (k + 1) * 128]
-        if layer:
+        if w is not None:
             up = dot(w[...], slope)
     if in_order:
         half = keep_out.shape[0]
@@ -324,13 +331,14 @@
             v_out[i, x] = flow_ref[i, x] + force
 
 
-def call(kernel, outs, args, scratch, scalars=0, flops=0, name=None):
+def call(kernel, outs, args, scratch, scalars=0, flops=0, name=None, final=0):
+    args = list(args[:scalars]) + [pltpu.with_memory_space_constraint(a, pltpu.VMEM) for a in args[scalars:]]
     vm = pl.BlockSpec(memory_space=pltpu.VMEM)
     sm = pl.BlockSpec(memory_space=pltpu.SMEM)
     size = sum(a.size * a.dtype.itemsize for a in args) + sum(int(np.prod(s)) * np.dtype(t).itemsize for s, t in outs)
     return pl.pallas_call(
         kernel,
-        out_shape=[jax.ShapeDtypeStruct(s, t) for s, t in outs],
+        out_shape=[jax.ShapeDtypeStruct(s, t) if i < final else pltpu.VMEM(s, t) for i, (s, t) in enumerate(outs)],
         in_specs=[sm] * scalars + [vm] * (len(args) - scalars),
         out_specs=[vm] * len(outs),
         scratch_shapes=[pltpu.VMEM(s, t) for s, t in scratch],
@@ -342,6 +350,8 @@
 
 WEIGHTS = [((FEAT, HID), BF16), ((HID, HID), BF16), ((HID, HID), BF16), ((HID, TGT), BF16)]
 PADDED = ((3, 12, 80, 128), F32)
+ACT = ((HID, NPATCH), BF16)
+DER = ((HID, NPATCH), F32)
 
 
 def bits(size):
@@ -396,27 +406,40 @@
     up, down = shifts("role")
     xlo = lax.ppermute(velocity[:, CX - 2 :], "role", up)
     xhi = lax.ppermute(velocity[:, :2], "role", down)
-    x, act, slope, pred = call(
-        forward_kernel,
-        [((FEAT, NPATCH), BF16), ((3, HID, NPATCH), BF16), ((3, HID, NPATCH), F32), ((TGT, NPATCH), F32)],
+    x, a1, d1, *weights = call(
+        forward_first_kernel,
+        [((FEAT, NPATCH), BF16), ACT, DER] + WEIGHTS,
         [velocity, p2] + mats,
-        WEIGHTS,
-        flops=2 * 819200 * NPATCH,
-        name="forward",
-    )
+        [],
+        flops=2 * FEAT * HID * NPATCH,
+        name="forward_first",
+    )
+    xlo, xhi, a1 = lax.optimization_barrier((xlo, xhi, a1))
     up, down = shifts("tile")
     last = jnp.concatenate([xlo[:, :, CY - 2 :], velocity[:, :, CY - 2 :], xhi[:, :, CY - 2 :]], axis=1)
     first = jnp.concatenate([xlo[:, :, :2], velocity[:, :, :2], xhi[:, :, :2]], axis=1)
     ylo = lax.ppermute(last, "tile", up)
     yhi = lax.ppermute(first, "tile", down)
+    a2, d2, a3, d3, pred = call(
+        forward_rest_kernel,
+        [ACT, DER, ACT, DER, ((TGT, NPATCH), F32)],
+        [a1] + weights[1:],
+        [],
+        flops=2 * (819200 - FEAT * HID) * NPATCH,
+        name="forward_rest",
+    )
     halos = [xlo, xhi, ylo, yhi]
 
     grad_outs = [((half, rows, 128), BF16), ((half, rows, 128), F32)] if in_order else [((ROWS, 128), F32)]
     grads = call(
         functools.partial(backward_kernel, row_scale, rows, in_order),
         grad_outs,
-        [order, patch_count, patch_index.reshape(1, selected), velocity] + halos + [p2] + mats + [x, act, slope, pred],
-        [PADDED] + WEIGHTS + ([((ROWS, 128), F32)] if in_order else []),
+        [order, patch_count, patch_index.reshape(1, selected), velocity]
+        + halos
+        + mats
+        + weights[1:]
+        + [x, a1, a2, a3, d1, d2, d3, pred],
+        [PADDED] + ([((ROWS, 128), F32)] if in_order else []),
         scalars=2,
         flops=4 * 819200 * NPATCH,
         name="backward",
@@ -427,21 +450,25 @@
         placed = grads[0].reshape(devices, rows, 128)[order]
         send, keep = placed[half:].astype(BF16), placed[:half]
 
+    size = half
     got = exchange(send, 0)
-    flow, x_new = call(
-        flow_kernel,
-        [((3, CX, CY, CZ), F32), ((FEAT, NPATCH), BF16)],
-        [velocity] + halos + mats,
-        [PADDED, PADDED],
-        flops=1 << 30,
-        name="flow",
-    )
-    size = half
     for step in range(1, steps):
         size //= 2
         send = (keep[size:] + got[size:].astype(F32)).astype(BF16)
         keep = keep[:size] + got[:size].astype(F32)
+        if step == 1:
+            send, still = lax.optimization_barrier((send, velocity))
         got = exchange(send, step)
+        if step == 1:
+            flow, x_new = call(
+                flow_kernel,
+                [((3, CX, CY, CZ), F32), ((FEAT, NPATCH), BF16)],
+                [still] + halos + mats,
+                [PADDED, PADDED],
+                flops=1 << 30,
+                name="flow",
+            )
+            got, flow, x_new = lax.optimization_barrier((got, flow, x_new))
     grad = (keep + got.astype(F32)).reshape(-1)
     first_out = BETA_ONE * first_moment + (1.0 - BETA_ONE) * grad
     second_out = BETA_TWO * second_moment + (1.0 - BETA_TWO) * grad * grad
@@ -463,6 +490,7 @@
         WEIGHTS,
         scalars=1,
         flops=2 * 819200 * NPATCH,
+        final=1,
         name="model",
     )
     up, down = shifts("role")
@@ -476,6 +504,7 @@
         [((3, CX, CY, CZ), F32)] * 2,
         [stress, flow, sxlo, sxhi, sylo, syhi],
         [((3, CX, 80, CZ), F32)],
+        final=2,
         name="force",
     )
     return (velocity_out, sgs_force, p_new.reshape(-1), first_out, second_out)

time: 120 us -> 97.6 us (0.81)
  Pallas kernels: 38.9 us -> 19 us
  waiting for transfers between devices: 48.9 us -> 44.4 us
  local copies, waits for them, and re-layouts: 4.27 us -> 7.94 us
  other arithmetic: 3.81 us -> 1.2 us
    pallas_call x5 -> x6, Pallas kernels: 38.9 us -> 19 us  [call(): pl.pallas_call(kernel, out_shape=[jax.ShapeDtypeStruct(s, t) if i < final...]
    unnamed x27 -> x33, local copies, waits for them, and re-layouts: 2.18 us -> 5.86 us
    ppermute x1, waiting for transfers between devices: 1.91 us -> 0.01 us  [local(): xhi = lax.ppermute(velocity[:, :2], 'role', down)]
    ppermute x1, starting transfers between devices: 0.06 us -> 1.55 us  [local(): ylo = lax.ppermute(last, 'tile', up)]
    convert_element_type x4, other arithmetic: 1.77 us -> 0.32 us  [local(): send = (keep[size:] + got[size:].astype(F32)).astype(BF16)]
    ppermute x1, starting transfers between devices: 4.58 us -> 3.28 us  [local(): yhi = lax.ppermute(first, 'tile', down)]
    ppermute x10, waiting for transfers between devices: 44.1 us -> 42.8 us  [exchange(): return lax.ppermute(x, BOTH, pairs)]
  transfers between devices with their start and end apart: 18 -> 18, of which waited for: 12 -> 11; matrix products, arithmetic and copies ran while one was open for 2% -> 1% of each run, Pallas kernels for 12% -> 6%
where the time goes in v1:
time: 97.6 us; the launch traced here: 97.2 us
  waiting for transfers between devices  44.4 us (45%)
  starting transfers between devices  23.2 us (24%)
  Pallas kernels  19 us (19%)
  local copies, waits for them, and re-layouts  7.94 us (8%)
  between operations  1.54 us (2%)
  other arithmetic  1.2 us (1%)
    ppermute x10, waiting for transfers between devices, exchange(): return lax.ppermute(x, BOTH, pairs)  42.8 us
    pallas_call x6, Pallas kernels, call(): pl.pallas_call(kernel, out_shape=[jax.ShapeDtypeStruct(s, t) if i < final...  19 us
    ppermute x10, starting transfers between devices, exchange(): return lax.ppermute(x, BOTH, pairs)  9.33 us
    unnamed x33, local copies, waits for them, and re-layouts  5.86 us
    ppermute x1, starting transfers between devices, local(): syhi = lax.ppermute(yfirst, 'tile', down)  3.66 us
    ppermute x1, starting transfers between devices, local(): yhi = lax.ppermute(first, 'tile', down)  3.28 us
    ppermute x1, starting transfers between devices, local(): xhi = lax.ppermute(velocity[:, :2], 'role', down)  2.46 us
  transfers between devices with their start and end apart: 18, of which 11 were waited for; matrix products, arithmetic and copies ran while one was open for 1% of the time, Pallas kernels for 6%

profile of v1, /device:TPU:0, one launch (start us, length us, event | category | flops | bytes accessed | tf_op | source)
XLA Modules:
  0.0 97.2 jit_solution(2726804800576379914)
XLA Ops:
  1.7 2.5 %collective-permute-start.1 = (f32[3,2,64,128]{3,2,1,0:T(8,128)S(1)}, f32[3,2,64,128]{3,2,1,0:T(8,128)S(1)}, u32[]{:S(2)}, u32[]{:S(2)}) collective-permute-start(f32[3,2,64,128]{3,2,1,0:T(8,128)S(1)} %get-tuple-element.77), channel_id=1, source_target_pairs={{8,0},{16,8},{24,16},{0,24},{9,1},{17,9},{25,17},{1,25},{10,2},{18... | collective-permute-start | bytes 589832 | tf_op jit(solution)/shard_map/ppermute | solution.py:408
  6.9 1.9 %copy-done.2 = f32[819200]{0:T(1024)S(1)} copy-done((f32[819200]{0:T(1024)S(1)}, f32[819200]{0:T(1024)}, u32[]{:S(2)}) %copy-start.2) | copy-done | bytes 3276824
  11.5 1.7 %forward_first.1 = (bf16[192,1024]{1,0:T(8,128)(2,1)S(1)}, bf16[512,1024]{1,0:T(8,128)(2,1)S(1)}, f32[512,1024]{1,0:T(8,128)S(1)}, bf16[192,512]{1,0:T(8,128)(2,...) custom-call(f32[3,8,64,128]{3,2,1,0:T(8,128)S(1)} %copy-done, ...), custom_call_target="tpu_custom_call" | custom-call | flops 201326592 | bytes 9928704 | tf_op jit(solution)/shard_map/forward_first/pallas_call | solution.py:339
  13.4 1.5 %collective-permute-start.2 = (f32[3,12,2,128]{3,2,1,0:T(2,128)S(1)}, f32[3,12,2,128]{3,2,1,0:T(2,128)S(1)}, u32[]{:S(2)}, u32[]{:S(2)}) collective-permute-start(f32[3,12,2,128]{3,2,1,0:T(2,128)S(1)} %pad_maximum_fusion.3), channel_id=1, source_target_pairs={{0,1},{1,2},{2,3},{3,4},{4,5},{5,6},{6,7},{7,0},{8,9},{9,10},{10,1... | collective-permute-start | bytes 110600 | tf_op jit(solution)/shard_map/ppermute | solution.py:421
  15.0 3.3 %collective-permute-start.3 = (f32[3,12,2,128]{3,2,1,0:T(2,128)S(1)}, f32[3,12,2,128]{3,2,1,0:T(2,128)S(1)}, u32[]{:S(2)}, u32[]{:S(2)}) collective-permute-start(f32[3,12,2,128]{3,2,1,0:T(2,128)S(1)} %pad_maximum_fusion.4), channel_id=1, source_target_pairs={{1,0},{2,1},{3,2},{4,3},{5,4},{6,5},{7,6},{0,7},{9,8},{10,9},{11,1... | collective-permute-start | bytes 110600 | tf_op jit(solution)/shard_map/ppermute | solution.py:422
  18.3 2.1 %forward_rest.1 = (bf16[512,1024]{1,0:T(8,128)(2,1)S(1)}, f32[512,1024]{1,0:T(8,128)S(1)}, bf16[512,1024]{1,0:T(8,128)(2,1)S(1)}, f32[512,1024]{1,0:T(8,128)S(1)}, f32[384,1024]{1,0:T(8,128)S(1)}) custom-call(bf16[512,1024]{1,0:T(8,128)(2,1)S(1)} %get-tuple-element.43.a1_ref, bf16[512,512]{1,0:T(8,128)(2,1)S(1)} %get-tuple-element.39.w1, ...), custom_call_target="tpu_custom_call" | custom-call | flops 1476395008 | bytes 10354688 | tf_op jit(solution)/shard_map/forward_rest/pallas_call | solution.py:339
  20.4 7.0 %backward.1 = (bf16[16,200,128]{2,1,0:T(8,128)(2,1)S(1)}, f32[16,200,128]{2,1,0:T(8,128)S(1)}) custom-call(s32[32]{0:T(128)S(1)} %fusion.7.order_ref, s32[1]{0:T(128)S(6)} %copy.20.count_ref, s32[1,2048]{1,0:T(1,128)S(1)} %bitcast.16, f32[3,8,64,128]{3,2,1,0:T(8,128)S(1)} %copy-done.1, f32[3,2,64,128]{3,2,1,0:T(8,128)S(1)} %collective-permute-done.xlo_ref, ...), custom_call_target="tpu_custom_call" | custom-call | flops 3355443200 | bytes 17252484 | tf_op jit(solution)/shard_map/backward/pallas_call | solution.py:339
  27.8 2.0 %collective-permute-done.4 = bf16[16,200,128]{2,1,0:T(8,128)(2,1)S(1)} collective-permute-done((bf16[16,200,128]{2,1,0:T(8,128)(2,1)S(1)}, bf16[16,200,128]{2,1,0:T(8,128)(2,1)S(1)}, u32[]{:S(2)}, u32[]{:S(2)}) %collective-permute-start.4) | collective-permute-done | bytes 819232 | tf_op jit(solution)/shard_map/ppermute | solution.py:387
  31.1 2.1 %flow.1 = (f32[3,8,64,128]{3,2,1,0:T(8,128)S(1)}, bf16[192,1024]{1,0:T(8,128)(2,1)S(1)}) custom-call(f32[3,8,64,128]{3,2,1,0:T(8,128)S(1)} %copy-done.1, f32[3,2,64,128]{3,2,1,0:T(8,128)S(1)} %collective-permute-done.xlo_ref, f32[3,2,64,128]{3,2,1,0:T(8,128)S(1)} %collective-permute-done.1.xhi_ref, f32[3,12,2,128]{3,2,1,0:T(2,128)S(1)} %collective-permute-done.2.ylo_ref, ...), custom_call_target="tpu_custom_call" | custom-call | flops 1073741824 | bytes 3121152 | tf_op jit(solution)/shard_map/flow/pallas_call | solution.py:339
  33.3 4.7 %collective-permute-done.5 = bf16[8,200,128]{2,1,0:T(8,128)(2,1)S(1)} collective-permute-done((bf16[8,200,128]{2,1,0:T(8,128)(2,1)S(1)}, bf16[8,200,128]{2,1,0:T(8,128)(2,1)S(1)}, u32[]{:S(2)}, u32[]{:S(2)}) %collective-permute-start.5) | collective-permute-done | bytes 409632 | tf_op jit(solution)/shard_map/ppermute | solution.py:387
  39.5 4.4 %collective-permute-done.6 = bf16[4,200,128]{2,1,0:T(8,128)(2,1)S(1)} collective-permute-done((bf16[4,200,128]{2,1,0:T(8,128)(2,1)S(1)}, bf16[4,200,128]{2,1,0:T(8,128)(2,1)S(1)}, u32[]{:S(2)}, u32[]{:S(2)}) %collective-permute-start.6) | collective-permute-done | bytes 204832 | tf_op jit(solution)/shard_map/ppermute | solution.py:387
  44.6 4.1 %collective-permute-done.7 = bf16[2,200,128]{2,1,0:T(8,128)(2,1)S(1)} collective-permute-done((bf16[2,200,128]{2,1,0:T(8,128)(2,1)S(1)}, bf16[2,200,128]{2,1,0:T(8,128)(2,1)S(1)}, u32[]{:S(2)}, u32[]{:S(2)}) %collective-permute-start.7) | collective-permute-done | bytes 102432 | tf_op jit(solution)/shard_map/ppermute | solution.py:387
  48.7 1.7 %collective-permute-start.8 = (bf16[1,200,128]{2,1,0:T(8,128)(2,1)S(1)}, bf16[1,200,128]{2,1,0:T(8,128)(2,1)S(1)}, u32[]{:S(2)}, u32[]{:S(2)}) collective-permute-start(bf16[1,200,128]{2,1,0:T(8,128)(2,1)S(1)} %fusion.3), channel_id=1, source_target_pairs={{0,4},{1,5},{2,6},{3,7},{4,0},{5,1},{6,2},{7,3},{8,12},{9,13},{10,... | collective-permute-start | bytes 153608 | tf_op jit(solution)/shard_map/ppermute | solution.py:387
  50.4 4.0 %collective-permute-done.8 = bf16[1,200,128]{2,1,0:T(8,128)(2,1)S(1)} collective-permute-done((bf16[1,200,128]{2,1,0:T(8,128)(2,1)S(1)}, bf16[1,200,128]{2,1,0:T(8,128)(2,1)S(1)}, u32[]{:S(2)}, u32[]{:S(2)}) %collective-permute-start.8) | collective-permute-done | bytes 51232 | tf_op jit(solution)/shard_map/ppermute | solution.py:387
  56.2 4.3 %collective-permute-done.9 = bf16[1,200,128]{2,1,0:T(8,128)(2,1)S(1)} collective-permute-done((bf16[1,200,128]{2,1,0:T(8,128)(2,1)S(1)}, bf16[1,200,128]{2,1,0:T(8,128)(2,1)S(1)}, u32[]{:S(2)}, u32[]{:S(2)}) %collective-permute-start.9) | collective-permute-done | bytes 51232 | tf_op jit(solution)/shard_map/ppermute | solution.py:387
  61.0 4.2 %collective-permute-done.10 = bf16[2,200,128]{2,1,0:T(8,128)(2,1)S(1)} collective-permute-done((bf16[2,200,128]{2,1,0:T(8,128)(2,1)S(1)}, bf16[2,200,128]{2,1,0:T(8,128)(2,1)S(1)}, u32[]{:S(2)}, u32[]{:S(2)}) %collective-permute-start.10) | collective-permute-done | bytes 102432 | tf_op jit(solution)/shard_map/ppermute | solution.py:387
  66.7 5.8 %collective-permute-done.11 = bf16[4,200,128]{2,1,0:T(8,128)(2,1)S(1)} collective-permute-done((bf16[4,200,128]{2,1,0:T(8,128)(2,1)S(1)}, bf16[4,200,128]{2,1,0:T(8,128)(2,1)S(1)}, u32[]{:S(2)}, u32[]{:S(2)}) %collective-permute-start.11) | collective-permute-done | bytes 204832 | tf_op jit(solution)/shard_map/ppermute | solution.py:387
  73.8 6.8 %collective-permute-done.12 = bf16[8,200,128]{2,1,0:T(8,128)(2,1)S(1)} collective-permute-done((bf16[8,200,128]{2,1,0:T(8,128)(2,1)S(1)}, bf16[8,200,128]{2,1,0:T(8,128)(2,1)S(1)}, u32[]{:S(2)}, u32[]{:S(2)}) %collective-permute-start.12) | collective-permute-done | bytes 409632 | tf_op jit(solution)/shard_map/ppermute | solution.py:387
  80.7 2.3 %collective-permute-done.13.other_ref = bf16[16,200,128]{2,1,0:T(8,128)(2,1)S(1)} collective-permute-done((bf16[16,200,128]{2,1,0:T(8,128)(2,1)S(1)}, bf16[16,200,128]{2,1,0:T(8,128)(2,1)S(1)}, u32[]{:S(2)}, u32[]{:S(2)}) %collective-permute-start.13) | collective-permute-done | bytes 819232 | tf_op jit(solution)/shard_map/ppermute | solution.py:387
  83.0 4.4 %model.1 = (f32[6400,128]{1,0:T(8,128)}, f32[6,8,64,128]{3,2,1,0:T(8,128)S(1)}, bf16[3,64,128]{2,1,0:T(8,128)(2,1)S(1)}, bf16[3,64,128]{2,1,0:T(8,128)(2,1)S(1)}...) custom-call(s32[32]{0:T(128)S(1)} %fusion.7.order_ref, f32[6400,128]{1,0:T(8,128)S(1)} %bitcast.15, ...), custom_call_target="tpu_custom_call" | custom-call | flops 1677721600 | bytes 10956928 | tf_op jit(solution)/shard_map/model/pallas_call | solution.py:339
  87.6 1.6 %collective-permute-start.15 = (bf16[3,64,128]{2,1,0:T(8,128)(2,1)S(1)}, bf16[3,64,128]{2,1,0:T(8,128)(2,1)S(1)}, u32[]{:S(2)}, u32[]{:S(2)}) collective-permute-start(bf16[3,64,128]{2,1,0:T(8,128)(2,1)S(1)} %get-tuple-element.61), channel_id=1, source_target_pairs={{8,0},{16,8},{24,16},{0,24},{9,1},{17,9},{25,17},{1,25},{10,2},{18... | collective-permute-start | bytes 147464 | tf_op jit(solution)/shard_map/ppermute | solution.py:498
  90.3 3.7 %collective-permute-start.17 = (bf16[3,8,128]{2,1,0:T(8,128)(2,1)S(1)}, bf16[3,8,128]{2,1,0:T(8,128)(2,1)S(1)}, u32[]{:S(2)}, u32[]{:S(2)}) collective-permute-start(bf16[3,8,128]{2,1,0:T(8,128)(2,1)S(1)} %get-tuple-element.63), channel_id=1, source_target_pairs={{1,0},{2,1},{3,2},{4,3},{5,4},{6,5},{7,6},{0,7},{9,8},{10,9},{11,1... | collective-permute-start | bytes 18440 | tf_op jit(solution)/shard_map/ppermute | solution.py:501
  93.9 1.6 %collective-permute-done.16.ylo_ref = bf16[3,8,128]{2,1,0:T(8,128)(2,1)S(1)} collective-permute-done((bf16[3,8,128]{2,1,0:T(8,128)(2,1)S(1)}, bf16[3,8,128]{2,1,0:T(8,128)(2,1)S(1)}, u32[]{:S(2)}, u32[]{:S(2)}) %collective-permute-start.16) | collective-permute-done | bytes 6176 | tf_op jit(solution)/shard_map/ppermute | solution.py:500
  95.6 1.7 %force.1 = (f32[3,8,64,128]{3,2,1,0:T(8,128)}, f32[3,8,64,128]{3,2,1,0:T(8,128)}) custom-call(f32[6,8,64,128]{3,2,1,0:T(8,128)S(1)} %get-tuple-element.58.s_ref, f32[3,8,64,128]{3,2,1,0:T(8,128)S(1)} %get-tuple-element.59.flow_ref, bf16[3,64,128]{2,1,0:T(8,128)(2,1)S(1)} %collective-permute-done.14.xlo_ref, ...), custom_call_target="tpu_custom_call" | custom-call | bytes 4042752 | tf_op jit(solution)/shard_map/force/pallas_call | solution.py:339
  (66 shorter events, 16.2 us)
Async XLA Ops:
  1.7 11.6 %collective-permute-start.1 = (f32[3,2,64,128]{3,2,1,0:T(8,128)S(1)}, f32[3,2,64,128]{3,2,1,0:T(8,128)S(1)}, u32[]{:S(2)}, u32[]{:S(2)}) collective-permute-start(f32[3,2,64,128]{3,2,1,0:T(8,128)S(1)} %get-tuple-element.77), channel_id=1, source_target_pairs={{8,0},{16,8},{24,16},{0,24},{9,1},{17,9},{25,17},{1,25},{10,2},{18... | collective-permute-start | bytes 589832 | tf_op jit(solution)/shard_map/ppermute | solution.py:408
  4.1 9.2 %collective-permute-start = (f32[3,2,64,128]{3,2,1,0:T(8,128)S(1)}, f32[3,2,64,128]{3,2,1,0:T(8,128)S(1)}, u32[]{:S(2)}, u32[]{:S(2)}) collective-permute-start(f32[3,2,64,128]{3,2,1,0:T(8,128)S(1)} %get-tuple-element.78), channel_id=1, source_target_pairs={{0,8},{8,16},{16,24},{24,0},{1,9},{9,17},{17,25},{25,1},{2,10},{10... | collective-permute-start | bytes 589832 | tf_op jit(solution)/shard_map/ppermute | solution.py:407
  13.4 7.0 %collective-permute-start.2 = (f32[3,12,2,128]{3,2,1,0:T(2,128)S(1)}, f32[3,12,2,128]{3,2,1,0:T(2,128)S(1)}, u32[]{:S(2)}, u32[]{:S(2)}) collective-permute-start(f32[3,12,2,128]{3,2,1,0:T(2,128)S(1)} %pad_maximum_fusion.3), channel_id=1, source_target_pairs={{0,1},{1,2},{2,3},{3,4},{4,5},{5,6},{6,7},{7,0},{8,9},{9,10},{10,1... | collective-permute-start | bytes 110600 | tf_op jit(solution)/shard_map/ppermute | solution.py:421
  15.0 5.4 %collective-permute-start.3 = (f32[3,12,2,128]{3,2,1,0:T(2,128)S(1)}, f32[3,12,2,128]{3,2,1,0:T(2,128)S(1)}, u32[]{:S(2)}, u32[]{:S(2)}) collective-permute-start(f32[3,12,2,128]{3,2,1,0:T(2,128)S(1)} %pad_maximum_fusion.4), channel_id=1, source_target_pairs={{1,0},{2,1},{3,2},{4,3},{5,4},{6,5},{7,6},{0,7},{9,8},{10,9},{11,1... | collective-permute-start | bytes 110600 | tf_op jit(solution)/shard_map/ppermute | solution.py:422
  18.3 2.1 %copy-start.7 = (bf16[256,256]{1,0:T(8,128)(2,1)S(1)}, bf16[256,256]{1,0:T(8,128)(2,1)}, u32[]{:S(2)}) copy-start(bf16[256,256]{1,0:T(8,128)(2,1)} %constant.66.clone.row_ref) | copy-start | bytes 393220
  18.3 2.1 %copy-start.9 = (bf16[128,128]{1,0:T(8,128)(2,1)S(1)}, bf16[128,128]{1,0:T(8,128)(2,1)}, u32[]{:S(2)}) copy-start(bf16[128,128]{1,0:T(8,128)(2,1)} %constant.68.clone.feat_ref) | copy-start | bytes 98308
  18.3 2.1 %copy-start.10 = (s32[2048]{0:T(1024)S(1)}, s32[2048]{0:T(1024)}, u32[]{:S(2)}) copy-start(s32[2048]{0:T(1024)} %param.15) | copy-start | bytes 24580
  27.4 2.4 %collective-permute-start.4 = (bf16[16,200,128]{2,1,0:T(8,128)(2,1)S(1)}, bf16[16,200,128]{2,1,0:T(8,128)(2,1)S(1)}, u32[]{:S(2)}, u32[]{:S(2)}) collective-permute-start(bf16[16,200,128]{2,1,0:T(8,128)(2,1)S(1)} %get-tuple-element.51), channel_id=1, source_target_pairs={{0,8},{1,9},{2,10},{3,11},{4,12},{5,13},{6,14},{7,15},{8,0},{9,1},... | collective-permute-start | bytes 2457608 | tf_op jit(solution)/shard_map/ppermute | solution.py:387
  30.0 8.0 %collective-permute-start.5 = (bf16[8,200,128]{2,1,0:T(8,128)(2,1)S(1)}, bf16[8,200,128]{2,1,0:T(8,128)(2,1)S(1)}, u32[]{:S(2)}, u32[]{:S(2)}) collective-permute-start(bf16[8,200,128]{2,1,0:T(8,128)(2,1)S(1)} %get-tuple-element.52), channel_id=1, source_target_pairs={{0,1},{1,0},{2,3},{3,2},{4,5},{5,4},{6,7},{7,6},{8,24},{9,25},{10,... | collective-permute-start | bytes 1228808 | tf_op jit(solution)/shard_map/ppermute | solution.py:387
  33.2 21.1 %copy-start.11 = (f32[25600]{0:T(1024)S(1)}, f32[25600]{0:T(1024)}, u32[]{:S(2)}) copy-start(f32[25600]{0:T(1024)} %param.13) | copy-start | bytes 307204
  33.2 21.1 %copy-start.12 = (f32[25600]{0:T(1024)S(1)}, f32[25600]{0:T(1024)}, u32[]{:S(2)}) copy-start(f32[25600]{0:T(1024)} %param.14) | copy-start | bytes 307204
  38.1 5.8 %collective-permute-start.6 = (bf16[4,200,128]{2,1,0:T(8,128)(2,1)S(1)}, bf16[4,200,128]{2,1,0:T(8,128)(2,1)S(1)}, u32[]{:S(2)}, u32[]{:S(2)}) collective-permute-start(bf16[4,200,128]{2,1,0:T(8,128)(2,1)S(1)} %get-tuple-element.73), channel_id=1, source_target_pairs={{0,16},{1,17},{2,18},{3,19},{4,20},{5,21},{6,22},{7,23},{8,9},{9,8... | collective-permute-start | bytes 614408 | tf_op jit(solution)/shard_map/ppermute | solution.py:387
  43.9 39.1 %copy-start.3 = (f32[819200]{0:T(1024)S(1)}, f32[819200]{0:T(1024)}, u32[]{:S(2)}) copy-start(f32[819200]{0:T(1024)} %param.12) | copy-start | bytes 9830404
  44.0 4.7 %collective-permute-start.7 = (bf16[2,200,128]{2,1,0:T(8,128)(2,1)S(1)}, bf16[2,200,128]{2,1,0:T(8,128)(2,1)S(1)}, u32[]{:S(2)}, u32[]{:S(2)}) collective-permute-start(bf16[2,200,128]{2,1,0:T(8,128)(2,1)S(1)} %get-tuple-element.79), channel_id=1, source_target_pairs={{0,2},{1,3},{2,0},{3,1},{4,6},{5,7},{6,4},{7,5},{8,10},{9,11},{10,... | collective-permute-start | bytes 307208 | tf_op jit(solution)/shard_map/ppermute | solution.py:387
  48.7 5.6 %collective-permute-start.8 = (bf16[1,200,128]{2,1,0:T(8,128)(2,1)S(1)}, bf16[1,200,128]{2,1,0:T(8,128)(2,1)S(1)}, u32[]{:S(2)}, u32[]{:S(2)}) collective-permute-start(bf16[1,200,128]{2,1,0:T(8,128)(2,1)S(1)} %fusion.3), channel_id=1, source_target_pairs={{0,4},{1,5},{2,6},{3,7},{4,0},{5,1},{6,2},{7,3},{8,12},{9,13},{10,... | collective-permute-start | bytes 153608 | tf_op jit(solution)/shard_map/ppermute | solution.py:387
  55.1 5.4 %collective-permute-start.9 = (bf16[1,200,128]{2,1,0:T(8,128)(2,1)S(1)}, bf16[1,200,128]{2,1,0:T(8,128)(2,1)S(1)}, u32[]{:S(2)}, u32[]{:S(2)}) collective-permute-start(bf16[1,200,128]{2,1,0:T(8,128)(2,1)S(1)} %get-tuple-element.68), channel_id=1, source_target_pairs={{0,4},{1,5},{2,6},{3,7},{4,0},{5,1},{6,2},{7,3},{8,12},{9,13},{10,... | collective-permute-start | bytes 153608 | tf_op jit(solution)/shard_map/ppermute | solution.py:387
  60.5 4.7 %collective-permute-start.10 = (bf16[2,200,128]{2,1,0:T(8,128)(2,1)S(1)}, bf16[2,200,128]{2,1,0:T(8,128)(2,1)S(1)}, u32[]{:S(2)}, u32[]{:S(2)}) collective-permute-start(bf16[2,200,128]{2,1,0:T(8,128)(2,1)S(1)} %pad_maximum_fusion.2), channel_id=1, source_target_pairs={{0,2},{1,3},{2,0},{3,1},{4,6},{5,7},{6,4},{7,5},{8,10},{9,11},{10,... | collective-permute-start | bytes 307208 | tf_op jit(solution)/shard_map/ppermute | solution.py:387
  65.3 7.2 %collective-permute-start.11 = (bf16[4,200,128]{2,1,0:T(8,128)(2,1)S(1)}, bf16[4,200,128]{2,1,0:T(8,128)(2,1)S(1)}, u32[]{:S(2)}, u32[]{:S(2)}) collective-permute-start(bf16[4,200,128]{2,1,0:T(8,128)(2,1)S(1)} %pad_maximum_fusion.1), channel_id=1, source_target_pairs={{0,16},{1,17},{2,18},{3,19},{4,20},{5,21},{6,22},{7,23},{8,9},{9,8... | collective-permute-start | bytes 614408 | tf_op jit(solution)/shard_map/ppermute | solution.py:387
  72.5 8.0 %collective-permute-start.12 = (bf16[8,200,128]{2,1,0:T(8,128)(2,1)S(1)}, bf16[8,200,128]{2,1,0:T(8,128)(2,1)S(1)}, u32[]{:S(2)}, u32[]{:S(2)}) collective-permute-start(bf16[8,200,128]{2,1,0:T(8,128)(2,1)S(1)} %pad_maximum_fusion), channel_id=1, source_target_pairs={{0,1},{1,0},{2,3},{3,2},{4,5},{5,4},{6,7},{7,6},{8,24},{9,25},{10,... | collective-permute-start | bytes 1228808 | tf_op jit(solution)/shard_map/ppermute | solution.py:387
  80.6 2.4 %collective-permute-start.13 = (bf16[16,200,128]{2,1,0:T(8,128)(2,1)S(1)}, bf16[16,200,128]{2,1,0:T(8,128)(2,1)S(1)}, u32[]{:S(2)}, u32[]{:S(2)}) collective-permute-start(bf16[16,200,128]{2,1,0:T(8,128)(2,1)S(1)} %constant_dynamic-update-slice_fusion.own_ref), channel_id=1, source_target_pairs={{0,8},{1,9},{2,10},{3,11},{4,12},{5,13},{6,14},{7,15},{8,0},{9,1},... | collective-permute-start | bytes 2457608 | tf_op jit(solution)/shard_map/ppermute | solution.py:387
  87.4 8.2 %collective-permute-start.14 = (bf16[3,64,128]{2,1,0:T(8,128)(2,1)S(1)}, bf16[3,64,128]{2,1,0:T(8,128)(2,1)S(1)}, u32[]{:S(2)}, u32[]{:S(2)}) collective-permute-start(bf16[3,64,128]{2,1,0:T(8,128)(2,1)S(1)} %get-tuple-element.60), channel_id=1, source_target_pairs={{0,8},{8,16},{16,24},{24,0},{1,9},{9,17},{17,25},{25,1},{2,10},{10... | collective-permute-start | bytes 147464 | tf_op jit(solution)/shard_map/ppermute | solution.py:497
  87.6 8.0 %collective-permute-start.15 = (bf16[3,64,128]{2,1,0:T(8,128)(2,1)S(1)}, bf16[3,64,128]{2,1,0:T(8,128)(2,1)S(1)}, u32[]{:S(2)}, u32[]{:S(2)}) collective-permute-start(bf16[3,64,128]{2,1,0:T(8,128)(2,1)S(1)} %get-tuple-element.61), channel_id=1, source_target_pairs={{8,0},{16,8},{24,16},{0,24},{9,1},{17,9},{25,17},{1,25},{10,2},{18... | collective-permute-start | bytes 147464 | tf_op jit(solution)/shard_map/ppermute | solution.py:498
  89.2 6.3 %collective-permute-start.16 = (bf16[3,8,128]{2,1,0:T(8,128)(2,1)S(1)}, bf16[3,8,128]{2,1,0:T(8,128)(2,1)S(1)}, u32[]{:S(2)}, u32[]{:S(2)}) collective-permute-start(bf16[3,8,128]{2,1,0:T(8,128)(2,1)S(1)} %get-tuple-element.62), channel_id=1, source_target_pairs={{0,1},{1,2},{2,3},{3,4},{4,5},{5,6},{6,7},{7,0},{8,9},{9,10},{10,1... | collective-permute-start | bytes 18440 | tf_op jit(solution)/shard_map/ppermute | solution.py:500
  90.3 5.3 %collective-permute-start.17 = (bf16[3,8,128]{2,1,0:T(8,128)(2,1)S(1)}, bf16[3,8,128]{2,1,0:T(8,128)(2,1)S(1)}, u32[]{:S(2)}, u32[]{:S(2)}) collective-permute-start(bf16[3,8,128]{2,1,0:T(8,128)(2,1)S(1)} %get-tuple-element.63), channel_id=1, source_target_pairs={{1,0},{2,1},{3,2},{4,3},{5,4},{6,5},{7,6},{0,7},{9,8},{10,9},{11,1... | collective-permute-start | bytes 18440 | tf_op jit(solution)/shard_map/ppermute | solution.py:501
  (9 other events, 13.5 us)

commit v2 on v1

--- a/solution.py
+++ b/solution.py
@@ -106,28 +106,27 @@
     return permute_features(feature_mat, jnp.concatenate(bands, axis=0), channels)
 
 
-def patches_to_cells(x, row_mat, lane_mat, feature_mat, channels):
-    pieces = []
-    for at in range(0, channels * 64, 128):
-        pieces.append(dot_tn(feature_mat, x[at : at + 128]).astype(BF16))
-    x = jnp.concatenate(pieces, axis=0)
-    rows = []
-    for c in range(channels):
-        for px in range(2):
-            for j in range(4):
-                lanes = (px * 4 + j) * 128
-                rows.append(
-                    jnp.concatenate(
-                        [x[c * 64 + dz * 16 : c * 64 + dz * 16 + 16, lanes : lanes + 128] for dz in range(4)], axis=1
-                    )
-                )
-    spread = dot_nt(jnp.concatenate(rows, axis=0), lane_mat).astype(BF16)
+def spread_rows(x, lane_mat):
+    rows = [
+        jnp.concatenate([x[at + dz * 16 : at + dz * 16 + 16] for dz in range(4)], axis=1) for at in range(0, x.shape[0], 64)
+    ]
+    return dot_nt(jnp.concatenate(rows, axis=0), lane_mat).astype(BF16)
+
+
+def regroup_features(feature_mat, x):
+    return jnp.concatenate(
+        [dot_tn(feature_mat, x[at : at + 128]).astype(BF16) for at in range(0, x.shape[0], 128)], axis=0
+    )
+
+
+def rows_to_blocks(spread, row_mat):
+    count = spread.shape[0] // 64
     columns = []
-    for i in range(2 * channels):
+    for i in range(count):
         part = spread[i * 64 : (i + 1) * 64]
         columns.append(jnp.concatenate([part[:, p * 128 : (p + 1) * 128] for p in range(4)], axis=0))
     moved = dot_tn(row_mat, jnp.concatenate(columns, axis=1))
-    return [moved[:, i * 128 : (i + 1) * 128] for i in range(2 * channels)]
+    return [moved[:, i * 128 : (i + 1) * 128] for i in range(count)]
 
 
 def load_weights(p_ref, w0, w1, w2, wo):
@@ -156,11 +155,48 @@
     return hidden
 
 
-def forward_first_kernel(v_ref, p_ref, row_ref, lane_ref, feat_ref, x_out, a_out, d_out, w0, w1, w2, wo):
-    load_weights(p_ref, w0, w1, w2, wo)
-    x = cells_to_patches(velocity_blocks(v_ref), row_ref[...], lane_ref[...], feat_ref[...], 3)
+def forward_first_kernel(
+    v_hbm, p_hbm, row_hbm, lane_hbm, feat_hbm, v_out, p_out, row_out, lane_out, feat_out, x_out, a_out, d_out, w0, w1, w2, wo, sems
+):
+    copies = [
+        pltpu.make_async_copy(src, dst, sems.at[i])
+        for i, (src, dst) in enumerate(
+            ((v_hbm, v_out), (row_hbm, row_out), (lane_hbm, lane_out), (feat_hbm, feat_out), (p_hbm, p_out))
+        )
+    ]
+    for copy in copies:
+        copy.start()
+    for copy in copies[:-1]:
+        copy.wait()
+    x = cells_to_patches(velocity_blocks(v_out), row_out[...], lane_out[...], feat_out[...], 3)
     x_out[...] = x
+    copies[-1].wait()
+    load_weights(p_out, w0, w1, w2, wo)
     layer(w0, x, a_out, d_out)
+
+
+def parity(rank_ref, n_tile):
+    rank = rank_ref[0]
+    return (rank // n_tile) % 2 == 0, rank % 2 == 0
+
+
+def strips_kernel(n_tile, rank_ref, v_ref, xa_ref, xb_ref, ya_out, yb_out):
+    role_even, tile_even = parity(rank_ref, n_tile)
+
+    def fill(first_out, last_out, low_ref, high_ref):
+        for out, at in ((first_out, 0), (last_out, CY - 2)):
+            out[:, 2:10] = v_ref[:, :, at : at + 2, :]
+            out[:, 0:2] = low_ref[:, :, at : at + 2, :]
+            out[:, 10:12] = high_ref[:, :, at : at + 2, :]
+
+    for even_r in (True, False):
+        for even_t in (True, False):
+
+            @pl.when((role_even == even_r) & (tile_even == even_t))
+            def _():
+                first_out, last_out = (yb_out, ya_out) if even_t else (ya_out, yb_out)
+                low_ref, high_ref = (xb_ref, xa_ref) if even_r else (xa_ref, xb_ref)
+                fill(first_out, last_out, low_ref, high_ref)
 
 
 def forward_rest_kernel(a1_ref, w1, w2, wo, a2_out, d2_out, a3_out, d3_out, pred_out):
@@ -169,12 +205,32 @@
     pred_out[...] = dot_tn(wo[...], hidden)
 
 
-def fill_padded(pad, v_ref, xlo_ref, xhi_ref, ylo_ref, yhi_ref):
+def fill_padded(pad, rank_ref, n_tile, v_ref, xa_ref, xb_ref, ya_ref, yb_ref):
+    role_even, tile_even = parity(rank_ref, n_tile)
     pad[:, 2:10, 8:72, :] = v_ref[...]
-    pad[:, 0:2, 8:72, :] = xlo_ref[...]
-    pad[:, 10:12, 8:72, :] = xhi_ref[...]
-    pad[:, :, 6:8, :] = ylo_ref[...]
-    pad[:, :, 72:74, :] = yhi_ref[...]
+    for even in (True, False):
+
+        @pl.when(role_even == even)
+        def _():
+            pad[:, 0:2, 8:72, :] = (xb_ref if even else xa_ref)[...]
+            pad[:, 10:12, 8:72, :] = (xa_ref if even else xb_ref)[...]
+
+        @pl.when(tile_even == even)
+        def _():
+            pad[:, :, 6:8, :] = (yb_ref if even else ya_ref)[...]
+            pad[:, :, 72:74, :] = (ya_ref if even else yb_ref)[...]
+
+
+def block_of(position, rank, masks, n_tile, send):
+    core = (rank // n_tile) % 2
+    if send:
+        core = 1 - core
+    steps = len(masks[0])
+    out = rank
+    for i in range(steps):
+        mask = jnp.where(core == 0, masks[0][i], masks[1][i])
+        out = out ^ (((position >> (steps - 1 - i)) & 1) * mask)
+    return out
 
 
 def box(field_sum):
@@ -214,7 +270,7 @@
     return dot_nt(left, right)
 
 
-def backward_kernel(row_scale, rows, in_order, order_ref, count_ref, index_ref, v_ref, xlo_ref, xhi_ref, ylo_ref, yhi_ref, row_ref, lane_ref,
+def backward_kernel(row_scale, rows, masks, n_tile, in_order, rank_ref, count_ref, index_ref, v_ref, xa_ref, xb_ref, ya_ref, yb_ref, row_ref, lane_ref,
                     feat_ref, w1, w2, wo, x_ref, a1_ref, a2_ref, a3_ref, d1_ref, d2_ref, d3_ref, pred_ref, *rest):
     if in_order:
         send_out, keep_out, pad, grads = rest
@@ -222,7 +278,7 @@
         grads, pad = rest
     weight = multiplicity(index_ref, count_ref) * row_scale
     weight = jnp.concatenate([weight[q : q + 1] for q in range(8)], axis=1)
-    fill_padded(pad, v_ref, xlo_ref, xhi_ref, ylo_ref, yhi_ref)
+    fill_padded(pad, rank_ref, n_tile, v_ref, xa_ref, xb_ref, ya_ref, yb_ref)
     target = cells_to_patches(stress_blocks(pad), row_ref[...], lane_ref[...], feat_ref[...], 6)
     error = ((pred_ref[...] - target.astype(F32)) * weight).astype(BF16)
     grad = dot_nt(a3_ref[...], error)
@@ -241,9 +297,9 @@
         half = keep_out.shape[0]
 
         def place(i, carry):
-            here = pl.multiple_of(order_ref[i + half] * rows, 8)
+            here = pl.multiple_of(block_of(i + half, rank_ref[0], masks, n_tile, True) * rows, 8)
             send_out[i] = grads[pl.ds(here, rows), :].astype(BF16)
-            here = pl.multiple_of(order_ref[i] * rows, 8)
+            here = pl.multiple_of(block_of(i, rank_ref[0], masks, n_tile, False) * rows, 8)
             keep_out[i] = grads[pl.ds(here, rows), :]
             return carry
 
@@ -263,8 +319,8 @@
     return out
 
 
-def flow_kernel(v_ref, xlo_ref, xhi_ref, ylo_ref, yhi_ref, row_ref, lane_ref, feat_ref, flow_out, x_out, pad, mid):
-    fill_padded(pad, v_ref, xlo_ref, xhi_ref, ylo_ref, yhi_ref)
+def flow_kernel(n_tile, rank_ref, v_ref, xa_ref, xb_ref, ya_ref, yb_ref, row_ref, lane_ref, feat_ref, flow_out, x_out, xa_out, xb_out, ya_out, yb_out, pad, mid):
+    fill_padded(pad, rank_ref, n_tile, v_ref, xa_ref, xb_ref, ya_ref, yb_ref)
     for src, dst, first, count, low, high in ((pad, mid, 1, 10, 7, 73), (mid, flow_out, 2, 8, 8, 72)):
         for i in range(first, first + count):
             now = [src[c, i, low:high, :] for c in range(3)]
@@ -278,70 +334,115 @@
                     mid[c, i, low:high, :] = new[c]
                 else:
                     flow_out[c, i - 2] = new[c]
-    x_out[...] = cells_to_patches(velocity_blocks(flow_out), row_ref[...], lane_ref[...], feat_ref[...], 3)
-
-
-def model_kernel(rows, in_order, order_ref, p_ref, own_ref, other_ref, x_ref, row_ref, lane_ref, feat_ref, p_out, s_out, xfirst, xlast, yfirst, ylast, w0, w1, w2, wo):
-    half = own_ref.shape[0]
+    x = cells_to_patches(velocity_blocks(flow_out), row_ref[...], lane_ref[...], feat_ref[...], 3)
+    x_out[...] = x
+    role_even, tile_even = parity(rank_ref, n_tile)
+    halves = (x[:, :512], x[:, 512:])
+    edges = [jnp.concatenate([half[:, at : at + 32] for half in halves] * 2, axis=1) for at in (0, 480)]
+    for even in (True, False):
+
+        @pl.when(role_even == even)
+        def _():
+            (xb_out if even else xa_out)[...] = halves[0]
+            (xa_out if even else xb_out)[...] = halves[1]
+
+        @pl.when(tile_even == even)
+        def _():
+            (yb_out if even else ya_out)[...] = edges[0]
+            (ya_out if even else yb_out)[...] = edges[1]
+
+
+def model_kernel(rows, masks, n_tile, in_order, rank_ref, p_ref, own_ref, other_ref, flow_ref, x_ref, xa_ref, xb_ref, ya_ref, yb_ref, row_ref, lane_ref,
+                 feat_ref, p_hbm, v_hbm, force_hbm, p_new, w0, w1, w2, wo, x_all, cells, side, edge, pad, v_new, force_new, sems):
     if in_order:
+        half = own_ref.shape[0]
 
         def place(i, carry):
-            here = pl.ds(pl.multiple_of(order_ref[i] * rows, 8), rows)
-            p_out[here, :] = p_ref[here, :] - own_ref[i].astype(F32)
-            here = pl.ds(pl.multiple_of(order_ref[i + half] * rows, 8), rows)
-            p_out[here, :] = p_ref[here, :] - other_ref[i].astype(F32)
+            here = pl.ds(pl.multiple_of(block_of(i, rank_ref[0], masks, n_tile, False) * rows, 8), rows)
+            p_new[here, :] = p_ref[here, :] - own_ref[i].astype(F32)
+            here = pl.ds(pl.multiple_of(block_of(i + half, rank_ref[0], masks, n_tile, True) * rows, 8), rows)
+            p_new[here, :] = p_ref[here, :] - other_ref[i].astype(F32)
             return carry
 
         lax.fori_loop(0, half, place, 0)
     else:
-        p_out[...] = p_ref[...] - own_ref[...].astype(F32)
-    load_weights(p_out, w0, w1, w2, wo)
-    hidden = x_ref[...]
+        p_new[...] = p_ref[...] - own_ref[...].astype(F32)
+    copies = [pltpu.make_async_copy(p_new, p_hbm, sems.at[0])]
+    copies[0].start()
+    load_weights(p_new, w0, w1, w2, wo)
+    role_even, tile_even = parity(rank_ref, n_tile)
+    x_all[:, 0:1024] = x_ref[...]
+    low = lax.broadcasted_iota(jnp.int32, (FEAT, 128), 1) < 64
+    for even in (True, False):
+
+        @pl.when(role_even == even)
+        def _():
+            x_all[:, 1024:1536] = (xb_ref if even else xa_ref)[...]
+            x_all[:, 1536:2048] = (xa_ref if even else xb_ref)[...]
+
+        @pl.when(tile_even == even)
+        def _():
+            before, after = (yb_ref, ya_ref) if even else (ya_ref, yb_ref)
+            x_all[:, 2048:2176] = jnp.where(low, before[...].astype(F32), after[...].astype(F32)).astype(BF16)
+
+    hidden = x_all[...]
     for w in (w0, w1, w2):
         z = dot_tn(w[...], hidden)
         hidden = (z * (0.5 * jnp.tanh(0.5 * z) + 0.5)).astype(BF16)
-    modelled = dot_tn(wo[...], hidden).astype(BF16)
-    blocks = patches_to_cells(modelled, row_ref[...], lane_ref[...], feat_ref[...], 6)
+    modelled = regroup_features(feat_ref[...], dot_tn(wo[...], hidden).astype(BF16))
+    groups = []
+    for k in range(6):
+        groups += [modelled[k * 64 : k * 64 + 64, q * 128 : q * 128 + 128] for q in range(8)]
+    for first in (8, 12):
+        for k in (0, 3, 4):
+            groups += [modelled[k * 64 : k * 64 + 64, q * 128 : q * 128 + 128] for q in range(first, first + 4)]
+    groups += [modelled[k * 64 : k * 64 + 64, 2048:2176] for k in (3, 1, 5)]
+    spread = spread_rows(jnp.concatenate(groups, axis=0), lane_ref[...])
+    blocks = rows_to_blocks(spread[: 18 * 64], row_ref[...])
     for k in range(6):
         for px in range(2):
-            s_out[k, px * 4 : px * 4 + 4] = blocks[k * 2 + px].reshape(4, 64, 128)
-    for n, k in enumerate((0, 3, 4)):
-        xfirst[n] = s_out[k, 0].astype(BF16)
-        xlast[n] = s_out[k, CX - 1].astype(BF16)
-    for n, k in enumerate((3, 1, 5)):
-        yfirst[n] = s_out[k, :, 0, :].astype(BF16)
-        ylast[n] = s_out[k, :, CY - 1, :].astype(BF16)
-
-
-def force_kernel(s_ref, flow_ref, xlo_ref, xhi_ref, ylo_ref, yhi_ref, v_out, force_out, pad):
-    pad[:, :, 8:72, :] = jnp.stack([s_ref[k] for k in (3, 1, 5)])
-    pad[:, :, 7, :] = ylo_ref[...].astype(F32)
-    pad[:, :, 72, :] = yhi_ref[...].astype(F32)
+            cells[k, px * 4 : px * 4 + 4] = blocks[k * 2 + px].reshape(4, CY, CZ)
+    for i in range(3):
+        side[0, i] = blocks[12 + i][3 * CY :]
+        side[1, i] = blocks[15 + i][:CY]
+    for slot in range(4):
+        edge[slot] = spread[18 * 64 :, slot * 128 : slot * 128 + 128].astype(F32)
+    for i, k in enumerate((3, 1, 5)):
+        pad[i, :, 8:72, :] = cells[k]
+        for px in range(2):
+            pad[i, px * 4 : px * 4 + 4, 7, :] = edge[px, pl.ds(i * 16 + 3, 4, stride=4), :]
+            pad[i, px * 4 : px * 4 + 4, 72, :] = edge[2 + px, pl.ds(i * 16, 4, stride=4), :]
     for i in range(3):
         kx, kz = COMPONENT[i][0], COMPONENT[i][2]
         for x in range(CX):
-            after = s_ref[kx, x + 1] if x < CX - 1 else xhi_ref[i].astype(F32)
-            before = s_ref[kx, x - 1] if x else xlo_ref[i].astype(F32)
+            after = cells[kx, x + 1] if x < CX - 1 else side[1, i]
+            before = cells[kx, x - 1] if x else side[0, i]
             total = 0.5 * (after - before)
             total = total + 0.5 * (pad[i, x, 9:73, :] - pad[i, x, 7:71, :])
-            centre = s_ref[kz, x]
+            centre = cells[kz, x]
             total = total + 0.5 * (roll_z(centre, CZ - 1) - roll_z(centre, 1))
             force = -SGS_SCALE * total
-            force_out[i, x] = force
-            v_out[i, x] = flow_ref[i, x] + force
-
-
-def call(kernel, outs, args, scratch, scalars=0, flops=0, name=None, final=0):
-    args = list(args[:scalars]) + [pltpu.with_memory_space_constraint(a, pltpu.VMEM) for a in args[scalars:]]
-    vm = pl.BlockSpec(memory_space=pltpu.VMEM)
-    sm = pl.BlockSpec(memory_space=pltpu.SMEM)
+            force_new[i, x] = force
+            v_new[i, x] = flow_ref[i, x] + force
+        for n, (src, dst) in enumerate(((v_new, v_hbm), (force_new, force_hbm))):
+            copies.append(pltpu.make_async_copy(src.at[i], dst.at[i], sems.at[1 + 2 * i + n]))
+            copies[-1].start()
+    for copy in copies:
+        copy.wait()
+
+
+def call(kernel, outs, args, scratch, scalars=0, flops=0, name=None, sems=0, hbm_in=False, hbm_out=False):
+    space = {True: pltpu.HBM, False: pltpu.VMEM}
     size = sum(a.size * a.dtype.itemsize for a in args) + sum(int(np.prod(s)) * np.dtype(t).itemsize for s, t in outs)
+    args = list(args)
+    args[scalars:] = [pltpu.with_memory_space_constraint(a, space[hbm_in]) for a in args[scalars:]]
     return pl.pallas_call(
         kernel,
-        out_shape=[jax.ShapeDtypeStruct(s, t) if i < final else pltpu.VMEM(s, t) for i, (s, t) in enumerate(outs)],
-        in_specs=[sm] * scalars + [vm] * (len(args) - scalars),
-        out_specs=[vm] * len(outs),
-        scratch_shapes=[pltpu.VMEM(s, t) for s, t in scratch],
+        out_shape=[space[hbm_out](s, t) for s, t in outs],
+        in_specs=[pl.BlockSpec(memory_space=pltpu.SMEM)] * scalars
+        + [pl.BlockSpec(memory_space=space[hbm_in])] * (len(args) - scalars),
+        out_specs=[pl.BlockSpec(memory_space=space[hbm_out])] * len(outs),
+        scratch_shapes=[pltpu.VMEM(s, t) for s, t in scratch] + ([pltpu.SemaphoreType.DMA((sems,))] if sems else []),
         compiler_params=pltpu.CompilerParams(vmem_limit_bytes=VMEM_LIMIT),
         cost_estimate=pl.CostEstimate(flops=flops, transcendentals=0, bytes_accessed=size),
         name=name,
@@ -366,10 +467,10 @@
     return role[:1] + rest, role[:1] + other
 
 
-def shifts(axis):
+def swaps(axis):
     size = lax.axis_size(axis)
-    up = [(i, (i + 1) % size) for i in range(size)]
-    return up, [(j, i) for i, j in up]
+    first = [(i, i ^ 1) for i in range(size)]
+    return first, [(i, (i + 1) % size if i % 2 else (i - 1) % size) for i in range(size)]
 
 
 def local(velocity, params, first_moment, second_moment, patch_index, patch_count):
@@ -393,33 +494,34 @@
         ]
 
     half = devices // 2
-    both = [offsets(0), offsets(1)]
-    table = np.array([both[c][:half] + both[1 - c][half:] for c in range(2)], np.int32)
-    order = own_rank ^ jnp.where((own_rank // n_tile) % 2 == 0, table[0], table[1])
-
-    row_mat, lane_mat, feat_mat = (jnp.asarray(m, BF16) for m in (row_matrix(), lane_matrix(), feature_matrix()))
-    mats = [row_mat, lane_mat, feat_mat]
+    rank = own_rank.astype(jnp.int32).reshape(1)
+    role_even = (own_rank // n_tile) % 2 == 0
+    role_swaps, tile_swaps = swaps("role"), swaps("tile")
     p2 = params.reshape(ROWS, 128)
     selected = patch_index.shape[0]
     row_scale = 1.0 / (selected // 4)
 
-    up, down = shifts("role")
-    xlo = lax.ppermute(velocity[:, CX - 2 :], "role", up)
-    xhi = lax.ppermute(velocity[:, :2], "role", down)
-    x, a1, d1, *weights = call(
+    first, last = velocity[:, :2], velocity[:, CX - 2 :]
+    xb = lax.ppermute(jnp.where(role_even, first, last), "role", role_swaps[1])
+    xa = lax.ppermute(jnp.where(role_even, last, first), "role", role_swaps[0])
+    v_in, p_in, row_mat, lane_mat, feat_mat, x, a1, d1, *weights = call(
         forward_first_kernel,
-        [((FEAT, NPATCH), BF16), ACT, DER] + WEIGHTS,
-        [velocity, p2] + mats,
+        [((3, CX, CY, CZ), F32), ((ROWS, 128), F32), ((256, 256), BF16), ((512, 512), BF16), ((128, 128), BF16)]
+        + [((FEAT, NPATCH), BF16), ACT, DER]
+        + WEIGHTS,
+        [velocity, p2] + [jnp.asarray(m, BF16) for m in (row_matrix(), lane_matrix(), feature_matrix())],
         [],
         flops=2 * FEAT * HID * NPATCH,
         name="forward_first",
+        sems=5,
+        hbm_in=True,
     )
-    xlo, xhi, a1 = lax.optimization_barrier((xlo, xhi, a1))
-    up, down = shifts("tile")
-    last = jnp.concatenate([xlo[:, :, CY - 2 :], velocity[:, :, CY - 2 :], xhi[:, :, CY - 2 :]], axis=1)
-    first = jnp.concatenate([xlo[:, :, :2], velocity[:, :, :2], xhi[:, :, :2]], axis=1)
-    ylo = lax.ppermute(last, "tile", up)
-    yhi = lax.ppermute(first, "tile", down)
+    mats = [row_mat, lane_mat, feat_mat]
+    xa, xb, v_in, a1 = lax.optimization_barrier((xa, xb, v_in, a1))
+    strip = ((3, CX + 4, 2, CZ), F32)
+    ya, yb = call(functools.partial(strips_kernel, n_tile), [strip] * 2, [rank, v_in, xa, xb], [], scalars=1, name="strips")
+    yb = lax.ppermute(yb, "tile", tile_swaps[1])
+    ya = lax.ppermute(ya, "tile", tile_swaps[0])
     a2, d2, a3, d3, pred = call(
         forward_rest_kernel,
         [ACT, DER, ACT, DER, ((TGT, NPATCH), F32)],
@@ -428,13 +530,13 @@
         flops=2 * (819200 - FEAT * HID) * NPATCH,
         name="forward_rest",
     )
-    halos = [xlo, xhi, ylo, yhi]
+    halos = [xa, xb, ya, yb]
 
     grad_outs = [((half, rows, 128), BF16), ((half, rows, 128), F32)] if in_order else [((ROWS, 128), F32)]
     grads = call(
-        functools.partial(backward_kernel, row_scale, rows, in_order),
+        functools.partial(backward_kernel, row_scale, rows, masks, n_tile, in_order),
         grad_outs,
-        [order, patch_count, patch_index.reshape(1, selected), velocity]
+        [rank, patch_count, patch_index.reshape(1, selected), v_in]
         + halos
         + mats
         + weights[1:]
@@ -447,6 +549,12 @@
     if in_order:
         send, keep = grads
     else:
+        here = jnp.arange(devices, dtype=jnp.int32)
+        order = jnp.where(
+            here < half,
+            block_of(here, own_rank, masks, n_tile, False),
+            block_of(here, own_rank, masks, n_tile, True),
+        )
         placed = grads[0].reshape(devices, rows, 128)[order]
         send, keep = placed[half:].astype(BF16), placed[:half]
 
@@ -457,18 +565,27 @@
         send = (keep[size:] + got[size:].astype(F32)).astype(BF16)
         keep = keep[:size] + got[:size].astype(F32)
         if step == 1:
-            send, still = lax.optimization_barrier((send, velocity))
+            send, still = lax.optimization_barrier((send, v_in))
         got = exchange(send, step)
         if step == 1:
-            flow, x_new = call(
-                flow_kernel,
-                [((3, CX, CY, CZ), F32), ((FEAT, NPATCH), BF16)],
-                [still] + halos + mats,
+            flow, x_new, fxa, fxb, fya, fyb = call(
+                functools.partial(flow_kernel, n_tile),
+                [((3, CX, CY, CZ), F32), ((FEAT, NPATCH), BF16)]
+                + [((FEAT, NPATCH // 2), BF16)] * 2
+                + [((FEAT, 128), BF16)] * 2,
+                [rank, still] + halos + mats,
                 [PADDED, PADDED],
+                scalars=1,
                 flops=1 << 30,
                 name="flow",
             )
-            got, flow, x_new = lax.optimization_barrier((got, flow, x_new))
+            fxa = lax.ppermute(fxa, "role", role_swaps[0])
+            fxb = lax.ppermute(fxb, "role", role_swaps[1])
+            got, flow, x_new, fya, fyb = lax.optimization_barrier((got, flow, x_new, fya, fyb))
+        if step == 2:
+            fya = lax.ppermute(fya, "tile", tile_swaps[0])
+        if step == 3:
+            fyb = lax.ppermute(fyb, "tile", tile_swaps[1])
     grad = (keep + got.astype(F32)).reshape(-1)
     first_out = BETA_ONE * first_moment + (1.0 - BETA_ONE) * grad
     second_out = BETA_TWO * second_moment + (1.0 - BETA_TWO) * grad * grad
@@ -483,29 +600,19 @@
         slots = jnp.zeros((devices,), jnp.int32).at[order].set(jnp.arange(devices, dtype=jnp.int32))
         held = other = jnp.concatenate([held, other], axis=0)[slots].reshape(ROWS, 128)
 
-    p_new, stress, xfirst, xlast, yfirst, ylast = call(
-        functools.partial(model_kernel, rows, in_order),
-        [((ROWS, 128), F32), ((6, CX, CY, CZ), F32)] + [((3, CY, CZ), BF16)] * 2 + [((3, CX, CZ), BF16)] * 2,
-        [order, p2, held, other, x_new] + mats,
-        WEIGHTS,
+    p_new, velocity_out, sgs_force = call(
+        functools.partial(model_kernel, rows, masks, n_tile, in_order),
+        [((ROWS, 128), F32)] + [((3, CX, CY, CZ), F32)] * 2,
+        [rank, p_in, held, other, flow, x_new, fxa, fxb, fya, fyb] + mats,
+        [((ROWS, 128), F32)]
+        + WEIGHTS
+        + [((FEAT, 17 * 128), BF16), ((6, CX, CY, CZ), F32), ((2, 3, CY, CZ), F32), ((4, 48, 128), F32), ((3, CX, 80, CZ), F32)]
+        + [((3, CX, CY, CZ), F32)] * 2,
         scalars=1,
-        flops=2 * 819200 * NPATCH,
-        final=1,
+        flops=4 * 819200 * NPATCH,
         name="model",
-    )
-    up, down = shifts("role")
-    sxlo = lax.ppermute(xlast, "role", up)
-    sxhi = lax.ppermute(xfirst, "role", down)
-    up, down = shifts("tile")
-    sylo = lax.ppermute(ylast, "tile", up)
-    syhi = lax.ppermute(yfirst, "tile", down)
-    velocity_out, sgs_force = call(
-        force_kernel,
-        [((3, CX, CY, CZ), F32)] * 2,
-        [stress, flow, sxlo, sxhi, sylo, syhi],
-        [((3, CX, 80, CZ), F32)],
-        final=2,
-        name="force",
+        sems=7,
+        hbm_out=True,
     )
     return (velocity_out, sgs_force, p_new.reshape(-1), first_out, second_out)
 

time: 97.6 us -> 95.9 us (0.983)
  local copies, waits for them, and re-layouts: 7.94 us -> 0.13 us
  Pallas kernels: 19 us -> 23.1 us
  waiting for transfers between devices: 44.4 us -> 48.4 us
  starting transfers between devices: 23.2 us -> 20.2 us
  other arithmetic: 1.2 us -> 2.19 us
    unnamed x33 -> x9, local copies, waits for them, and re-layouts: 5.86 us -> 0.08 us
    pallas_call x6, Pallas kernels: 19 us -> 23.1 us  [call(): pl.pallas_call(kernel, out_shape=[space[hbm_out](s, t) for s, t in outs],...]
    ppermute x10, starting transfers between devices: 9.33 us -> 5.65 us  [exchange(): return lax.ppermute(x, BOTH, pairs)]
    ppermute x8, waiting for transfers between devices: 1.64 us -> 4.53 us  [the longest x1 2.07 us: local(): fxb = lax.ppermute(fxb, 'role', role_swaps[1])]
    slice x3 -> x0, local copies, waits for them, and re-layouts: 2.03 us -> none  [the longest x1 1.05 us: local(): xhi = lax.ppermute(velocity[:, :2], 'role', down)]
    ppermute x10, waiting for transfers between devices: 42.8 us -> 43.9 us  [exchange(): return lax.ppermute(x, BOTH, pairs)]
    select_n x0 -> x1, other arithmetic: none -> 1.06 us  [local(): xb = lax.ppermute(jnp.where(role_even, first, last), 'role', role_swaps[1])]
  transfers between devices with their start and end apart: 18 -> 18, of which waited for: 11 -> 13; matrix products, arithmetic and copies ran while one was open for 1% -> 0% of each run, Pallas kernels for 6% -> 9%
where the time goes in v2:
time: 95.9 us; the launch traced here: 95.7 us
  waiting for transfers between devices  48.4 us (50%)
  Pallas kernels  23.1 us (24%)
  starting transfers between devices  20.2 us (21%)
  other arithmetic  2.19 us (2%)
  between operations  1.65 us (2%)
    ppermute x10, waiting for transfers between devices, exchange(): return lax.ppermute(x, BOTH, pairs)  43.9 us
    pallas_call x6, Pallas kernels, call(): pl.pallas_call(kernel, out_shape=[space[hbm_out](s, t) for s, t in outs],...  23.1 us
    ppermute x10, starting transfers between devices, exchange(): return lax.ppermute(x, BOTH, pairs)  5.65 us
    ppermute x1, starting transfers between devices, local(): fyb = lax.ppermute(fyb, 'tile', tile_swaps[1])  3.6 us
    ppermute x1, starting transfers between devices, local(): yb = lax.ppermute(yb, 'tile', tile_swaps[1])  3.58 us
    ppermute x1, starting transfers between devices, local(): xb = lax.ppermute(jnp.where(role_even, first, last), 'role', role_swaps[1])  2.47 us
    ppermute x1, starting transfers between devices, local(): ya = lax.ppermute(ya, 'tile', tile_swaps[0])  2.43 us
    ppermute x1, waiting for transfers between devices, local(): fxb = lax.ppermute(fxb, 'role', role_swaps[1])  2.07 us
  transfers between devices with their start and end apart: 18, of which 13 were waited for; matrix products, arithmetic and copies ran while one was open for 0% of the time, Pallas kernels for 9%

profile of v2, /device:TPU:0, one launch (start us, length us, event | category | flops | bytes accessed | tf_op | source)
XLA Modules:
  0.0 95.7 jit_solution(5062494641856278581)
XLA Ops:
  0.7 1.1 %slice_select_fusion = (f32[3,2,64,128]{3,2,1,0:T(8,128)S(1)}, f32[3,2,64,128]{3,2,1,0:T(8,128)S(1)}) fusion(f32[3,8,64,128]{3,2,1,0:T(8,128)} %v_hbm.1, pred[]{:T(512)S(6)} %eq.5), kind=kLoop, calls=%fused_computation.10 | loop fusion | flops 98304 | bytes 786433 | tf_op jit(solution)/shard_map/jit(_where)/select_n | solution.py:505
  1.7 2.5 %collective-permute-start.1 = (f32[3,2,64,128]{3,2,1,0:T(8,128)S(1)}, f32[3,2,64,128]{3,2,1,0:T(8,128)S(1)}, u32[]{:S(2)}, u32[]{:S(2)}) collective-permute-start(f32[3,2,64,128]{3,2,1,0:T(8,128)S(1)} %get-tuple-element.93), channel_id=1, source_target_pairs={{0,24},{8,16},{16,8},{24,0},{1,25},{9,17},{17,9},{25,1},{2,26},{10... | collective-permute-start | bytes 589832 | tf_op jit(solution)/shard_map/ppermute | solution.py:505
  5.5 3.6 %forward_first.1 = (f32[3,8,64,128]{3,2,1,0:T(8,128)S(1)}, f32[6400,128]{1,0:T(8,128)S(1)}, bf16[256,256]{1,0:T(8,128)(2,1)S(1)}, bf16[512,512]{1,0:T(8,128)(2,1...) custom-call(f32[3,8,64,128]{3,2,1,0:T(8,128)} %v_hbm.1, ...), custom_call_target="tpu_custom_call" | custom-call | flops 201326592 | bytes 14680064 | tf_op jit(solution)/shard_map/forward_first/pallas_call | solution.py:439
  9.5 2.4 %collective-permute-start.2 = (f32[3,12,2,128]{3,2,1,0:T(2,128)S(1)}, f32[3,12,2,128]{3,2,1,0:T(2,128)S(1)}, u32[]{:S(2)}, u32[]{:S(2)}) collective-permute-start(f32[3,12,2,128]{3,2,1,0:T(2,128)S(1)} %get-tuple-element.51), channel_id=1, source_target_pairs={{0,1},{1,0},{2,3},{3,2},{4,5},{5,4},{6,7},{7,6},{8,9},{9,8},{10,11... | collective-permute-start | bytes 110600 | tf_op jit(solution)/shard_map/ppermute | solution.py:524
  12.0 3.6 %collective-permute-start.3 = (f32[3,12,2,128]{3,2,1,0:T(2,128)S(1)}, f32[3,12,2,128]{3,2,1,0:T(2,128)S(1)}, u32[]{:S(2)}, u32[]{:S(2)}) collective-permute-start(f32[3,12,2,128]{3,2,1,0:T(2,128)S(1)} %get-tuple-element.52), channel_id=1, source_target_pairs={{0,7},{1,2},{2,1},{3,4},{4,3},{5,6},{6,5},{7,0},{8,15},{9,10},{10,... | collective-permute-start | bytes 110600 | tf_op jit(solution)/shard_map/ppermute | solution.py:523
  15.6 2.0 %forward_rest.1 = (bf16[512,1024]{1,0:T(8,128)(2,1)S(1)}, f32[512,1024]{1,0:T(8,128)S(1)}, bf16[512,1024]{1,0:T(8,128)(2,1)S(1)}, f32[512,1024]{1,0:T(8,128)S(1)}, f32[384,1024]{1,0:T(8,128)S(1)}) custom-call(bf16[512,1024]{1,0:T(8,128)(2,1)S(1)} %get-tuple-element.60.a1_ref, bf16[512,512]{1,0:T(8,128)(2,1)S(1)} %get-tuple-element.56.w1, ...), custom_call_target="tpu_custom_call" | custom-call | flops 1476395008 | bytes 10354688 | tf_op jit(solution)/shard_map/forward_rest/pallas_call | solution.py:439
  18.6 6.8 %backward.1 = (bf16[16,200,128]{2,1,0:T(8,128)(2,1)S(1)}, f32[16,200,128]{2,1,0:T(8,128)S(1)}) custom-call(s32[1]{0:T(128)} %bitcast.rank_ref, s32[1]{0:T(128)S(6)} %copy.18.count_ref, s32[1,2048]{1,0:T(1,128)S(1)} %bitcast.15, f32[3,8,64,128]{3,2,1,0:T(8,128)S(1)} %get-tuple-element.70.v_ref, f32[3,2,64,128]{3,2,1,0:T(8,128)S(1)} %collective-permute-done.xa_ref, ...), custom_call_target="tpu_custom_call" | custom-call | flops 3355443200 | bytes 17252360 | tf_op jit(solution)/shard_map/backward/pallas_call | solution.py:439
  25.5 2.3 %collective-permute-done.4 = bf16[16,200,128]{2,1,0:T(8,128)(2,1)S(1)} collective-permute-done((bf16[16,200,128]{2,1,0:T(8,128)(2,1)S(1)}, bf16[16,200,128]{2,1,0:T(8,128)(2,1)S(1)}, u32[]{:S(2)}, u32[]{:S(2)}) %collective-permute-start.4) | collective-permute-done | bytes 819232 | tf_op jit(solution)/shard_map/ppermute | solution.py:488
  28.1 2.5 %flow.1 = (f32[3,8,64,128]{3,2,1,0:T(8,128)S(1)}, bf16[192,1024]{1,0:T(8,128)(2,1)S(1)}, bf16[192,512]{1,0:T(8,128)(2,1)S(1)}, bf16[192,512]{1,0:T(8,128)(2,1)S(...) custom-call(s32[1]{0:T(128)} %bitcast.rank_ref, f32[3,8,64,128]{3,2,1,0:T(8,128)S(1)} %get-tuple-element.70.v_ref, ...), custom_call_target="tpu_custom_call" | custom-call | flops 1073741824 | bytes 3612676 | tf_op jit(solution)/shard_map/flow/pallas_call | solution.py:439
  30.7 5.4 %collective-permute-done.5 = bf16[8,200,128]{2,1,0:T(8,128)(2,1)S(1)} collective-permute-done((bf16[8,200,128]{2,1,0:T(8,128)(2,1)S(1)}, bf16[8,200,128]{2,1,0:T(8,128)(2,1)S(1)}, u32[]{:S(2)}, u32[]{:S(2)}) %collective-permute-start.5) | collective-permute-done | bytes 409632 | tf_op jit(solution)/shard_map/ppermute | solution.py:488
  36.1 1.6 %collective-permute-start.6 = (bf16[4,200,128]{2,1,0:T(8,128)(2,1)S(1)}, bf16[4,200,128]{2,1,0:T(8,128)(2,1)S(1)}, u32[]{:S(2)}, u32[]{:S(2)}) collective-permute-start(bf16[4,200,128]{2,1,0:T(8,128)(2,1)S(1)} %get-tuple-element.91), channel_id=1, source_target_pairs={{0,16},{1,17},{2,18},{3,19},{4,20},{5,21},{6,22},{7,23},{8,9},{9,8... | collective-permute-start | bytes 614408 | tf_op jit(solution)/shard_map/ppermute | solution.py:488
  37.8 4.2 %collective-permute-done.6 = bf16[4,200,128]{2,1,0:T(8,128)(2,1)S(1)} collective-permute-done((bf16[4,200,128]{2,1,0:T(8,128)(2,1)S(1)}, bf16[4,200,128]{2,1,0:T(8,128)(2,1)S(1)}, u32[]{:S(2)}, u32[]{:S(2)}) %collective-permute-start.6) | collective-permute-done | bytes 204832 | tf_op jit(solution)/shard_map/ppermute | solution.py:488
  42.1 4.6 %collective-permute-done.7 = bf16[2,200,128]{2,1,0:T(8,128)(2,1)S(1)} collective-permute-done((bf16[2,200,128]{2,1,0:T(8,128)(2,1)S(1)}, bf16[2,200,128]{2,1,0:T(8,128)(2,1)S(1)}, u32[]{:S(2)}, u32[]{:S(2)}) %collective-permute-start.7) | collective-permute-done | bytes 102432 | tf_op jit(solution)/shard_map/ppermute | solution.py:488
  47.6 4.2 %collective-permute-done.8 = bf16[1,200,128]{2,1,0:T(8,128)(2,1)S(1)} collective-permute-done((bf16[1,200,128]{2,1,0:T(8,128)(2,1)S(1)}, bf16[1,200,128]{2,1,0:T(8,128)(2,1)S(1)}, u32[]{:S(2)}, u32[]{:S(2)}) %collective-permute-start.8) | collective-permute-done | bytes 51232 | tf_op jit(solution)/shard_map/ppermute | solution.py:488
  53.4 4.5 %collective-permute-done.9 = bf16[1,200,128]{2,1,0:T(8,128)(2,1)S(1)} collective-permute-done((bf16[1,200,128]{2,1,0:T(8,128)(2,1)S(1)}, bf16[1,200,128]{2,1,0:T(8,128)(2,1)S(1)}, u32[]{:S(2)}, u32[]{:S(2)}) %collective-permute-start.9) | collective-permute-done | bytes 51232 | tf_op jit(solution)/shard_map/ppermute | solution.py:488
  58.2 4.4 %collective-permute-done.10 = bf16[2,200,128]{2,1,0:T(8,128)(2,1)S(1)} collective-permute-done((bf16[2,200,128]{2,1,0:T(8,128)(2,1)S(1)}, bf16[2,200,128]{2,1,0:T(8,128)(2,1)S(1)}, u32[]{:S(2)}, u32[]{:S(2)}) %collective-permute-start.10) | collective-permute-done | bytes 102432 | tf_op jit(solution)/shard_map/ppermute | solution.py:488
  62.6 1.6 %collective-permute-start.11 = (bf16[4,200,128]{2,1,0:T(8,128)(2,1)S(1)}, bf16[4,200,128]{2,1,0:T(8,128)(2,1)S(1)}, u32[]{:S(2)}, u32[]{:S(2)}) collective-permute-start(bf16[4,200,128]{2,1,0:T(8,128)(2,1)S(1)} %pad_maximum_fusion.1), channel_id=1, source_target_pairs={{0,16},{1,17},{2,18},{3,19},{4,20},{5,21},{6,22},{7,23},{8,9},{9,8... | collective-permute-start | bytes 614408 | tf_op jit(solution)/shard_map/ppermute | solution.py:488
  64.3 6.4 %collective-permute-done.11 = bf16[4,200,128]{2,1,0:T(8,128)(2,1)S(1)} collective-permute-done((bf16[4,200,128]{2,1,0:T(8,128)(2,1)S(1)}, bf16[4,200,128]{2,1,0:T(8,128)(2,1)S(1)}, u32[]{:S(2)}, u32[]{:S(2)}) %collective-permute-start.11) | collective-permute-done | bytes 204832 | tf_op jit(solution)/shard_map/ppermute | solution.py:488
  70.9 7.9 %collective-permute-done.12 = bf16[8,200,128]{2,1,0:T(8,128)(2,1)S(1)} collective-permute-done((bf16[8,200,128]{2,1,0:T(8,128)(2,1)S(1)}, bf16[8,200,128]{2,1,0:T(8,128)(2,1)S(1)}, u32[]{:S(2)}, u32[]{:S(2)}) %collective-permute-start.12) | collective-permute-done | bytes 409632 | tf_op jit(solution)/shard_map/ppermute | solution.py:488
  79.4 1.3 %collective-permute-start.15 = (bf16[192,512]{1,0:T(8,128)(2,1)S(1)}, bf16[192,512]{1,0:T(8,128)(2,1)S(1)}, u32[]{:S(2)}, u32[]{:S(2)}) collective-permute-start(bf16[192,512]{1,0:T(8,128)(2,1)S(1)} %get-tuple-element.79), channel_id=1, source_target_pairs={{0,24},{8,16},{16,8},{24,0},{1,25},{9,17},{17,9},{25,1},{2,26},{10... | collective-permute-start | bytes 589832 | tf_op jit(solution)/shard_map/ppermute | solution.py:583
  80.7 3.6 %collective-permute-start.17 = (bf16[192,128]{1,0:T(8,128)(2,1)S(1)}, bf16[192,128]{1,0:T(8,128)(2,1)S(1)}, u32[]{:S(2)}, u32[]{:S(2)}) collective-permute-start(bf16[192,128]{1,0:T(8,128)(2,1)S(1)} %get-tuple-element.81), channel_id=1, source_target_pairs={{0,7},{1,2},{2,1},{3,4},{4,3},{5,6},{6,5},{7,0},{8,15},{9,10},{10,... | collective-permute-start | bytes 147464 | tf_op jit(solution)/shard_map/ppermute | solution.py:588
  84.3 2.1 %collective-permute-done.15.xb_ref = bf16[192,512]{1,0:T(8,128)(2,1)S(1)} collective-permute-done((bf16[192,512]{1,0:T(8,128)(2,1)S(1)}, bf16[192,512]{1,0:T(8,128)(2,1)S(1)}, u32[]{:S(2)}, u32[]{:S(2)}) %collective-permute-start.15) | collective-permute-done | bytes 196640 | tf_op jit(solution)/shard_map/ppermute | solution.py:583
  86.3 1.1 %collective-permute-done.17.yb_ref = bf16[192,128]{1,0:T(8,128)(2,1)S(1)} collective-permute-done((bf16[192,128]{1,0:T(8,128)(2,1)S(1)}, bf16[192,128]{1,0:T(8,128)(2,1)S(1)}, u32[]{:S(2)}, u32[]{:S(2)}) %collective-permute-start.17) | collective-permute-done | bytes 49184 | tf_op jit(solution)/shard_map/ppermute | solution.py:588
  87.5 8.1 %model.1 = (f32[6400,128]{1,0:T(8,128)}, f32[3,8,64,128]{3,2,1,0:T(8,128)}, f32[3,8,64,128]{3,2,1,0:T(8,128)}) custom-call(s32[1]{0:T(128)} %bitcast.rank_ref, f32[6400,128]{1,0:T(8,128)S(1)} %get-tuple-element.45.p_ref, bf16[16,200,128]{2,1,0:T(8,128)(2,1)S(1)} %constant_dynamic-update-slice_fusion.own_ref, ...), custom_call_target="tpu_custom_call" | custom-call | flops 3355443200 | bytes 12124164 | tf_op jit(solution)/shard_map/model/pallas_call | solution.py:439
  (37 shorter events, 6.2 us)
Async XLA Ops:
  1.7 7.8 %collective-permute-start.1 = (f32[3,2,64,128]{3,2,1,0:T(8,128)S(1)}, f32[3,2,64,128]{3,2,1,0:T(8,128)S(1)}, u32[]{:S(2)}, u32[]{:S(2)}) collective-permute-start(f32[3,2,64,128]{3,2,1,0:T(8,128)S(1)} %get-tuple-element.93), channel_id=1, source_target_pairs={{0,24},{8,16},{16,8},{24,0},{1,25},{9,17},{17,9},{25,1},{2,26},{10... | collective-permute-start | bytes 589832 | tf_op jit(solution)/shard_map/ppermute | solution.py:505
  4.2 5.3 %collective-permute-start = (f32[3,2,64,128]{3,2,1,0:T(8,128)S(1)}, f32[3,2,64,128]{3,2,1,0:T(8,128)S(1)}, u32[]{:S(2)}, u32[]{:S(2)}) collective-permute-start(f32[3,2,64,128]{3,2,1,0:T(8,128)S(1)} %get-tuple-element.94), channel_id=1, source_target_pairs={{0,8},{8,0},{16,24},{24,16},{1,9},{9,1},{17,25},{25,17},{2,10},{10... | collective-permute-start | bytes 589832 | tf_op jit(solution)/shard_map/ppermute | solution.py:506
  9.5 8.1 %collective-permute-start.2 = (f32[3,12,2,128]{3,2,1,0:T(2,128)S(1)}, f32[3,12,2,128]{3,2,1,0:T(2,128)S(1)}, u32[]{:S(2)}, u32[]{:S(2)}) collective-permute-start(f32[3,12,2,128]{3,2,1,0:T(2,128)S(1)} %get-tuple-element.51), channel_id=1, source_target_pairs={{0,1},{1,0},{2,3},{3,2},{4,5},{5,4},{6,7},{7,6},{8,9},{9,8},{10,11... | collective-permute-start | bytes 110600 | tf_op jit(solution)/shard_map/ppermute | solution.py:524
  12.0 6.7 %collective-permute-start.3 = (f32[3,12,2,128]{3,2,1,0:T(2,128)S(1)}, f32[3,12,2,128]{3,2,1,0:T(2,128)S(1)}, u32[]{:S(2)}, u32[]{:S(2)}) collective-permute-start(f32[3,12,2,128]{3,2,1,0:T(2,128)S(1)} %get-tuple-element.52), channel_id=1, source_target_pairs={{0,7},{1,2},{2,1},{3,4},{4,3},{5,6},{6,5},{7,0},{8,15},{9,10},{10,... | collective-permute-start | bytes 110600 | tf_op jit(solution)/shard_map/ppermute | solution.py:523
  15.5 3.1 %copy-start = (s32[2048]{0:T(1024)S(1)}, s32[2048]{0:T(1024)}, u32[]{:S(2)}) copy-start(s32[2048]{0:T(1024)} %param.13) | copy-start | bytes 24580
  25.5 2.4 %collective-permute-start.4 = (bf16[16,200,128]{2,1,0:T(8,128)(2,1)S(1)}, bf16[16,200,128]{2,1,0:T(8,128)(2,1)S(1)}, u32[]{:S(2)}, u32[]{:S(2)}) collective-permute-start(bf16[16,200,128]{2,1,0:T(8,128)(2,1)S(1)} %get-tuple-element.68), channel_id=1, source_target_pairs={{0,8},{1,9},{2,10},{3,11},{4,12},{5,13},{6,14},{7,15},{8,0},{9,1},... | collective-permute-start | bytes 2457608 | tf_op jit(solution)/shard_map/ppermute | solution.py:488
  28.0 8.0 %collective-permute-start.5 = (bf16[8,200,128]{2,1,0:T(8,128)(2,1)S(1)}, bf16[8,200,128]{2,1,0:T(8,128)(2,1)S(1)}, u32[]{:S(2)}, u32[]{:S(2)}) collective-permute-start(bf16[8,200,128]{2,1,0:T(8,128)(2,1)S(1)} %get-tuple-element.69), channel_id=1, source_target_pairs={{0,1},{1,0},{2,3},{3,2},{4,5},{5,4},{6,7},{7,6},{8,24},{9,25},{10,... | collective-permute-start | bytes 1228808 | tf_op jit(solution)/shard_map/ppermute | solution.py:488
  30.6 21.2 %copy-start.1 = (f32[25600]{0:T(1024)S(1)}, f32[25600]{0:T(1024)}, u32[]{:S(2)}) copy-start(f32[25600]{0:T(1024)} %param.11) | copy-start | bytes 307204
  30.7 21.2 %copy-start.2 = (f32[25600]{0:T(1024)S(1)}, f32[25600]{0:T(1024)}, u32[]{:S(2)}) copy-start(f32[25600]{0:T(1024)} %param.12) | copy-start | bytes 307204
  36.1 5.8 %collective-permute-start.6 = (bf16[4,200,128]{2,1,0:T(8,128)(2,1)S(1)}, bf16[4,200,128]{2,1,0:T(8,128)(2,1)S(1)}, u32[]{:S(2)}, u32[]{:S(2)}) collective-permute-start(bf16[4,200,128]{2,1,0:T(8,128)(2,1)S(1)} %get-tuple-element.91), channel_id=1, source_target_pairs={{0,16},{1,17},{2,18},{3,19},{4,20},{5,21},{6,22},{7,23},{8,9},{9,8... | collective-permute-start | bytes 614408 | tf_op jit(solution)/shard_map/ppermute | solution.py:488
  42.0 4.7 %collective-permute-start.7 = (bf16[2,200,128]{2,1,0:T(8,128)(2,1)S(1)}, bf16[2,200,128]{2,1,0:T(8,128)(2,1)S(1)}, u32[]{:S(2)}, u32[]{:S(2)}) collective-permute-start(bf16[2,200,128]{2,1,0:T(8,128)(2,1)S(1)} %get-tuple-element.95), channel_id=1, source_target_pairs={{0,2},{1,3},{2,0},{3,1},{4,6},{5,7},{6,4},{7,5},{8,10},{9,11},{10,... | collective-permute-start | bytes 307208 | tf_op jit(solution)/shard_map/ppermute | solution.py:488
  46.7 5.1 %collective-permute-start.8 = (bf16[1,200,128]{2,1,0:T(8,128)(2,1)S(1)}, bf16[1,200,128]{2,1,0:T(8,128)(2,1)S(1)}, u32[]{:S(2)}, u32[]{:S(2)}) collective-permute-start(bf16[1,200,128]{2,1,0:T(8,128)(2,1)S(1)} %fusion.3), channel_id=1, source_target_pairs={{0,4},{1,5},{2,6},{3,7},{4,0},{5,1},{6,2},{7,3},{8,12},{9,13},{10,... | collective-permute-start | bytes 153608 | tf_op jit(solution)/shard_map/ppermute | solution.py:488
  52.6 5.3 %collective-permute-start.9 = (bf16[1,200,128]{2,1,0:T(8,128)(2,1)S(1)}, bf16[1,200,128]{2,1,0:T(8,128)(2,1)S(1)}, u32[]{:S(2)}, u32[]{:S(2)}) collective-permute-start(bf16[1,200,128]{2,1,0:T(8,128)(2,1)S(1)} %get-tuple-element.86), channel_id=1, source_target_pairs={{0,4},{1,5},{2,6},{3,7},{4,0},{5,1},{6,2},{7,3},{8,12},{9,13},{10,... | collective-permute-start | bytes 153608 | tf_op jit(solution)/shard_map/ppermute | solution.py:488
  57.9 4.7 %collective-permute-start.10 = (bf16[2,200,128]{2,1,0:T(8,128)(2,1)S(1)}, bf16[2,200,128]{2,1,0:T(8,128)(2,1)S(1)}, u32[]{:S(2)}, u32[]{:S(2)}) collective-permute-start(bf16[2,200,128]{2,1,0:T(8,128)(2,1)S(1)} %pad_maximum_fusion.2), channel_id=1, source_target_pairs={{0,2},{1,3},{2,0},{3,1},{4,6},{5,7},{6,4},{7,5},{8,10},{9,11},{10,... | collective-permute-start | bytes 307208 | tf_op jit(solution)/shard_map/ppermute | solution.py:488
  62.6 8.1 %collective-permute-start.11 = (bf16[4,200,128]{2,1,0:T(8,128)(2,1)S(1)}, bf16[4,200,128]{2,1,0:T(8,128)(2,1)S(1)}, u32[]{:S(2)}, u32[]{:S(2)}) collective-permute-start(bf16[4,200,128]{2,1,0:T(8,128)(2,1)S(1)} %pad_maximum_fusion.1), channel_id=1, source_target_pairs={{0,16},{1,17},{2,18},{3,19},{4,20},{5,21},{6,22},{7,23},{8,9},{9,8... | collective-permute-start | bytes 614408 | tf_op jit(solution)/shard_map/ppermute | solution.py:488
  70.7 8.0 %collective-permute-start.12 = (bf16[8,200,128]{2,1,0:T(8,128)(2,1)S(1)}, bf16[8,200,128]{2,1,0:T(8,128)(2,1)S(1)}, u32[]{:S(2)}, u32[]{:S(2)}) collective-permute-start(bf16[8,200,128]{2,1,0:T(8,128)(2,1)S(1)} %pad_maximum_fusion), channel_id=1, source_target_pairs={{0,1},{1,0},{2,3},{3,2},{4,5},{5,4},{6,7},{7,6},{8,24},{9,25},{10,... | collective-permute-start | bytes 1228808 | tf_op jit(solution)/shard_map/ppermute | solution.py:488
  78.8 8.6 %collective-permute-start.13 = (bf16[16,200,128]{2,1,0:T(8,128)(2,1)S(1)}, bf16[16,200,128]{2,1,0:T(8,128)(2,1)S(1)}, u32[]{:S(2)}, u32[]{:S(2)}) collective-permute-start(bf16[16,200,128]{2,1,0:T(8,128)(2,1)S(1)} %constant_dynamic-update-slice_fusion.own_ref), channel_id=1, source_target_pairs={{0,8},{1,9},{2,10},{3,11},{4,12},{5,13},{6,14},{7,15},{8,0},{9,1},... | collective-permute-start | bytes 2457608 | tf_op jit(solution)/shard_map/ppermute | solution.py:488
  78.9 5.4 %collective-permute-start.14 = (bf16[192,512]{1,0:T(8,128)(2,1)S(1)}, bf16[192,512]{1,0:T(8,128)(2,1)S(1)}, u32[]{:S(2)}, u32[]{:S(2)}) collective-permute-start(bf16[192,512]{1,0:T(8,128)(2,1)S(1)} %get-tuple-element.78), channel_id=1, source_target_pairs={{0,8},{8,0},{16,24},{24,16},{1,9},{9,1},{17,25},{25,17},{2,10},{10... | collective-permute-start | bytes 589832 | tf_op jit(solution)/shard_map/ppermute | solution.py:582
  79.4 6.9 %collective-permute-start.15 = (bf16[192,512]{1,0:T(8,128)(2,1)S(1)}, bf16[192,512]{1,0:T(8,128)(2,1)S(1)}, u32[]{:S(2)}, u32[]{:S(2)}) collective-permute-start(bf16[192,512]{1,0:T(8,128)(2,1)S(1)} %get-tuple-element.79), channel_id=1, source_target_pairs={{0,24},{8,16},{16,8},{24,0},{1,25},{9,17},{17,9},{25,1},{2,26},{10... | collective-permute-start | bytes 589832 | tf_op jit(solution)/shard_map/ppermute | solution.py:583
  80.7 5.7 %collective-permute-start.16 = (bf16[192,128]{1,0:T(8,128)(2,1)S(1)}, bf16[192,128]{1,0:T(8,128)(2,1)S(1)}, u32[]{:S(2)}, u32[]{:S(2)}) collective-permute-start(bf16[192,128]{1,0:T(8,128)(2,1)S(1)} %get-tuple-element.80), channel_id=1, source_target_pairs={{0,1},{1,0},{2,3},{3,2},{4,5},{5,4},{6,7},{7,6},{8,9},{9,8},{10,11... | collective-permute-start | bytes 147464 | tf_op jit(solution)/shard_map/ppermute | solution.py:586
  80.7 6.8 %collective-permute-start.17 = (bf16[192,128]{1,0:T(8,128)(2,1)S(1)}, bf16[192,128]{1,0:T(8,128)(2,1)S(1)}, u32[]{:S(2)}, u32[]{:S(2)}) collective-permute-start(bf16[192,128]{1,0:T(8,128)(2,1)S(1)} %get-tuple-element.81), channel_id=1, source_target_pairs={{0,7},{1,2},{2,1},{3,4},{4,3},{5,6},{6,5},{7,0},{8,15},{9,10},{10,... | collective-permute-start | bytes 147464 | tf_op jit(solution)/shard_map/ppermute | solution.py:588

commit v3 on v2

--- a/solution.py
+++ b/solution.py
@@ -559,15 +559,24 @@
         send, keep = placed[half:].astype(BF16), placed[:half]
 
     size = half
+    fence = lax.optimization_barrier
     got = exchange(send, 0)
     for step in range(1, steps):
         size //= 2
-        send = (keep[size:] + got[size:].astype(F32)).astype(BF16)
-        keep = keep[:size] + got[:size].astype(F32)
+        if step < steps - 1:
+            send = (keep[size:] + got[size:].astype(F32)).astype(BF16)
+            keep = keep[:size] + got[:size].astype(F32)
+        else:
+            send = keep = (keep + got.astype(F32)).astype(BF16)
         if step == 1:
-            send, still = lax.optimization_barrier((send, v_in))
+            send, still, moments = fence((send, v_in, jnp.stack([first_moment, second_moment])))
+        if step == 3:
+            send, fxb = fence((send, fxb))
+        if step == steps - 1:
+            send, fxa, fya = fence((send, fxa, fya))
         got = exchange(send, step)
         if step == 1:
+            moments_other = exchange(moments, steps - 1)
             flow, x_new, fxa, fxb, fya, fyb = call(
                 functools.partial(flow_kernel, n_tile),
                 [((3, CX, CY, CZ), F32), ((FEAT, NPATCH), BF16)]
@@ -579,22 +588,36 @@
                 flops=1 << 30,
                 name="flow",
             )
+            got, flow, x_new, fxa, fxb, fya, fyb = fence((got, flow, x_new, fxa, fxb, fya, fyb))
+        if step == 2:
+            got, moments_other = fence((got, moments_other))
+        if step == 3:
+            fxb = lax.ppermute(fxb, "role", role_swaps[1])
+        if step == steps - 1:
             fxa = lax.ppermute(fxa, "role", role_swaps[0])
-            fxb = lax.ppermute(fxb, "role", role_swaps[1])
-            got, flow, x_new, fya, fyb = lax.optimization_barrier((got, flow, x_new, fya, fyb))
-        if step == 2:
             fya = lax.ppermute(fya, "tile", tile_swaps[0])
-        if step == 3:
-            fyb = lax.ppermute(fyb, "tile", tile_swaps[1])
-    grad = (keep + got.astype(F32)).reshape(-1)
-    first_out = BETA_ONE * first_moment + (1.0 - BETA_ONE) * grad
-    second_out = BETA_TWO * second_moment + (1.0 - BETA_TWO) * grad * grad
+            got, fxb = fence((got, fxb))
+    grad = (keep.astype(F32) + got[::-1].astype(F32)).reshape(2, -1)
+    first_two = jnp.stack([first_moment, moments_other[0]])
+    second_two = jnp.stack([second_moment, moments_other[1]])
+    first_two = BETA_ONE * first_two + (1.0 - BETA_ONE) * grad
+    second_two = BETA_TWO * second_two + (1.0 - BETA_TWO) * grad * grad
+    first_out, second_out = first_two[0], second_two[0]
     fix_first = 1.0 - BETA_ONE**ADAM_STEP
     fix_second = 1.0 - BETA_TWO**ADAM_STEP
-    update = LEARN_RATE * (first_out / fix_first) / (jnp.sqrt(second_out / fix_second) + EPSILON)
-    held = update.astype(BF16).reshape(1, rows, 128)
-    for step in range(steps - 1, 0, -1):
-        held = jnp.concatenate([held, exchange(held, step)], axis=0)
+    update = LEARN_RATE * (first_two / fix_first) / (jnp.sqrt(second_two / fix_second) + EPSILON)
+    held = update.astype(BF16).reshape(2, rows, 128)
+    for step in range(steps - 2, 0, -1):
+        if step == 2:
+            held, fyb = fence((held, fyb))
+        got = exchange(held, step)
+        if step == 2:
+            fyb = lax.ppermute(fyb, "tile", tile_swaps[1])
+        if step == 1:
+            got, fyb = fence((got, fyb))
+        if step == steps - 2:
+            got, fxa, fya = fence((got, fxa, fya))
+        held = jnp.concatenate([held, got], axis=0)
     other = exchange(held, 0)
     if not in_order:
         slots = jnp.zeros((devices,), jnp.int32).at[order].set(jnp.arange(devices, dtype=jnp.int32))

time: 95.9 us -> 84.4 us (0.88)
  waiting for transfers between devices: 48.4 us -> 36.8 us
  starting transfers between devices: 20.2 us -> 19.2 us
    ppermute x10, waiting for transfers between devices: 43.9 us -> 25.7 us  [exchange(): return lax.ppermute(x, BOTH, pairs)]
    ppermute x1, waiting for transfers between devices: 1.12 us -> 4.56 us  [local(): fyb = lax.ppermute(fyb, 'tile', tile_swaps[1])]
    ppermute x1, waiting for transfers between devices: 0.01 us -> 3.27 us  [local(): fya = lax.ppermute(fya, 'tile', tile_swaps[0])]
    ppermute x10, starting transfers between devices: 5.65 us -> 7.37 us  [exchange(): return lax.ppermute(x, BOTH, pairs)]
    ppermute x1, starting transfers between devices: 3.6 us -> 2.24 us  [local(): fyb = lax.ppermute(fyb, 'tile', tile_swaps[1])]
    add x0 -> x2, other arithmetic: none -> 1.34 us  [the longest x1 1.25 us: local(): second_two = BETA_TWO * second_two + (1.0 - BETA_TWO) * grad * grad]
    ppermute x1, starting transfers between devices: 0.01 us -> 1.3 us  [local(): fya = lax.ppermute(fya, 'tile', tile_swaps[0])]
    ppermute x1, starting transfers between devices: 1.26 us -> 0.07 us  [local(): fxb = lax.ppermute(fxb, 'role', role_swaps[1])]
  transfers between devices with their start and end apart: 18 -> 18, of which waited for: 13 -> 14; matrix products, arithmetic and copies ran while one was open for 0% -> 2% of each run, Pallas kernels for 9% -> 10%
where the time goes in v3:
time: 84.4 us; the launch traced here: 84.3 us
  waiting for transfers between devices  36.8 us (44%)
  Pallas kernels  23.1 us (27%)
  starting transfers between devices  19.2 us (23%)
  other arithmetic  3.06 us (4%)
  between operations  1.68 us (2%)
    ppermute x10, waiting for transfers between devices, exchange(): return lax.ppermute(x, BOTH, pairs)  25.7 us
    pallas_call x6, Pallas kernels, call(): pl.pallas_call(kernel, out_shape=[space[hbm_out](s, t) for s, t in outs],...  23.1 us
    ppermute x10, starting transfers between devices, exchange(): return lax.ppermute(x, BOTH, pairs)  7.37 us
    ppermute x1, waiting for transfers between devices, local(): fyb = lax.ppermute(fyb, 'tile', tile_swaps[1])  4.56 us
    ppermute x1, starting transfers between devices, local(): yb = lax.ppermute(yb, 'tile', tile_swaps[1])  3.58 us
    ppermute x1, waiting for transfers between devices, local(): fya = lax.ppermute(fya, 'tile', tile_swaps[0])  3.27 us
    ppermute x1, starting transfers between devices, local(): xb = lax.ppermute(jnp.where(role_even, first, last), 'role', role_swaps[1])  2.64 us
    ppermute x1, starting transfers between devices, local(): fyb = lax.ppermute(fyb, 'tile', tile_swaps[1])  2.24 us
  transfers between devices with their start and end apart: 18, of which 14 were waited for; matrix products, arithmetic and copies ran while one was open for 2% of the time, Pallas kernels for 10%

profile of v3, /device:TPU:0, one launch (start us, length us, event | category | flops | bytes accessed | tf_op | source)
XLA Modules:
  0.0 84.3 jit_solution(9290248754869646520)
XLA Ops:
  2.2 2.6 %collective-permute-start.1 = (f32[3,2,64,128]{3,2,1,0:T(8,128)S(1)}, f32[3,2,64,128]{3,2,1,0:T(8,128)S(1)}, u32[]{:S(2)}, u32[]{:S(2)}) collective-permute-start(f32[3,2,64,128]{3,2,1,0:T(8,128)S(1)} %get-tuple-element.127), channel_id=1, source_target_pairs={{0,24},{8,16},{16,8},{24,0},{1,25},{9,17},{17,9},{25,1},{2,26},{10... | collective-permute-start | bytes 589832 | tf_op jit(solution)/shard_map/ppermute | solution.py:505
  5.5 3.6 %forward_first.1 = (f32[3,8,64,128]{3,2,1,0:T(8,128)S(1)}, f32[6400,128]{1,0:T(8,128)S(1)}, bf16[256,256]{1,0:T(8,128)(2,1)S(1)}, bf16[512,512]{1,0:T(8,128)(2,1...) custom-call(f32[3,8,64,128]{3,2,1,0:T(8,128)} %v_hbm.1, ...), custom_call_target="tpu_custom_call" | custom-call | flops 201326592 | bytes 14680064 | tf_op jit(solution)/shard_map/forward_first/pallas_call | solution.py:439
  10.1 1.5 %collective-permute-start.2 = (f32[3,12,2,128]{3,2,1,0:T(2,128)S(1)}, f32[3,12,2,128]{3,2,1,0:T(2,128)S(1)}, u32[]{:S(2)}, u32[]{:S(2)}) collective-permute-start(f32[3,12,2,128]{3,2,1,0:T(2,128)S(1)} %get-tuple-element.70), channel_id=1, source_target_pairs={{0,1},{1,0},{2,3},{3,2},{4,5},{5,4},{6,7},{7,6},{8,9},{9,8},{10,11... | collective-permute-start | bytes 110600 | tf_op jit(solution)/shard_map/ppermute | solution.py:524
  11.6 3.6 %collective-permute-start.3 = (f32[3,12,2,128]{3,2,1,0:T(2,128)S(1)}, f32[3,12,2,128]{3,2,1,0:T(2,128)S(1)}, u32[]{:S(2)}, u32[]{:S(2)}) collective-permute-start(f32[3,12,2,128]{3,2,1,0:T(2,128)S(1)} %get-tuple-element.71), channel_id=1, source_target_pairs={{0,7},{1,2},{2,1},{3,4},{4,3},{5,6},{6,5},{7,0},{8,15},{9,10},{10,... | collective-permute-start | bytes 110600 | tf_op jit(solution)/shard_map/ppermute | solution.py:523
  15.2 2.0 %forward_rest.1 = (bf16[512,1024]{1,0:T(8,128)(2,1)S(1)}, f32[512,1024]{1,0:T(8,128)S(1)}, bf16[512,1024]{1,0:T(8,128)(2,1)S(1)}, f32[512,1024]{1,0:T(8,128)S(1)}, f32[384,1024]{1,0:T(8,128)S(1)}) custom-call(bf16[512,1024]{1,0:T(8,128)(2,1)S(1)} %get-tuple-element.79.a1_ref, bf16[512,512]{1,0:T(8,128)(2,1)S(1)} %get-tuple-element.75.w1, ...), custom_call_target="tpu_custom_call" | custom-call | flops 1476395008 | bytes 10354688 | tf_op jit(solution)/shard_map/forward_rest/pallas_call | solution.py:439
  18.2 6.8 %backward.1 = (bf16[16,200,128]{2,1,0:T(8,128)(2,1)S(1)}, f32[16,200,128]{2,1,0:T(8,128)S(1)}) custom-call(s32[1]{0:T(128)} %bitcast.rank_ref, s32[1]{0:T(128)S(6)} %copy.19.count_ref, s32[1,2048]{1,0:T(1,128)S(1)} %bitcast.17, f32[3,8,64,128]{3,2,1,0:T(8,128)S(1)} %get-tuple-element.89.v_ref, f32[3,2,64,128]{3,2,1,0:T(8,128)S(1)} %collective-permute-done.xa_ref, ...), custom_call_target="tpu_custom_call" | custom-call | flops 3355443200 | bytes 17252360 | tf_op jit(solution)/shard_map/backward/pallas_call | solution.py:439
  25.4 2.1 %collective-permute-done.4 = bf16[16,200,128]{2,1,0:T(8,128)(2,1)S(1)} collective-permute-done((bf16[16,200,128]{2,1,0:T(8,128)(2,1)S(1)}, bf16[16,200,128]{2,1,0:T(8,128)(2,1)S(1)}, u32[]{:S(2)}, u32[]{:S(2)}) %collective-permute-start.4) | collective-permute-done | bytes 819232 | tf_op jit(solution)/shard_map/ppermute | solution.py:488
  27.7 1.3 %collective-permute-start.7 = (f32[2,25600]{1,0:T(2,128)S(1)}, f32[2,25600]{1,0:T(2,128)S(1)}, u32[]{:S(2)}, u32[]{:S(2)}) collective-permute-start(f32[2,25600]{1,0:T(2,128)S(1)} %pad_maximum_fusion.1), channel_id=1, source_target_pairs={{0,4},{1,5},{2,6},{3,7},{4,0},{5,1},{6,2},{7,3},{8,12},{9,13},{10,... | collective-permute-start | bytes 614408 | tf_op jit(solution)/shard_map/ppermute | solution.py:488
  29.0 2.5 %flow.1 = (f32[3,8,64,128]{3,2,1,0:T(8,128)S(1)}, bf16[192,1024]{1,0:T(8,128)(2,1)S(1)}, bf16[192,512]{1,0:T(8,128)(2,1)S(1)}, bf16[192,512]{1,0:T(8,128)(2,1)S(...) custom-call(s32[1]{0:T(128)} %bitcast.rank_ref, f32[3,8,64,128]{3,2,1,0:T(8,128)S(1)} %get-tuple-element.89.v_ref, ...), custom_call_target="tpu_custom_call" | custom-call | flops 1073741824 | bytes 3612676 | tf_op jit(solution)/shard_map/flow/pallas_call | solution.py:439
  31.6 4.1 %collective-permute-done.5 = bf16[8,200,128]{2,1,0:T(8,128)(2,1)S(1)} collective-permute-done((bf16[8,200,128]{2,1,0:T(8,128)(2,1)S(1)}, bf16[8,200,128]{2,1,0:T(8,128)(2,1)S(1)}, u32[]{:S(2)}, u32[]{:S(2)}) %collective-permute-start.5) | collective-permute-done | bytes 409632 | tf_op jit(solution)/shard_map/ppermute | solution.py:488
  35.8 1.6 %collective-permute-start.6 = (bf16[4,200,128]{2,1,0:T(8,128)(2,1)S(1)}, bf16[4,200,128]{2,1,0:T(8,128)(2,1)S(1)}, u32[]{:S(2)}, u32[]{:S(2)}) collective-permute-start(bf16[4,200,128]{2,1,0:T(8,128)(2,1)S(1)} %get-tuple-element.126), channel_id=1, source_target_pairs={{0,16},{1,17},{2,18},{3,19},{4,20},{5,21},{6,22},{7,23},{8,9},{9,8... | collective-permute-start | bytes 614408 | tf_op jit(solution)/shard_map/ppermute | solution.py:488
  37.3 3.2 %collective-permute-done.7 = f32[2,25600]{1,0:T(2,128)S(1)} collective-permute-done((f32[2,25600]{1,0:T(2,128)S(1)}, f32[2,25600]{1,0:T(2,128)S(1)}, u32[]{:S(2)}, u32[]{:S(2)}) %collective-permute-start.7) | collective-permute-done | bytes 204832 | tf_op jit(solution)/shard_map/ppermute | solution.py:488
  41.8 4.6 %collective-permute-done.8 = bf16[2,200,128]{2,1,0:T(8,128)(2,1)S(1)} collective-permute-done((bf16[2,200,128]{2,1,0:T(8,128)(2,1)S(1)}, bf16[2,200,128]{2,1,0:T(8,128)(2,1)S(1)}, u32[]{:S(2)}, u32[]{:S(2)}) %collective-permute-start.8) | collective-permute-done | bytes 102432 | tf_op jit(solution)/shard_map/ppermute | solution.py:488
  47.5 1.4 %collective-permute-done.10.xb_ref = bf16[192,512]{1,0:T(8,128)(2,1)S(1)} collective-permute-done((bf16[192,512]{1,0:T(8,128)(2,1)S(1)}, bf16[192,512]{1,0:T(8,128)(2,1)S(1)}, u32[]{:S(2)}, u32[]{:S(2)}) %collective-permute-start.10) | collective-permute-done | bytes 196640 | tf_op jit(solution)/shard_map/ppermute | solution.py:595
  48.9 3.7 %collective-permute-done.9 = bf16[2,200,128]{2,1,0:T(8,128)(2,1)S(1)} collective-permute-done((bf16[2,200,128]{2,1,0:T(8,128)(2,1)S(1)}, bf16[2,200,128]{2,1,0:T(8,128)(2,1)S(1)}, u32[]{:S(2)}, u32[]{:S(2)}) %collective-permute-start.9) | collective-permute-done | bytes 102432 | tf_op jit(solution)/shard_map/ppermute | solution.py:488
  52.8 1.3 %collective-permute-start.13 = (bf16[192,128]{1,0:T(8,128)(2,1)S(1)}, bf16[192,128]{1,0:T(8,128)(2,1)S(1)}, u32[]{:S(2)}, u32[]{:S(2)}) collective-permute-start(bf16[192,128]{1,0:T(8,128)(2,1)S(1)} %get-tuple-element.108), channel_id=1, source_target_pairs={{0,1},{1,0},{2,3},{3,2},{4,5},{5,4},{6,7},{7,6},{8,9},{9,8},{10,11... | collective-permute-start | bytes 147464 | tf_op jit(solution)/shard_map/ppermute | solution.py:598
  54.1 3.3 %collective-permute-done.13.ya_ref = bf16[192,128]{1,0:T(8,128)(2,1)S(1)} collective-permute-done((bf16[192,128]{1,0:T(8,128)(2,1)S(1)}, bf16[192,128]{1,0:T(8,128)(2,1)S(1)}, u32[]{:S(2)}, u32[]{:S(2)}) %collective-permute-start.13) | collective-permute-done | bytes 49184 | tf_op jit(solution)/shard_map/ppermute | solution.py:598
  57.5 1.7 %collective-permute-start.14 = (bf16[4,200,128]{2,1,0:T(8,128)(2,1)S(1)}, bf16[4,200,128]{2,1,0:T(8,128)(2,1)S(1)}, u32[]{:S(2)}, u32[]{:S(2)}) collective-permute-start(bf16[4,200,128]{2,1,0:T(8,128)(2,1)S(1)} %pad_maximum_fusion.2), channel_id=1, source_target_pairs={{0,16},{1,17},{2,18},{3,19},{4,20},{5,21},{6,22},{7,23},{8,9},{9,8... | collective-permute-start | bytes 614408 | tf_op jit(solution)/shard_map/ppermute | solution.py:488
  59.1 5.8 %collective-permute-done.14 = bf16[4,200,128]{2,1,0:T(8,128)(2,1)S(1)} collective-permute-done((bf16[4,200,128]{2,1,0:T(8,128)(2,1)S(1)}, bf16[4,200,128]{2,1,0:T(8,128)(2,1)S(1)}, u32[]{:S(2)}, u32[]{:S(2)}) %collective-permute-start.14) | collective-permute-done | bytes 204832 | tf_op jit(solution)/shard_map/ppermute | solution.py:488
  65.0 1.6 %collective-permute-start.15 = (bf16[8,200,128]{2,1,0:T(8,128)(2,1)S(1)}, bf16[8,200,128]{2,1,0:T(8,128)(2,1)S(1)}, u32[]{:S(2)}, u32[]{:S(2)}) collective-permute-start(bf16[8,200,128]{2,1,0:T(8,128)(2,1)S(1)} %pad_maximum_fusion), channel_id=1, source_target_pairs={{0,1},{1,0},{2,3},{3,2},{4,5},{5,4},{6,7},{7,6},{8,24},{9,25},{10,... | collective-permute-start | bytes 1228808 | tf_op jit(solution)/shard_map/ppermute | solution.py:488
  66.7 2.2 %collective-permute-start.16 = (bf16[192,128]{1,0:T(8,128)(2,1)S(1)}, bf16[192,128]{1,0:T(8,128)(2,1)S(1)}, u32[]{:S(2)}, u32[]{:S(2)}) collective-permute-start(bf16[192,128]{1,0:T(8,128)(2,1)S(1)} %get-tuple-element.112), channel_id=1, source_target_pairs={{0,7},{1,2},{2,1},{3,4},{4,3},{5,6},{6,5},{7,0},{8,15},{9,10},{10,... | collective-permute-start | bytes 147464 | tf_op jit(solution)/shard_map/ppermute | solution.py:615
  69.0 4.6 %collective-permute-done.16.yb_ref = bf16[192,128]{1,0:T(8,128)(2,1)S(1)} collective-permute-done((bf16[192,128]{1,0:T(8,128)(2,1)S(1)}, bf16[192,128]{1,0:T(8,128)(2,1)S(1)}, u32[]{:S(2)}, u32[]{:S(2)}) %collective-permute-start.16) | collective-permute-done | bytes 49184 | tf_op jit(solution)/shard_map/ppermute | solution.py:615
  73.7 1.2 %fusion.13 = (f32[1,25600]{1,0:T(1,128)}, f32[1,25600]{1,0:T(1,128)}) fusion(f32[1,25600]{1,0:T(1,128)S(1)} %get-tuple-element.134, f32[1,25600]{1,0:T(1,128)S(1)} %bitcast.21, f32[2,25600]{1,0:T(2,128)S(1)} %bitcast.27, f32[1,25600]{1,0:T(1,128)S(1)} %get-tuple-element.133, f32[1,25600]{1,0:T(1,128)S(1)} %bitcast.24), kind=kLoop, calls=%fused_computation.30 | loop fusion | flops 230400 | bytes 716800 | tf_op jit(solution)/shard_map/add | solution.py:604
  76.0 8.1 %model.1 = (f32[6400,128]{1,0:T(8,128)}, f32[3,8,64,128]{3,2,1,0:T(8,128)}, f32[3,8,64,128]{3,2,1,0:T(8,128)}) custom-call(s32[1]{0:T(128)} %bitcast.rank_ref, f32[6400,128]{1,0:T(8,128)S(1)} %get-tuple-element.64.p_ref, bf16[16,200,128]{2,1,0:T(8,128)(2,1)S(1)} %constant_dynamic-update-slice_fusion.own_ref, ...), custom_call_target="tpu_custom_call" | custom-call | flops 3355443200 | bytes 12124164 | tf_op jit(solution)/shard_map/model/pallas_call | solution.py:439
  (39 shorter events, 8.2 us)
Async XLA Ops:
  1.7 7.5 %collective-permute-start = (f32[3,2,64,128]{3,2,1,0:T(8,128)S(1)}, f32[3,2,64,128]{3,2,1,0:T(8,128)S(1)}, u32[]{:S(2)}, u32[]{:S(2)}) collective-permute-start(f32[3,2,64,128]{3,2,1,0:T(8,128)S(1)} %get-tuple-element.128), channel_id=1, source_target_pairs={{0,8},{8,0},{16,24},{24,16},{1,9},{9,1},{17,25},{25,17},{2,10},{10... | collective-permute-start | bytes 589832 | tf_op jit(solution)/shard_map/ppermute | solution.py:506
  2.2 7.8 %collective-permute-start.1 = (f32[3,2,64,128]{3,2,1,0:T(8,128)S(1)}, f32[3,2,64,128]{3,2,1,0:T(8,128)S(1)}, u32[]{:S(2)}, u32[]{:S(2)}) collective-permute-start(f32[3,2,64,128]{3,2,1,0:T(8,128)S(1)} %get-tuple-element.127), channel_id=1, source_target_pairs={{0,24},{8,16},{16,8},{24,0},{1,25},{9,17},{17,9},{25,1},{2,26},{10... | collective-permute-start | bytes 589832 | tf_op jit(solution)/shard_map/ppermute | solution.py:505
  10.1 7.1 %collective-permute-start.2 = (f32[3,12,2,128]{3,2,1,0:T(2,128)S(1)}, f32[3,12,2,128]{3,2,1,0:T(2,128)S(1)}, u32[]{:S(2)}, u32[]{:S(2)}) collective-permute-start(f32[3,12,2,128]{3,2,1,0:T(2,128)S(1)} %get-tuple-element.70), channel_id=1, source_target_pairs={{0,1},{1,0},{2,3},{3,2},{4,5},{5,4},{6,7},{7,6},{8,9},{9,8},{10,11... | collective-permute-start | bytes 110600 | tf_op jit(solution)/shard_map/ppermute | solution.py:524
  11.6 6.7 %collective-permute-start.3 = (f32[3,12,2,128]{3,2,1,0:T(2,128)S(1)}, f32[3,12,2,128]{3,2,1,0:T(2,128)S(1)}, u32[]{:S(2)}, u32[]{:S(2)}) collective-permute-start(f32[3,12,2,128]{3,2,1,0:T(2,128)S(1)} %get-tuple-element.71), channel_id=1, source_target_pairs={{0,7},{1,2},{2,1},{3,4},{4,3},{5,6},{6,5},{7,0},{8,15},{9,10},{10,... | collective-permute-start | bytes 110600 | tf_op jit(solution)/shard_map/ppermute | solution.py:523
  15.2 3.1 %copy-start = (s32[2048]{0:T(1024)S(1)}, s32[2048]{0:T(1024)}, u32[]{:S(2)}) copy-start(s32[2048]{0:T(1024)} %param.13) | copy-start | bytes 24580
  18.2 6.9 %copy-start.1 = (f32[25600]{0:T(1024)S(1)}, f32[25600]{0:T(1024)}, u32[]{:S(2)}) copy-start(f32[25600]{0:T(1024)} %param.12) | copy-start | bytes 307204
  18.2 6.9 %copy-start.2 = (f32[25600]{0:T(1024)S(1)}, f32[25600]{0:T(1024)}, u32[]{:S(2)}) copy-start(f32[25600]{0:T(1024)} %param.11) | copy-start | bytes 307204
  25.1 2.4 %collective-permute-start.4 = (bf16[16,200,128]{2,1,0:T(8,128)(2,1)S(1)}, bf16[16,200,128]{2,1,0:T(8,128)(2,1)S(1)}, u32[]{:S(2)}, u32[]{:S(2)}) collective-permute-start(bf16[16,200,128]{2,1,0:T(8,128)(2,1)S(1)} %get-tuple-element.87), channel_id=1, source_target_pairs={{0,8},{1,9},{2,10},{3,11},{4,12},{5,13},{6,14},{7,15},{8,0},{9,1},... | collective-permute-start | bytes 2457608 | tf_op jit(solution)/shard_map/ppermute | solution.py:488
  27.6 8.0 %collective-permute-start.5 = (bf16[8,200,128]{2,1,0:T(8,128)(2,1)S(1)}, bf16[8,200,128]{2,1,0:T(8,128)(2,1)S(1)}, u32[]{:S(2)}, u32[]{:S(2)}) collective-permute-start(bf16[8,200,128]{2,1,0:T(8,128)(2,1)S(1)} %get-tuple-element.88), channel_id=1, source_target_pairs={{0,1},{1,0},{2,3},{3,2},{4,5},{5,4},{6,7},{7,6},{8,24},{9,25},{10,... | collective-permute-start | bytes 1228808 | tf_op jit(solution)/shard_map/ppermute | solution.py:488
  27.7 12.8 %collective-permute-start.7 = (f32[2,25600]{1,0:T(2,128)S(1)}, f32[2,25600]{1,0:T(2,128)S(1)}, u32[]{:S(2)}, u32[]{:S(2)}) collective-permute-start(f32[2,25600]{1,0:T(2,128)S(1)} %pad_maximum_fusion.1), channel_id=1, source_target_pairs={{0,4},{1,5},{2,6},{3,7},{4,0},{5,1},{6,2},{7,3},{8,12},{9,13},{10,... | collective-permute-start | bytes 614408 | tf_op jit(solution)/shard_map/ppermute | solution.py:488
  35.8 5.8 %collective-permute-start.6 = (bf16[4,200,128]{2,1,0:T(8,128)(2,1)S(1)}, bf16[4,200,128]{2,1,0:T(8,128)(2,1)S(1)}, u32[]{:S(2)}, u32[]{:S(2)}) collective-permute-start(bf16[4,200,128]{2,1,0:T(8,128)(2,1)S(1)} %get-tuple-element.126), channel_id=1, source_target_pairs={{0,16},{1,17},{2,18},{3,19},{4,20},{5,21},{6,22},{7,23},{8,9},{9,8... | collective-permute-start | bytes 614408 | tf_op jit(solution)/shard_map/ppermute | solution.py:488
  41.6 4.7 %collective-permute-start.8 = (bf16[2,200,128]{2,1,0:T(8,128)(2,1)S(1)}, bf16[2,200,128]{2,1,0:T(8,128)(2,1)S(1)}, u32[]{:S(2)}, u32[]{:S(2)}) collective-permute-start(bf16[2,200,128]{2,1,0:T(8,128)(2,1)S(1)} %fusion.6), channel_id=1, source_target_pairs={{0,2},{1,3},{2,0},{3,1},{4,6},{5,7},{6,4},{7,5},{8,10},{9,11},{10,... | collective-permute-start | bytes 307208 | tf_op jit(solution)/shard_map/ppermute | solution.py:488
  41.7 7.2 %collective-permute-start.10 = (bf16[192,512]{1,0:T(8,128)(2,1)S(1)}, bf16[192,512]{1,0:T(8,128)(2,1)S(1)}, u32[]{:S(2)}, u32[]{:S(2)}) collective-permute-start(bf16[192,512]{1,0:T(8,128)(2,1)S(1)} %get-tuple-element.105), channel_id=1, source_target_pairs={{0,24},{8,16},{16,8},{24,0},{1,25},{9,17},{17,9},{25,1},{2,26},{10... | collective-permute-start | bytes 589832 | tf_op jit(solution)/shard_map/ppermute | solution.py:595
  46.4 6.2 %collective-permute-start.9 = (bf16[2,200,128]{2,1,0:T(8,128)(2,1)S(1)}, bf16[2,200,128]{2,1,0:T(8,128)(2,1)S(1)}, u32[]{:S(2)}, u32[]{:S(2)}) collective-permute-start(bf16[2,200,128]{2,1,0:T(8,128)(2,1)S(1)} %fusion.8), channel_id=1, source_target_pairs={{0,4},{1,5},{2,6},{3,7},{4,0},{5,1},{6,2},{7,3},{8,12},{9,13},{10,... | collective-permute-start | bytes 307208 | tf_op jit(solution)/shard_map/ppermute | solution.py:488
  47.4 10.0 %collective-permute-start.12 = (bf16[192,512]{1,0:T(8,128)(2,1)S(1)}, bf16[192,512]{1,0:T(8,128)(2,1)S(1)}, u32[]{:S(2)}, u32[]{:S(2)}) collective-permute-start(bf16[192,512]{1,0:T(8,128)(2,1)S(1)} %get-tuple-element.107), channel_id=1, source_target_pairs={{0,8},{8,0},{16,24},{24,16},{1,9},{9,1},{17,25},{25,17},{2,10},{10... | collective-permute-start | bytes 589832 | tf_op jit(solution)/shard_map/ppermute | solution.py:597
  52.7 4.7 %collective-permute-start.11 = (bf16[2,200,128]{2,1,0:T(8,128)(2,1)S(1)}, bf16[2,200,128]{2,1,0:T(8,128)(2,1)S(1)}, u32[]{:S(2)}, u32[]{:S(2)}) collective-permute-start(bf16[2,200,128]{2,1,0:T(8,128)(2,1)S(1)} %get-tuple-element.132), channel_id=1, source_target_pairs={{0,2},{1,3},{2,0},{3,1},{4,6},{5,7},{6,4},{7,5},{8,10},{9,11},{10,... | collective-permute-start | bytes 307208 | tf_op jit(solution)/shard_map/ppermute | solution.py:488
  52.8 4.6 %collective-permute-start.13 = (bf16[192,128]{1,0:T(8,128)(2,1)S(1)}, bf16[192,128]{1,0:T(8,128)(2,1)S(1)}, u32[]{:S(2)}, u32[]{:S(2)}) collective-permute-start(bf16[192,128]{1,0:T(8,128)(2,1)S(1)} %get-tuple-element.108), channel_id=1, source_target_pairs={{0,1},{1,0},{2,3},{3,2},{4,5},{5,4},{6,7},{7,6},{8,9},{9,8},{10,11... | collective-permute-start | bytes 147464 | tf_op jit(solution)/shard_map/ppermute | solution.py:598
  57.5 7.5 %collective-permute-start.14 = (bf16[4,200,128]{2,1,0:T(8,128)(2,1)S(1)}, bf16[4,200,128]{2,1,0:T(8,128)(2,1)S(1)}, u32[]{:S(2)}, u32[]{:S(2)}) collective-permute-start(bf16[4,200,128]{2,1,0:T(8,128)(2,1)S(1)} %pad_maximum_fusion.2), channel_id=1, source_target_pairs={{0,16},{1,17},{2,18},{3,19},{4,20},{5,21},{6,22},{7,23},{8,9},{9,8... | collective-permute-start | bytes 614408 | tf_op jit(solution)/shard_map/ppermute | solution.py:488
  65.0 8.6 %collective-permute-start.15 = (bf16[8,200,128]{2,1,0:T(8,128)(2,1)S(1)}, bf16[8,200,128]{2,1,0:T(8,128)(2,1)S(1)}, u32[]{:S(2)}, u32[]{:S(2)}) collective-permute-start(bf16[8,200,128]{2,1,0:T(8,128)(2,1)S(1)} %pad_maximum_fusion), channel_id=1, source_target_pairs={{0,1},{1,0},{2,3},{3,2},{4,5},{5,4},{6,7},{7,6},{8,24},{9,25},{10,... | collective-permute-start | bytes 1228808 | tf_op jit(solution)/shard_map/ppermute | solution.py:488
  66.7 6.9 %collective-permute-start.16 = (bf16[192,128]{1,0:T(8,128)(2,1)S(1)}, bf16[192,128]{1,0:T(8,128)(2,1)S(1)}, u32[]{:S(2)}, u32[]{:S(2)}) collective-permute-start(bf16[192,128]{1,0:T(8,128)(2,1)S(1)} %get-tuple-element.112), channel_id=1, source_target_pairs={{0,7},{1,2},{2,1},{3,4},{4,3},{5,6},{6,5},{7,0},{8,15},{9,10},{10,... | collective-permute-start | bytes 147464 | tf_op jit(solution)/shard_map/ppermute | solution.py:615
  73.6 2.4 %collective-permute-start.17 = (bf16[16,200,128]{2,1,0:T(8,128)(2,1)S(1)}, bf16[16,200,128]{2,1,0:T(8,128)(2,1)S(1)}, u32[]{:S(2)}, u32[]{:S(2)}) collective-permute-start(bf16[16,200,128]{2,1,0:T(8,128)(2,1)S(1)} %constant_dynamic-update-slice_fusion.own_ref), channel_id=1, source_target_pairs={{0,8},{1,9},{2,10},{3,11},{4,12},{5,13},{6,14},{7,15},{8,0},{9,1},... | collective-permute-start | bytes 2457608 | tf_op jit(solution)/shard_map/ppermute | solution.py:488

commit v4 on v3

--- a/solution.py
+++ b/solution.py
@@ -61,6 +61,16 @@
     return matrix
 
 
+def side_matrix():
+    matrix = np.zeros((TGT, 128), np.float32)
+    for side, dx in enumerate((3, 0)):
+        for dz in range(4):
+            for slot, k in enumerate((0, 3, 4)):
+                for dy in range(4):
+                    matrix[k * 64 + dz * 16 + dx * 4 + dy, side * 64 + dz * 16 + slot * 4 + dy] = 1
+    return matrix
+
+
 def dot(a, b):
     return jnp.dot(a, b, preferred_element_type=F32)
 
@@ -73,17 +83,7 @@
     return lax.dot_general(a, b, (((1,), (1,)), ((), ())), preferred_element_type=F32)
 
 
-def permute_features(feature_mat, x, channels):
-    pieces = []
-    at = 0
-    while at < channels * 64:
-        size = min(128, channels * 64 - at)
-        pieces.append(dot(feature_mat[:size, :size], x[at : at + size]).astype(BF16))
-        at += size
-    return jnp.concatenate(pieces, axis=0)
-
-
-def cells_to_patches(blocks, row_mat, lane_mat, feature_mat, channels):
+def cells_to_patches(blocks, row_mat, lane_mat, channels):
     moved = dot(row_mat, jnp.concatenate(blocks, axis=1)).astype(BF16)
     rows = []
     for i in range(2 * channels):
@@ -103,7 +103,7 @@
                     axis=1,
                 )
             )
-    return permute_features(feature_mat, jnp.concatenate(bands, axis=0), channels)
+    return jnp.concatenate(bands, axis=0)
 
 
 def spread_rows(x, lane_mat):
@@ -111,12 +111,6 @@
         jnp.concatenate([x[at + dz * 16 : at + dz * 16 + 16] for dz in range(4)], axis=1) for at in range(0, x.shape[0], 64)
     ]
     return dot_nt(jnp.concatenate(rows, axis=0), lane_mat).astype(BF16)
-
-
-def regroup_features(feature_mat, x):
-    return jnp.concatenate(
-        [dot_tn(feature_mat, x[at : at + 128]).astype(BF16) for at in range(0, x.shape[0], 128)], axis=0
-    )
 
 
 def rows_to_blocks(spread, row_mat):
@@ -129,14 +123,20 @@
     return [moved[:, i * 128 : (i + 1) * 128] for i in range(count)]
 
 
-def load_weights(p_ref, w0, w1, w2, wo):
+def load_weights(p_ref, feature_mat, w0, w1, w2, wo):
     for k in range(4):
         lanes = slice(k * 128, (k + 1) * 128)
-        w0[:, lanes] = p_ref[pl.ds(k, FEAT, stride=4), :].astype(BF16)
+        for at in first_rows():
+            w0[at[0] : at[0] + 16, lanes] = p_ref[pl.ds(at[1] + k, 16, stride=16), :].astype(BF16)
         w1[:, lanes] = p_ref[pl.ds(W1_AT + k, HID, stride=4), :].astype(BF16)
         w2[:, lanes] = p_ref[pl.ds(W2_AT + k, HID, stride=4), :].astype(BF16)
     for k in range(3):
-        wo[:, k * 128 : (k + 1) * 128] = p_ref[pl.ds(WO_AT + k, HID, stride=3), :].astype(BF16)
+        columns = p_ref[pl.ds(WO_AT + k, HID, stride=3), :].astype(BF16)
+        wo[:, k * 128 : (k + 1) * 128] = dot(columns, feature_mat).astype(BF16)
+
+
+def first_rows():
+    return [(c * 64 + dz * 16, (c * 64 + dz) * 4) for c in range(3) for dz in range(4)]
 
 
 def velocity_blocks(v_ref):
@@ -156,23 +156,22 @@
 
 
 def forward_first_kernel(
-    v_hbm, p_hbm, row_hbm, lane_hbm, feat_hbm, v_out, p_out, row_out, lane_out, feat_out, x_out, a_out, d_out, w0, w1, w2, wo, sems
+    v_hbm, p_hbm, row_hbm, lane_hbm, feat_hbm, side_hbm, index_hbm,
+    v_out, p_out, row_out, lane_out, feat_out, side_out, index_out, x_out, sems
 ):
     copies = [
         pltpu.make_async_copy(src, dst, sems.at[i])
         for i, (src, dst) in enumerate(
-            ((v_hbm, v_out), (row_hbm, row_out), (lane_hbm, lane_out), (feat_hbm, feat_out), (p_hbm, p_out))
+            ((v_hbm, v_out), (row_hbm, row_out), (lane_hbm, lane_out), (p_hbm, p_out), (feat_hbm, feat_out), (side_hbm, side_out), (index_hbm, index_out))
         )
     ]
     for copy in copies:
         copy.start()
-    for copy in copies[:-1]:
+    for copy in copies[:3]:
         copy.wait()
-    x = cells_to_patches(velocity_blocks(v_out), row_out[...], lane_out[...], feat_out[...], 3)
-    x_out[...] = x
-    copies[-1].wait()
-    load_weights(p_out, w0, w1, w2, wo)
-    layer(w0, x, a_out, d_out)
+    x_out[...] = cells_to_patches(velocity_blocks(v_out), row_out[...], lane_out[...], 3)
+    for copy in copies[3:]:
+        copy.wait()
 
 
 def parity(rank_ref, n_tile):
@@ -186,8 +185,8 @@
     def fill(first_out, last_out, low_ref, high_ref):
         for out, at in ((first_out, 0), (last_out, CY - 2)):
             out[:, 2:10] = v_ref[:, :, at : at + 2, :]
-            out[:, 0:2] = low_ref[:, :, at : at + 2, :]
-            out[:, 10:12] = high_ref[:, :, at : at + 2, :]
+            out[:, 0:2] = low_ref[...].astype(F32)[:, :, at : at + 2, :]
+            out[:, 10:12] = high_ref[...].astype(F32)[:, :, at : at + 2, :]
 
     for even_r in (True, False):
         for even_t in (True, False):
@@ -199,8 +198,10 @@
                 fill(first_out, last_out, low_ref, high_ref)
 
 
-def forward_rest_kernel(a1_ref, w1, w2, wo, a2_out, d2_out, a3_out, d3_out, pred_out):
-    hidden = layer(w1, a1_ref[...], a2_out, d2_out)
+def forward_rest_kernel(p_ref, feat_ref, x_ref, a1_out, d1_out, a2_out, d2_out, a3_out, d3_out, pred_out, w0, w1, w2, wo):
+    load_weights(p_ref, feat_ref[...], w0, w1, w2, wo)
+    hidden = layer(w0, x_ref[...], a1_out, d1_out)
+    hidden = layer(w1, hidden, a2_out, d2_out)
     hidden = layer(w2, hidden, a3_out, d3_out)
     pred_out[...] = dot_tn(wo[...], hidden)
 
@@ -212,8 +213,8 @@
 
         @pl.when(role_even == even)
         def _():
-            pad[:, 0:2, 8:72, :] = (xb_ref if even else xa_ref)[...]
-            pad[:, 10:12, 8:72, :] = (xa_ref if even else xb_ref)[...]
+            pad[:, 0:2, 8:72, :] = (xb_ref if even else xa_ref)[...].astype(F32)
+            pad[:, 10:12, 8:72, :] = (xa_ref if even else xb_ref)[...].astype(F32)
 
         @pl.when(tile_even == even)
         def _():
@@ -279,18 +280,26 @@
     weight = multiplicity(index_ref, count_ref) * row_scale
     weight = jnp.concatenate([weight[q : q + 1] for q in range(8)], axis=1)
     fill_padded(pad, rank_ref, n_tile, v_ref, xa_ref, xb_ref, ya_ref, yb_ref)
-    target = cells_to_patches(stress_blocks(pad), row_ref[...], lane_ref[...], feat_ref[...], 6)
+    target = cells_to_patches(stress_blocks(pad), row_ref[...], lane_ref[...], 6)
     error = ((pred_ref[...] - target.astype(F32)) * weight).astype(BF16)
     grad = dot_nt(a3_ref[...], error)
     for k in range(3):
-        grads[pl.ds(WO_AT + k, HID, stride=3), :] = grad[:, k * 128 : (k + 1) * 128]
+        part = grad[:, k * 128 : (k + 1) * 128]
+        high = part.astype(BF16)
+        low = (part - high.astype(F32)).astype(BF16)
+        grads[pl.ds(WO_AT + k, HID, stride=3), :] = dot_nt(high, feat_ref[...]) + dot_nt(low, feat_ref[...])
     up = dot(wo[...], error)
     for d_ref, left_ref, at, w in ((d3_ref, a2_ref, W2_AT, w2), (d2_ref, a1_ref, W1_AT, w1), (d1_ref, x_ref, 0, None)):
         slope = (up * d_ref[...]).astype(BF16)
         grad = dot_nt(left_ref[...], slope)
         size = left_ref.shape[0]
         for k in range(4):
-            grads[pl.ds(at + k, size, stride=4), :] = grad[:, k * 128 : (k + 1) * 128]
+            lanes = slice(k * 128, (k + 1) * 128)
+            if w is None:
+                for src, dst in first_rows():
+                    grads[pl.ds(dst + k, 16, stride=16), :] = grad[src : src + 16, lanes]
+            else:
+                grads[pl.ds(at + k, size, stride=4), :] = grad[:, lanes]
         if w is not None:
             up = dot(w[...], slope)
     if in_order:
@@ -319,7 +328,7 @@
     return out
 
 
-def flow_kernel(n_tile, rank_ref, v_ref, xa_ref, xb_ref, ya_ref, yb_ref, row_ref, lane_ref, feat_ref, flow_out, x_out, xa_out, xb_out, ya_out, yb_out, pad, mid):
+def flow_kernel(n_tile, rank_ref, v_ref, xa_ref, xb_ref, ya_ref, yb_ref, row_ref, lane_ref, flow_out, x_out, xa_out, xb_out, ya_out, yb_out, pad, mid):
     fill_padded(pad, rank_ref, n_tile, v_ref, xa_ref, xb_ref, ya_ref, yb_ref)
     for src, dst, first, count, low, high in ((pad, mid, 1, 10, 7, 73), (mid, flow_out, 2, 8, 8, 72)):
         for i in range(first, first + count):
@@ -334,7 +343,7 @@
                     mid[c, i, low:high, :] = new[c]
                 else:
                     flow_out[c, i - 2] = new[c]
-    x = cells_to_patches(velocity_blocks(flow_out), row_ref[...], lane_ref[...], feat_ref[...], 3)
+    x = cells_to_patches(velocity_blocks(flow_out), row_ref[...], lane_ref[...], 3)
     x_out[...] = x
     role_even, tile_even = parity(rank_ref, n_tile)
     halves = (x[:, :512], x[:, 512:])
@@ -352,24 +361,27 @@
             (ya_out if even else yb_out)[...] = edges[1]
 
 
-def model_kernel(rows, masks, n_tile, in_order, rank_ref, p_ref, own_ref, other_ref, flow_ref, x_ref, xa_ref, xb_ref, ya_ref, yb_ref, row_ref, lane_ref,
-                 feat_ref, p_hbm, v_hbm, force_hbm, p_new, w0, w1, w2, wo, x_all, cells, side, edge, pad, v_new, force_new, sems):
+def model_kernel(rows, masks, n_tile, in_order, rank_ref, p_ref, own_a, own_b, other_a, other_b, flow_ref, x_ref, xa_ref, xb_ref, ya_ref, yb_ref, row_ref, lane_ref,
+                 feat_ref, side_ref, p_hbm, v_hbm, force_hbm, p_new, w0, w1, w2, wo, x_all, cells, side, edge, pad, v_new, force_new, sems):
     if in_order:
-        half = own_ref.shape[0]
+        half, cut = own_a.shape[0], own_a.shape[1]
 
         def place(i, carry):
-            here = pl.ds(pl.multiple_of(block_of(i, rank_ref[0], masks, n_tile, False) * rows, 8), rows)
-            p_new[here, :] = p_ref[here, :] - own_ref[i].astype(F32)
-            here = pl.ds(pl.multiple_of(block_of(i + half, rank_ref[0], masks, n_tile, True) * rows, 8), rows)
-            p_new[here, :] = p_ref[here, :] - other_ref[i].astype(F32)
+            for low, high, at, send in ((own_a, own_b, i, False), (other_a, other_b, i + half, True)):
+                base = block_of(at, rank_ref[0], masks, n_tile, send) * rows
+                here = pl.ds(pl.multiple_of(base, 8), cut)
+                p_new[here, :] = p_ref[here, :] - low[i].astype(F32)
+                here = pl.ds(pl.multiple_of(base + cut, 8), rows - cut)
+                p_new[here, :] = p_ref[here, :] - high[i].astype(F32)
             return carry
 
         lax.fori_loop(0, half, place, 0)
     else:
-        p_new[...] = p_ref[...] - own_ref[...].astype(F32)
+        p_new[...] = p_ref[...] - own_a[...].astype(F32)
     copies = [pltpu.make_async_copy(p_new, p_hbm, sems.at[0])]
     copies[0].start()
-    load_weights(p_new, w0, w1, w2, wo)
+    load_weights(p_new, feat_ref[...], w0, w1, w2, wo)
+    w_side = dot(wo[...], side_ref[...]).astype(BF16)
     role_even, tile_even = parity(rank_ref, n_tile)
     x_all[:, 0:1024] = x_ref[...]
     low = lax.broadcasted_iota(jnp.int32, (FEAT, 128), 1) < 64
@@ -389,30 +401,33 @@
     for w in (w0, w1, w2):
         z = dot_tn(w[...], hidden)
         hidden = (z * (0.5 * jnp.tanh(0.5 * z) + 0.5)).astype(BF16)
-    modelled = regroup_features(feat_ref[...], dot_tn(wo[...], hidden).astype(BF16))
-    groups = []
-    for k in range(6):
-        groups += [modelled[k * 64 : k * 64 + 64, q * 128 : q * 128 + 128] for q in range(8)]
-    for first in (8, 12):
-        for k in (0, 3, 4):
-            groups += [modelled[k * 64 : k * 64 + 64, q * 128 : q * 128 + 128] for q in range(first, first + 4)]
-    groups += [modelled[k * 64 : k * 64 + 64, 2048:2176] for k in (3, 1, 5)]
-    spread = spread_rows(jnp.concatenate(groups, axis=0), lane_ref[...])
-    blocks = rows_to_blocks(spread[: 18 * 64], row_ref[...])
-    for k in range(6):
-        for px in range(2):
-            cells[k, px * 4 : px * 4 + 4] = blocks[k * 2 + px].reshape(4, CY, CZ)
-    for i in range(3):
-        side[0, i] = blocks[12 + i][3 * CY :]
-        side[1, i] = blocks[15 + i][:CY]
-    for slot in range(4):
-        edge[slot] = spread[18 * 64 :, slot * 128 : slot * 128 + 128].astype(F32)
-    for i, k in enumerate((3, 1, 5)):
-        pad[i, :, 8:72, :] = cells[k]
+    modelled = dot_tn(wo[...], hidden[:, :1024]).astype(BF16)
+    sides = dot_tn(w_side, hidden[:, 1024:2048]).astype(BF16)
+    edges = dot_tn(wo[...], hidden[:, 2048:]).astype(BF16)
+    for stage, ready in enumerate(((0, 3, 4), (1, 5), (2,))):
+        groups = []
+        for k in ready:
+            groups += [modelled[k * 64 : k * 64 + 64, q * 128 : q * 128 + 128] for q in range(8)]
+        if stage == 0:
+            groups += [sides[q // 4 * 64 : q // 4 * 64 + 64, q * 128 : q * 128 + 128] for q in range(8)]
+            groups += [edges[k * 64 : k * 64 + 64] for k in (3, 1, 5)]
+        spread = spread_rows(jnp.concatenate(groups, axis=0), lane_ref[...])
+        whole = spread.shape[0] // 64
+        blocks = rows_to_blocks(spread[: whole * 64], row_ref[...])
+        for n, k in enumerate(ready):
+            for px in range(2):
+                cells[k, px * 4 : px * 4 + 4] = blocks[n * 2 + px].reshape(4, CY, CZ)
+        if stage == 0:
+            for i in range(3):
+                side[0, i] = blocks[6][i * CY : (i + 1) * CY]
+                side[1, i] = blocks[7][i * CY : (i + 1) * CY]
+            for slot in range(4):
+                edge[slot] = spread[whole * 64 :, slot * 128 : slot * 128 + 128].astype(F32)
+        i = stage
+        pad[i, :, 8:72, :] = cells[(3, 1, 5)[i]]
         for px in range(2):
             pad[i, px * 4 : px * 4 + 4, 7, :] = edge[px, pl.ds(i * 16 + 3, 4, stride=4), :]
             pad[i, px * 4 : px * 4 + 4, 72, :] = edge[2 + px, pl.ds(i * 16, 4, stride=4), :]
-    for i in range(3):
         kx, kz = COMPONENT[i][0], COMPONENT[i][2]
         for x in range(CX):
             after = cells[kx, x + 1] if x < CX - 1 else side[1, i]
@@ -442,7 +457,7 @@
         in_specs=[pl.BlockSpec(memory_space=pltpu.SMEM)] * scalars
         + [pl.BlockSpec(memory_space=space[hbm_in])] * (len(args) - scalars),
         out_specs=[pl.BlockSpec(memory_space=space[hbm_out])] * len(outs),
-        scratch_shapes=[pltpu.VMEM(s, t) for s, t in scratch] + ([pltpu.SemaphoreType.DMA((sems,))] if sems else []),
+        scratch_shapes=[s if isinstance(s, pl.MemoryRef) else pltpu.VMEM(*s) for s in scratch] + ([pltpu.SemaphoreType.DMA((sems,))] if sems else []),
         compiler_params=pltpu.CompilerParams(vmem_limit_bytes=VMEM_LIMIT),
         cost_estimate=pl.CostEstimate(flops=flops, transcendentals=0, bytes_accessed=size),
         name=name,
@@ -501,33 +516,33 @@
     selected = patch_index.shape[0]
     row_scale = 1.0 / (selected // 4)
 
-    first, last = velocity[:, :2], velocity[:, CX - 2 :]
+    first, last = velocity[:, :2].astype(BF16), velocity[:, CX - 2 :].astype(BF16)
     xb = lax.ppermute(jnp.where(role_even, first, last), "role", role_swaps[1])
     xa = lax.ppermute(jnp.where(role_even, last, first), "role", role_swaps[0])
-    v_in, p_in, row_mat, lane_mat, feat_mat, x, a1, d1, *weights = call(
+    v_in, p_in, row_mat, lane_mat, feat_mat, side_mat, index, x = call(
         forward_first_kernel,
         [((3, CX, CY, CZ), F32), ((ROWS, 128), F32), ((256, 256), BF16), ((512, 512), BF16), ((128, 128), BF16)]
-        + [((FEAT, NPATCH), BF16), ACT, DER]
-        + WEIGHTS,
-        [velocity, p2] + [jnp.asarray(m, BF16) for m in (row_matrix(), lane_matrix(), feature_matrix())],
+        + [((TGT, 128), BF16), ((1, selected), jnp.int32), ((FEAT, NPATCH), BF16)],
+        [velocity, p2]
+        + [jnp.asarray(m, BF16) for m in (row_matrix(), lane_matrix(), feature_matrix(), side_matrix())]
+        + [patch_index.reshape(1, selected)],
         [],
-        flops=2 * FEAT * HID * NPATCH,
+        flops=1 << 28,
         name="forward_first",
-        sems=5,
+        sems=7,
         hbm_in=True,
     )
-    mats = [row_mat, lane_mat, feat_mat]
-    xa, xb, v_in, a1 = lax.optimization_barrier((xa, xb, v_in, a1))
+    xa, xb, v_in, x = lax.optimization_barrier((xa, xb, v_in, x))
     strip = ((3, CX + 4, 2, CZ), F32)
     ya, yb = call(functools.partial(strips_kernel, n_tile), [strip] * 2, [rank, v_in, xa, xb], [], scalars=1, name="strips")
     yb = lax.ppermute(yb, "tile", tile_swaps[1])
     ya = lax.ppermute(ya, "tile", tile_swaps[0])
-    a2, d2, a3, d3, pred = call(
+    a1, d1, a2, d2, a3, d3, pred, *weights = call(
         forward_rest_kernel,
-        [ACT, DER, ACT, DER, ((TGT, NPATCH), F32)],
-        [a1] + weights[1:],
+        [ACT, DER, ACT, DER, ACT, DER, ((TGT, NPATCH), F32)] + WEIGHTS,
+        [p_in, feat_mat, x],
         [],
-        flops=2 * (819200 - FEAT * HID) * NPATCH,
+        flops=2 * 819200 * NPATCH,
         name="forward_rest",
     )
     halos = [xa, xb, ya, yb]
@@ -536,9 +551,9 @@
     grads = call(
         functools.partial(backward_kernel, row_scale, rows, masks, n_tile, in_order),
         grad_outs,
-        [rank, patch_count, patch_index.reshape(1, selected), v_in]
+        [rank, patch_count, index, v_in]
         + halos
-        + mats
+        + [row_mat, lane_mat, feat_mat]
         + weights[1:]
         + [x, a1, a2, a3, d1, d2, d3, pred],
         [PADDED] + ([((ROWS, 128), F32)] if in_order else []),
@@ -582,7 +597,7 @@
                 [((3, CX, CY, CZ), F32), ((FEAT, NPATCH), BF16)]
                 + [((FEAT, NPATCH // 2), BF16)] * 2
                 + [((FEAT, 128), BF16)] * 2,
-                [rank, still] + halos + mats,
+                [rank, still] + halos + [row_mat, lane_mat],
                 [PADDED, PADDED],
                 scalars=1,
                 flops=1 << 30,
@@ -607,26 +622,29 @@
     fix_second = 1.0 - BETA_TWO**ADAM_STEP
     update = LEARN_RATE * (first_two / fix_first) / (jnp.sqrt(second_two / fix_second) + EPSILON)
     held = update.astype(BF16).reshape(2, rows, 128)
+    at = rows // 16 * 8
+    held = [held[:, :at], held[:, at:]]
     for step in range(steps - 2, 0, -1):
         if step == 2:
-            held, fyb = fence((held, fyb))
-        got = exchange(held, step)
+            held[0], fyb = fence((held[0], fyb))
+        got = [exchange(part, step) for part in held]
         if step == 2:
             fyb = lax.ppermute(fyb, "tile", tile_swaps[1])
         if step == 1:
-            got, fyb = fence((got, fyb))
+            got[0], fyb = fence((got[0], fyb))
         if step == steps - 2:
-            got, fxa, fya = fence((got, fxa, fya))
-        held = jnp.concatenate([held, got], axis=0)
-    other = exchange(held, 0)
+            got[0], fxa, fya = fence((got[0], fxa, fya))
+        held = [jnp.concatenate([part, new], axis=0) for part, new in zip(held, got)]
+    other = [exchange(part, 0) for part in held]
     if not in_order:
         slots = jnp.zeros((devices,), jnp.int32).at[order].set(jnp.arange(devices, dtype=jnp.int32))
-        held = other = jnp.concatenate([held, other], axis=0)[slots].reshape(ROWS, 128)
+        all_parts = jnp.concatenate([jnp.concatenate(held, axis=1), jnp.concatenate(other, axis=1)], axis=0)
+        held = other = [all_parts[slots].reshape(ROWS, 128)] * 2
 
     p_new, velocity_out, sgs_force = call(
         functools.partial(model_kernel, rows, masks, n_tile, in_order),
         [((ROWS, 128), F32)] + [((3, CX, CY, CZ), F32)] * 2,
-        [rank, p_in, held, other, flow, x_new, fxa, fxb, fya, fyb] + mats,
+        [rank, p_in, *held, *other, flow, x_new, fxa, fxb, fya, fyb, row_mat, lane_mat, feat_mat, side_mat],
         [((ROWS, 128), F32)]
         + WEIGHTS
         + [((FEAT, 17 * 128), BF16), ((6, CX, CY, CZ), F32), ((2, 3, CY, CZ), F32), ((4, 48, 128), F32), ((3, CX, 80, CZ), F32)]

time: 84.4 us -> 79.4 us (0.941)
  waiting for transfers between devices: 36.8 us -> 27.9 us
  starting transfers between devices: 19.2 us -> 23 us
    ppermute x1, waiting for transfers between devices: 4.56 us -> 0.01 us  [local(): fyb = lax.ppermute(fyb, 'tile', tile_swaps[1])]
    ppermute x10 -> x14, starting transfers between devices: 7.37 us -> 10.7 us  [exchange(): return lax.ppermute(x, BOTH, pairs)]
    ppermute x1, waiting for transfers between devices: 3.27 us -> 0.01 us  [local(): fya = lax.ppermute(fya, 'tile', tile_swaps[0])]
    another operation x0 -> x1, other arithmetic: none -> 1.2 us
    select_n x1, other arithmetic: 1.06 us -> 0.02 us  [local(): xb = lax.ppermute(jnp.where(role_even, first, last), 'role', role_swaps[1])]
    ppermute x1, waiting for transfers between devices: 1.03 us -> 0.01 us  [local(): yb = lax.ppermute(yb, 'tile', tile_swaps[1])]
    ppermute x1, waiting for transfers between devices: 0.87 us -> 0.01 us  [local(): xb = lax.ppermute(jnp.where(role_even, first, last), 'role', role_swaps[1])]
    ppermute x10 -> x14, waiting for transfers between devices: 25.7 us -> 26.2 us  [exchange(): return lax.ppermute(x, BOTH, pairs)]
  transfers between devices with their start and end apart: 18 -> 22, of which waited for: 14 -> 12; matrix products, arithmetic and copies ran while one was open for 2% -> 3% of each run, Pallas kernels for 10% -> 10%
where the time goes in v4:
time: 79.4 us; the launch traced here: 79.3 us
  waiting for transfers between devices  27.9 us (35%)
  Pallas kernels  23.1 us (29%)
  starting transfers between devices  23 us (29%)
  other arithmetic  3.24 us (4%)
  between operations  1.73 us (2%)
    ppermute x14, waiting for transfers between devices, exchange(): return lax.ppermute(x, BOTH, pairs)  26.2 us
    pallas_call x6, Pallas kernels, call(): pl.pallas_call(kernel, out_shape=[space[hbm_out](s, t) for s, t in outs],...  23.1 us
    ppermute x14, starting transfers between devices, exchange(): return lax.ppermute(x, BOTH, pairs)  10.7 us
    ppermute x1, starting transfers between devices, local(): yb = lax.ppermute(yb, 'tile', tile_swaps[1])  3.57 us
    ppermute x1, starting transfers between devices, local(): fyb = lax.ppermute(fyb, 'tile', tile_swaps[1])  2.87 us
    ppermute x1, starting transfers between devices, local(): xb = lax.ppermute(jnp.where(role_even, first, last), 'role', role_swaps[1])  2.64 us
    ppermute x1, waiting for transfers between devices, local(): fxb = lax.ppermute(fxb, 'role', role_swaps[1])  1.66 us
  transfers between devices with their start and end apart: 22, of which 12 were waited for; matrix products, arithmetic and copies ran while one was open for 3% of the time, Pallas kernels for 10%

profile of v4, /device:TPU:0, one launch (start us, length us, event | category | flops | bytes accessed | tf_op | source)
XLA Modules:
  0.0 79.3 jit_solution(3548337550790973184)
XLA Ops:
  2.4 2.6 %collective-permute-start.1 = (bf16[3,2,64,128]{3,2,1,0:T(8,128)(2,1)S(1)}, bf16[3,2,64,128]{3,2,1,0:T(8,128)(2,1)S(1)}, u32[]{:S(2)}, u32[]{:S(2)}) collective-permute-start(bf16[3,2,64,128]{3,2,1,0:T(8,128)(2,1)S(1)} %get-tuple-element.131), channel_id=1, source_target_pairs={{0,24},{8,16},{16,8},{24,0},{1,25},{9,17},{17,9},{25,1},{2,26},{10... | collective-permute-start | bytes 294920 | tf_op jit(solution)/shard_map/ppermute | solution.py:520
  5.7 2.4 %forward_first.1 = (f32[3,8,64,128]{3,2,1,0:T(8,128)S(1)}, f32[6400,128]{1,0:T(8,128)S(1)}, bf16[256,256]{1,0:T(8,128)(2,1)S(1)}, bf16[512,512]{1,0:T(8,128)(2,1...) custom-call(f32[3,8,64,128]{3,2,1,0:T(8,128)} %v_hbm.1, ...), custom_call_target="tpu_custom_call" | custom-call | flops 268435456 | bytes 10108928 | tf_op jit(solution)/shard_map/forward_first/pallas_call | solution.py:454
  8.2 1.6 %collective-permute-start.2 = (f32[3,12,2,128]{3,2,1,0:T(2,128)S(1)}, f32[3,12,2,128]{3,2,1,0:T(2,128)S(1)}, u32[]{:S(2)}, u32[]{:S(2)}) collective-permute-start(f32[3,12,2,128]{3,2,1,0:T(2,128)S(1)} %get-tuple-element.73), channel_id=1, source_target_pairs={{0,1},{1,0},{2,3},{3,2},{4,5},{5,4},{6,7},{7,6},{8,9},{9,8},{10,11... | collective-permute-start | bytes 110600 | tf_op jit(solution)/shard_map/ppermute | solution.py:539
  9.8 3.6 %collective-permute-start.3 = (f32[3,12,2,128]{3,2,1,0:T(2,128)S(1)}, f32[3,12,2,128]{3,2,1,0:T(2,128)S(1)}, u32[]{:S(2)}, u32[]{:S(2)}) collective-permute-start(f32[3,12,2,128]{3,2,1,0:T(2,128)S(1)} %get-tuple-element.74), channel_id=1, source_target_pairs={{0,7},{1,2},{2,1},{3,4},{4,3},{5,6},{6,5},{7,0},{8,15},{9,10},{10,... | collective-permute-start | bytes 110600 | tf_op jit(solution)/shard_map/ppermute | solution.py:538
  13.4 3.3 %forward_rest.1 = (bf16[512,1024]{1,0:T(8,128)(2,1)S(1)}, f32[512,1024]{1,0:T(8,128)S(1)}, bf16[512,1024]{1,0:T(8,128)(2,1)S(1)}, f32[512,1024]{1,0:T(8,128)S(1)...) custom-call(f32[6400,128]{1,0:T(8,128)S(1)} %get-tuple-element.66.p_, ...), custom_call_target="tpu_custom_call" | custom-call | flops 1677721600 | bytes 16351232 | tf_op jit(solution)/shard_map/forward_rest/pallas_call | solution.py:454
  16.7 7.0 %backward.1 = (bf16[16,200,128]{2,1,0:T(8,128)(2,1)S(1)}, f32[16,200,128]{2,1,0:T(8,128)S(1)}) custom-call(s32[1]{0:T(128)} %bitcast.rank_ref, s32[1]{0:T(128)S(6)} %copy.20.count_ref, s32[1,2048]{1,0:T(1,128)S(1)} %get-tuple-element.67.index_ref, f32[3,8,64,128]{3,2,1,0:T(8,128)S(1)} %get-tuple-element.92.v_ref, ...), custom_call_target="tpu_custom_call" | custom-call | flops 3355443200 | bytes 17055752 | tf_op jit(solution)/shard_map/backward/pallas_call | solution.py:454
  24.0 2.1 %collective-permute-done.4 = bf16[16,200,128]{2,1,0:T(8,128)(2,1)S(1)} collective-permute-done((bf16[16,200,128]{2,1,0:T(8,128)(2,1)S(1)}, bf16[16,200,128]{2,1,0:T(8,128)(2,1)S(1)}, u32[]{:S(2)}, u32[]{:S(2)}) %collective-permute-start.4) | collective-permute-done | bytes 819232 | tf_op jit(solution)/shard_map/ppermute | solution.py:503
  26.4 2.1 %collective-permute-start.7 = (f32[2,25600]{1,0:T(2,128)S(1)}, f32[2,25600]{1,0:T(2,128)S(1)}, u32[]{:S(2)}, u32[]{:S(2)}) collective-permute-start(f32[2,25600]{1,0:T(2,128)S(1)} %pad_maximum_fusion.2), channel_id=1, source_target_pairs={{0,4},{1,5},{2,6},{3,7},{4,0},{5,1},{6,2},{7,3},{8,12},{9,13},{10,... | collective-permute-start | bytes 614408 | tf_op jit(solution)/shard_map/ppermute | solution.py:503
  28.4 2.4 %flow.1 = (f32[3,8,64,128]{3,2,1,0:T(8,128)S(1)}, bf16[192,1024]{1,0:T(8,128)(2,1)S(1)}, bf16[192,512]{1,0:T(8,128)(2,1)S(1)}, bf16[192,512]{1,0:T(8,128)(2,1)S(...) custom-call(s32[1]{0:T(128)} %bitcast.rank_ref, f32[3,8,64,128]{3,2,1,0:T(8,128)S(1)} %get-tuple-element.92.v_ref, ...), custom_call_target="tpu_custom_call" | custom-call | flops 1073741824 | bytes 3383300 | tf_op jit(solution)/shard_map/flow/pallas_call | solution.py:454
  30.8 3.5 %collective-permute-done.5 = bf16[8,200,128]{2,1,0:T(8,128)(2,1)S(1)} collective-permute-done((bf16[8,200,128]{2,1,0:T(8,128)(2,1)S(1)}, bf16[8,200,128]{2,1,0:T(8,128)(2,1)S(1)}, u32[]{:S(2)}, u32[]{:S(2)}) %collective-permute-start.5) | collective-permute-done | bytes 409632 | tf_op jit(solution)/shard_map/ppermute | solution.py:503
  34.4 1.4 %collective-permute-start.6 = (bf16[4,200,128]{2,1,0:T(8,128)(2,1)S(1)}, bf16[4,200,128]{2,1,0:T(8,128)(2,1)S(1)}, u32[]{:S(2)}, u32[]{:S(2)}) collective-permute-start(bf16[4,200,128]{2,1,0:T(8,128)(2,1)S(1)} %get-tuple-element.130), channel_id=1, source_target_pairs={{0,16},{1,17},{2,18},{3,19},{4,20},{5,21},{6,22},{7,23},{8,9},{9,8... | collective-permute-start | bytes 614408 | tf_op jit(solution)/shard_map/ppermute | solution.py:503
  35.8 3.0 %collective-permute-done.7 = f32[2,25600]{1,0:T(2,128)S(1)} collective-permute-done((f32[2,25600]{1,0:T(2,128)S(1)}, f32[2,25600]{1,0:T(2,128)S(1)}, u32[]{:S(2)}, u32[]{:S(2)}) %collective-permute-start.7) | collective-permute-done | bytes 204832 | tf_op jit(solution)/shard_map/ppermute | solution.py:503
  38.8 1.4 %collective-permute-done.6 = bf16[4,200,128]{2,1,0:T(8,128)(2,1)S(1)} collective-permute-done((bf16[4,200,128]{2,1,0:T(8,128)(2,1)S(1)}, bf16[4,200,128]{2,1,0:T(8,128)(2,1)S(1)}, u32[]{:S(2)}, u32[]{:S(2)}) %collective-permute-start.6) | collective-permute-done | bytes 204832 | tf_op jit(solution)/shard_map/ppermute | solution.py:503
  40.4 4.6 %collective-permute-done.8 = bf16[2,200,128]{2,1,0:T(8,128)(2,1)S(1)} collective-permute-done((bf16[2,200,128]{2,1,0:T(8,128)(2,1)S(1)}, bf16[2,200,128]{2,1,0:T(8,128)(2,1)S(1)}, u32[]{:S(2)}, u32[]{:S(2)}) %collective-permute-start.8) | collective-permute-done | bytes 102432 | tf_op jit(solution)/shard_map/ppermute | solution.py:503
  45.8 1.7 %collective-permute-done.10.xb_ref = bf16[192,512]{1,0:T(8,128)(2,1)S(1)} collective-permute-done((bf16[192,512]{1,0:T(8,128)(2,1)S(1)}, bf16[192,512]{1,0:T(8,128)(2,1)S(1)}, u32[]{:S(2)}, u32[]{:S(2)}) %collective-permute-start.10) | collective-permute-done | bytes 196640 | tf_op jit(solution)/shard_map/ppermute | solution.py:610
  47.5 3.7 %collective-permute-done.9 = bf16[2,200,128]{2,1,0:T(8,128)(2,1)S(1)} collective-permute-done((bf16[2,200,128]{2,1,0:T(8,128)(2,1)S(1)}, bf16[2,200,128]{2,1,0:T(8,128)(2,1)S(1)}, u32[]{:S(2)}, u32[]{:S(2)}) %collective-permute-start.9) | collective-permute-done | bytes 102432 | tf_op jit(solution)/shard_map/ppermute | solution.py:503
  52.6 1.6 %collective-permute-start.11 = (bf16[2,96,128]{2,1,0:T(8,128)(2,1)S(1)}, bf16[2,96,128]{2,1,0:T(8,128)(2,1)S(1)}, u32[]{:S(2)}, u32[]{:S(2)}) collective-permute-start(bf16[2,96,128]{2,1,0:T(8,128)(2,1)S(1)} %slice.90), channel_id=1, source_target_pairs={{0,2},{1,3},{2,0},{3,1},{4,6},{5,7},{6,4},{7,5},{8,10},{9,11},{10,... | collective-permute-start | bytes 147464 | tf_op jit(solution)/shard_map/ppermute | solution.py:503
  54.2 1.4 %collective-permute-done.17 = bf16[2,104,128]{2,1,0:T(8,128)(2,1)S(1)} collective-permute-done((bf16[2,104,128]{2,1,0:T(8,128)(2,1)S(1)}, bf16[2,104,128]{2,1,0:T(8,128)(2,1)S(1)}, u32[]{:S(2)}, u32[]{:S(2)}) %collective-permute-start.17) | collective-permute-done | bytes 53280 | tf_op jit(solution)/shard_map/ppermute | solution.py:503
  55.6 1.4 %collective-permute-start.18 = (bf16[4,104,128]{2,1,0:T(8,128)(2,1)S(1)}, bf16[4,104,128]{2,1,0:T(8,128)(2,1)S(1)}, u32[]{:S(2)}, u32[]{:S(2)}) collective-permute-start(bf16[4,104,128]{2,1,0:T(8,128)(2,1)S(1)} %pad_maximum_fusion.4), channel_id=1, source_target_pairs={{0,16},{1,17},{2,18},{3,19},{4,20},{5,21},{6,22},{7,23},{8,9},{9,8... | collective-permute-start | bytes 319496 | tf_op jit(solution)/shard_map/ppermute | solution.py:503
  58.2 2.9 %collective-permute-start.16 = (bf16[192,128]{1,0:T(8,128)(2,1)S(1)}, bf16[192,128]{1,0:T(8,128)(2,1)S(1)}, u32[]{:S(2)}, u32[]{:S(2)}) collective-permute-start(bf16[192,128]{1,0:T(8,128)(2,1)S(1)} %get-tuple-element.115), channel_id=1, source_target_pairs={{0,7},{1,2},{2,1},{3,4},{4,3},{5,6},{6,5},{7,0},{8,15},{9,10},{10,... | collective-permute-start | bytes 147464 | tf_op jit(solution)/shard_map/ppermute | solution.py:632
  64.2 3.1 %collective-permute-done.19 = bf16[8,104,128]{2,1,0:T(8,128)(2,1)S(1)} collective-permute-done((bf16[8,104,128]{2,1,0:T(8,128)(2,1)S(1)}, bf16[8,104,128]{2,1,0:T(8,128)(2,1)S(1)}, u32[]{:S(2)}, u32[]{:S(2)}) %collective-permute-start.19) | collective-permute-done | bytes 213024 | tf_op jit(solution)/shard_map/ppermute | solution.py:503
  67.4 2.0 %collective-permute-done.15 = bf16[8,96,128]{2,1,0:T(8,128)(2,1)S(1)} collective-permute-done((bf16[8,96,128]{2,1,0:T(8,128)(2,1)S(1)}, bf16[8,96,128]{2,1,0:T(8,128)(2,1)S(1)}, u32[]{:S(2)}, u32[]{:S(2)}) %collective-permute-start.15) | collective-permute-done | bytes 196640 | tf_op jit(solution)/shard_map/ppermute | solution.py:503
  69.5 1.2 %fusion.13 = (f32[1,25600]{1,0:T(1,128)}, f32[1,25600]{1,0:T(1,128)}) fusion(f32[1,25600]{1,0:T(1,128)S(1)} %get-tuple-element.138, f32[1,25600]{1,0:T(1,128)S(1)} %bitcast.20, f32[2,25600]{1,0:T(2,128)S(1)} %bitcast.26, f32[1,25600]{1,0:T(1,128)S(1)} %get-tuple-element.137, f32[1,25600]{1,0:T(1,128)S(1)} %bitcast.23), kind=kLoop, calls=%fused_computation.30 | loop fusion | flops 230400 | bytes 716800 | tf_op jit(solution)/shard_map/add | solution.py:619
  71.2 7.9 %model.1 = (f32[6400,128]{1,0:T(8,128)}, f32[3,8,64,128]{3,2,1,0:T(8,128)}, f32[3,8,64,128]{3,2,1,0:T(8,128)}) custom-call(s32[1]{0:T(128)} %bitcast.rank_ref, f32[6400,128]{1,0:T(8,128)S(1)} %get-tuple-element.66.p_ref, bf16[16,96,128]{2,1,0:T(8,128)(2,1)S(1)} %constant_dynamic-update-slice_fusion.own_a, bf16[16,104,128]{2,1,0:T(8,128)(2,1)S(1)} %pad_maximum_fusion.own_b, ...), custom_call_target="tpu_custom_call" | custom-call | flops 3355443200 | bytes 12222468 | tf_op jit(solution)/shard_map/model/pallas_call | solution.py:454
  (51 shorter events, 9.7 us)
Async XLA Ops:
  1.9 6.3 %collective-permute-start = (bf16[3,2,64,128]{3,2,1,0:T(8,128)(2,1)S(1)}, bf16[3,2,64,128]{3,2,1,0:T(8,128)(2,1)S(1)}, u32[]{:S(2)}, u32[]{:S(2)}) collective-permute-start(bf16[3,2,64,128]{3,2,1,0:T(8,128)(2,1)S(1)} %get-tuple-element.132), channel_id=1, source_target_pairs={{0,8},{8,0},{16,24},{24,16},{1,9},{9,1},{17,25},{25,17},{2,10},{10... | collective-permute-start | bytes 294920 | tf_op jit(solution)/shard_map/ppermute | solution.py:521
  2.4 5.8 %collective-permute-start.1 = (bf16[3,2,64,128]{3,2,1,0:T(8,128)(2,1)S(1)}, bf16[3,2,64,128]{3,2,1,0:T(8,128)(2,1)S(1)}, u32[]{:S(2)}, u32[]{:S(2)}) collective-permute-start(bf16[3,2,64,128]{3,2,1,0:T(8,128)(2,1)S(1)} %get-tuple-element.131), channel_id=1, source_target_pairs={{0,24},{8,16},{16,8},{24,0},{1,25},{9,17},{17,9},{25,1},{2,26},{10... | collective-permute-start | bytes 294920 | tf_op jit(solution)/shard_map/ppermute | solution.py:520
  8.2 8.5 %collective-permute-start.2 = (f32[3,12,2,128]{3,2,1,0:T(2,128)S(1)}, f32[3,12,2,128]{3,2,1,0:T(2,128)S(1)}, u32[]{:S(2)}, u32[]{:S(2)}) collective-permute-start(f32[3,12,2,128]{3,2,1,0:T(2,128)S(1)} %get-tuple-element.73), channel_id=1, source_target_pairs={{0,1},{1,0},{2,3},{3,2},{4,5},{5,4},{6,7},{7,6},{8,9},{9,8},{10,11... | collective-permute-start | bytes 110600 | tf_op jit(solution)/shard_map/ppermute | solution.py:539
  9.8 6.9 %collective-permute-start.3 = (f32[3,12,2,128]{3,2,1,0:T(2,128)S(1)}, f32[3,12,2,128]{3,2,1,0:T(2,128)S(1)}, u32[]{:S(2)}, u32[]{:S(2)}) collective-permute-start(f32[3,12,2,128]{3,2,1,0:T(2,128)S(1)} %get-tuple-element.74), channel_id=1, source_target_pairs={{0,7},{1,2},{2,1},{3,4},{4,3},{5,6},{6,5},{7,0},{8,15},{9,10},{10,... | collective-permute-start | bytes 110600 | tf_op jit(solution)/shard_map/ppermute | solution.py:538
  16.7 7.1 %copy-start = (f32[25600]{0:T(1024)S(1)}, f32[25600]{0:T(1024)}, u32[]{:S(2)}) copy-start(f32[25600]{0:T(1024)} %param.13) | copy-start | bytes 307204
  16.7 7.1 %copy-start.1 = (f32[25600]{0:T(1024)S(1)}, f32[25600]{0:T(1024)}, u32[]{:S(2)}) copy-start(f32[25600]{0:T(1024)} %param.12) | copy-start | bytes 307204
  23.7 2.4 %collective-permute-start.4 = (bf16[16,200,128]{2,1,0:T(8,128)(2,1)S(1)}, bf16[16,200,128]{2,1,0:T(8,128)(2,1)S(1)}, u32[]{:S(2)}, u32[]{:S(2)}) collective-permute-start(bf16[16,200,128]{2,1,0:T(8,128)(2,1)S(1)} %get-tuple-element.90), channel_id=1, source_target_pairs={{0,8},{1,9},{2,10},{3,11},{4,12},{5,13},{6,14},{7,15},{8,0},{9,1},... | collective-permute-start | bytes 2457608 | tf_op jit(solution)/shard_map/ppermute | solution.py:503
  26.3 8.0 %collective-permute-start.5 = (bf16[8,200,128]{2,1,0:T(8,128)(2,1)S(1)}, bf16[8,200,128]{2,1,0:T(8,128)(2,1)S(1)}, u32[]{:S(2)}, u32[]{:S(2)}) collective-permute-start(bf16[8,200,128]{2,1,0:T(8,128)(2,1)S(1)} %get-tuple-element.91), channel_id=1, source_target_pairs={{0,1},{1,0},{2,3},{3,2},{4,5},{5,4},{6,7},{7,6},{8,24},{9,25},{10,... | collective-permute-start | bytes 1228808 | tf_op jit(solution)/shard_map/ppermute | solution.py:503
  26.4 12.4 %collective-permute-start.7 = (f32[2,25600]{1,0:T(2,128)S(1)}, f32[2,25600]{1,0:T(2,128)S(1)}, u32[]{:S(2)}, u32[]{:S(2)}) collective-permute-start(f32[2,25600]{1,0:T(2,128)S(1)} %pad_maximum_fusion.2), channel_id=1, source_target_pairs={{0,4},{1,5},{2,6},{3,7},{4,0},{5,1},{6,2},{7,3},{8,12},{9,13},{10,... | collective-permute-start | bytes 614408 | tf_op jit(solution)/shard_map/ppermute | solution.py:503
  34.4 5.8 %collective-permute-start.6 = (bf16[4,200,128]{2,1,0:T(8,128)(2,1)S(1)}, bf16[4,200,128]{2,1,0:T(8,128)(2,1)S(1)}, u32[]{:S(2)}, u32[]{:S(2)}) collective-permute-start(bf16[4,200,128]{2,1,0:T(8,128)(2,1)S(1)} %get-tuple-element.130), channel_id=1, source_target_pairs={{0,16},{1,17},{2,18},{3,19},{4,20},{5,21},{6,22},{7,23},{8,9},{9,8... | collective-permute-start | bytes 614408 | tf_op jit(solution)/shard_map/ppermute | solution.py:503
  40.2 4.7 %collective-permute-start.8 = (bf16[2,200,128]{2,1,0:T(8,128)(2,1)S(1)}, bf16[2,200,128]{2,1,0:T(8,128)(2,1)S(1)}, u32[]{:S(2)}, u32[]{:S(2)}) collective-permute-start(bf16[2,200,128]{2,1,0:T(8,128)(2,1)S(1)} %fusion.6), channel_id=1, source_target_pairs={{0,2},{1,3},{2,0},{3,1},{4,6},{5,7},{6,4},{7,5},{8,10},{9,11},{10,... | collective-permute-start | bytes 307208 | tf_op jit(solution)/shard_map/ppermute | solution.py:503
  40.3 7.2 %collective-permute-start.10 = (bf16[192,512]{1,0:T(8,128)(2,1)S(1)}, bf16[192,512]{1,0:T(8,128)(2,1)S(1)}, u32[]{:S(2)}, u32[]{:S(2)}) collective-permute-start(bf16[192,512]{1,0:T(8,128)(2,1)S(1)} %get-tuple-element.108), channel_id=1, source_target_pairs={{0,24},{8,16},{16,8},{24,0},{1,25},{9,17},{17,9},{25,1},{2,26},{10... | collective-permute-start | bytes 589832 | tf_op jit(solution)/shard_map/ppermute | solution.py:610
  45.0 6.2 %collective-permute-start.9 = (bf16[2,200,128]{2,1,0:T(8,128)(2,1)S(1)}, bf16[2,200,128]{2,1,0:T(8,128)(2,1)S(1)}, u32[]{:S(2)}, u32[]{:S(2)}) collective-permute-start(bf16[2,200,128]{2,1,0:T(8,128)(2,1)S(1)} %fusion.8), channel_id=1, source_target_pairs={{0,4},{1,5},{2,6},{3,7},{4,0},{5,1},{6,2},{7,3},{8,12},{9,13},{10,... | collective-permute-start | bytes 307208 | tf_op jit(solution)/shard_map/ppermute | solution.py:503
  45.8 11.3 %collective-permute-start.12 = (bf16[192,512]{1,0:T(8,128)(2,1)S(1)}, bf16[192,512]{1,0:T(8,128)(2,1)S(1)}, u32[]{:S(2)}, u32[]{:S(2)}) collective-permute-start(bf16[192,512]{1,0:T(8,128)(2,1)S(1)} %get-tuple-element.110), channel_id=1, source_target_pairs={{0,8},{8,0},{16,24},{24,16},{1,9},{9,1},{17,25},{25,17},{2,10},{10... | collective-permute-start | bytes 589832 | tf_op jit(solution)/shard_map/ppermute | solution.py:612
  51.4 4.2 %collective-permute-start.17 = (bf16[2,104,128]{2,1,0:T(8,128)(2,1)S(1)}, bf16[2,104,128]{2,1,0:T(8,128)(2,1)S(1)}, u32[]{:S(2)}, u32[]{:S(2)}) collective-permute-start(bf16[2,104,128]{2,1,0:T(8,128)(2,1)S(1)} %slice.91), channel_id=1, source_target_pairs={{0,2},{1,3},{2,0},{3,1},{4,6},{5,7},{6,4},{7,5},{8,10},{9,11},{10,... | collective-permute-start | bytes 159752 | tf_op jit(solution)/shard_map/ppermute | solution.py:503
  51.5 5.6 %collective-permute-start.13 = (bf16[192,128]{1,0:T(8,128)(2,1)S(1)}, bf16[192,128]{1,0:T(8,128)(2,1)S(1)}, u32[]{:S(2)}, u32[]{:S(2)}) collective-permute-start(bf16[192,128]{1,0:T(8,128)(2,1)S(1)} %get-tuple-element.111), channel_id=1, source_target_pairs={{0,1},{1,0},{2,3},{3,2},{4,5},{5,4},{6,7},{7,6},{8,9},{9,8},{10,11... | collective-permute-start | bytes 147464 | tf_op jit(solution)/shard_map/ppermute | solution.py:613
  52.6 4.4 %collective-permute-start.11 = (bf16[2,96,128]{2,1,0:T(8,128)(2,1)S(1)}, bf16[2,96,128]{2,1,0:T(8,128)(2,1)S(1)}, u32[]{:S(2)}, u32[]{:S(2)}) collective-permute-start(bf16[2,96,128]{2,1,0:T(8,128)(2,1)S(1)} %slice.90), channel_id=1, source_target_pairs={{0,2},{1,3},{2,0},{3,1},{4,6},{5,7},{6,4},{7,5},{8,10},{9,11},{10,... | collective-permute-start | bytes 147464 | tf_op jit(solution)/shard_map/ppermute | solution.py:503
  55.6 5.5 %collective-permute-start.18 = (bf16[4,104,128]{2,1,0:T(8,128)(2,1)S(1)}, bf16[4,104,128]{2,1,0:T(8,128)(2,1)S(1)}, u32[]{:S(2)}, u32[]{:S(2)}) collective-permute-start(bf16[4,104,128]{2,1,0:T(8,128)(2,1)S(1)} %pad_maximum_fusion.4), channel_id=1, source_target_pairs={{0,16},{1,17},{2,18},{3,19},{4,20},{5,21},{6,22},{7,23},{8,9},{9,8... | collective-permute-start | bytes 319496 | tf_op jit(solution)/shard_map/ppermute | solution.py:503
  57.1 6.0 %collective-permute-start.14 = (bf16[4,96,128]{2,1,0:T(8,128)(2,1)S(1)}, bf16[4,96,128]{2,1,0:T(8,128)(2,1)S(1)}, u32[]{:S(2)}, u32[]{:S(2)}) collective-permute-start(bf16[4,96,128]{2,1,0:T(8,128)(2,1)S(1)} %pad_maximum_fusion.7), channel_id=1, source_target_pairs={{0,16},{1,17},{2,18},{3,19},{4,20},{5,21},{6,22},{7,23},{8,9},{9,8... | collective-permute-start | bytes 294920 | tf_op jit(solution)/shard_map/ppermute | solution.py:503
  58.2 9.2 %collective-permute-start.16 = (bf16[192,128]{1,0:T(8,128)(2,1)S(1)}, bf16[192,128]{1,0:T(8,128)(2,1)S(1)}, u32[]{:S(2)}, u32[]{:S(2)}) collective-permute-start(bf16[192,128]{1,0:T(8,128)(2,1)S(1)} %get-tuple-element.115), channel_id=1, source_target_pairs={{0,7},{1,2},{2,1},{3,4},{4,3},{5,6},{6,5},{7,0},{8,15},{9,10},{10,... | collective-permute-start | bytes 147464 | tf_op jit(solution)/shard_map/ppermute | solution.py:632
  61.1 6.2 %collective-permute-start.19 = (bf16[8,104,128]{2,1,0:T(8,128)(2,1)S(1)}, bf16[8,104,128]{2,1,0:T(8,128)(2,1)S(1)}, u32[]{:S(2)}, u32[]{:S(2)}) collective-permute-start(bf16[8,104,128]{2,1,0:T(8,128)(2,1)S(1)} %pad_maximum_fusion.1), channel_id=1, source_target_pairs={{0,1},{1,0},{2,3},{3,2},{4,5},{5,4},{6,7},{7,6},{8,24},{9,25},{10,... | collective-permute-start | bytes 638984 | tf_op jit(solution)/shard_map/ppermute | solution.py:503
  63.1 6.2 %collective-permute-start.15 = (bf16[8,96,128]{2,1,0:T(8,128)(2,1)S(1)}, bf16[8,96,128]{2,1,0:T(8,128)(2,1)S(1)}, u32[]{:S(2)}, u32[]{:S(2)}) collective-permute-start(bf16[8,96,128]{2,1,0:T(8,128)(2,1)S(1)} %pad_maximum_fusion.3), channel_id=1, source_target_pairs={{0,1},{1,0},{2,3},{3,2},{4,5},{5,4},{6,7},{7,6},{8,24},{9,25},{10,... | collective-permute-start | bytes 589832 | tf_op jit(solution)/shard_map/ppermute | solution.py:503
  67.3 3.9 %collective-permute-start.21 = (bf16[16,104,128]{2,1,0:T(8,128)(2,1)S(1)}, bf16[16,104,128]{2,1,0:T(8,128)(2,1)S(1)}, u32[]{:S(2)}, u32[]{:S(2)}) collective-permute-start(bf16[16,104,128]{2,1,0:T(8,128)(2,1)S(1)} %pad_maximum_fusion.own_b), channel_id=1, source_target_pairs={{0,8},{1,9},{2,10},{3,11},{4,12},{5,13},{6,14},{7,15},{8,0},{9,1},... | collective-permute-start | bytes 1277960 | tf_op jit(solution)/shard_map/ppermute | solution.py:503
  69.4 1.8 %collective-permute-start.20 = (bf16[16,96,128]{2,1,0:T(8,128)(2,1)S(1)}, bf16[16,96,128]{2,1,0:T(8,128)(2,1)S(1)}, u32[]{:S(2)}, u32[]{:S(2)}) collective-permute-start(bf16[16,96,128]{2,1,0:T(8,128)(2,1)S(1)} %constant_dynamic-update-slice_fusion.own_a), channel_id=1, source_target_pairs={{0,8},{1,9},{2,10},{3,11},{4,12},{5,13},{6,14},{7,15},{8,0},{9,1},... | collective-permute-start | bytes 1179656 | tf_op jit(solution)/shard_map/ppermute | solution.py:503

commit v5 on v4

--- a/solution.py
+++ b/solution.py
@@ -156,13 +156,13 @@
 
 
 def forward_first_kernel(
-    v_hbm, p_hbm, row_hbm, lane_hbm, feat_hbm, side_hbm, index_hbm,
-    v_out, p_out, row_out, lane_out, feat_out, side_out, index_out, x_out, sems
+    v_hbm, row_hbm, lane_hbm, feat_hbm, side_hbm, index_hbm,
+    v_out, row_out, lane_out, feat_out, side_out, index_out, x_out, sems
 ):
     copies = [
         pltpu.make_async_copy(src, dst, sems.at[i])
         for i, (src, dst) in enumerate(
-            ((v_hbm, v_out), (row_hbm, row_out), (lane_hbm, lane_out), (p_hbm, p_out), (feat_hbm, feat_out), (side_hbm, side_out), (index_hbm, index_out))
+            ((v_hbm, v_out), (row_hbm, row_out), (lane_hbm, lane_out), (feat_hbm, feat_out), (side_hbm, side_out), (index_hbm, index_out))
         )
     ]
     for copy in copies:
@@ -284,10 +284,8 @@
     error = ((pred_ref[...] - target.astype(F32)) * weight).astype(BF16)
     grad = dot_nt(a3_ref[...], error)
     for k in range(3):
-        part = grad[:, k * 128 : (k + 1) * 128]
-        high = part.astype(BF16)
-        low = (part - high.astype(F32)).astype(BF16)
-        grads[pl.ds(WO_AT + k, HID, stride=3), :] = dot_nt(high, feat_ref[...]) + dot_nt(low, feat_ref[...])
+        part = grad[:, k * 128 : (k + 1) * 128].astype(BF16)
+        grads[pl.ds(WO_AT + k, HID, stride=3), :] = dot_nt(part, feat_ref[...])
     up = dot(wo[...], error)
     for d_ref, left_ref, at, w in ((d3_ref, a2_ref, W2_AT, w2), (d2_ref, a1_ref, W1_AT, w1), (d1_ref, x_ref, 0, None)):
         slope = (up * d_ref[...]).astype(BF16)
@@ -519,17 +517,17 @@
     first, last = velocity[:, :2].astype(BF16), velocity[:, CX - 2 :].astype(BF16)
     xb = lax.ppermute(jnp.where(role_even, first, last), "role", role_swaps[1])
     xa = lax.ppermute(jnp.where(role_even, last, first), "role", role_swaps[0])
-    v_in, p_in, row_mat, lane_mat, feat_mat, side_mat, index, x = call(
+    v_in, row_mat, lane_mat, feat_mat, side_mat, index, x = call(
         forward_first_kernel,
-        [((3, CX, CY, CZ), F32), ((ROWS, 128), F32), ((256, 256), BF16), ((512, 512), BF16), ((128, 128), BF16)]
+        [((3, CX, CY, CZ), F32), ((256, 256), BF16), ((512, 512), BF16), ((128, 128), BF16)]
         + [((TGT, 128), BF16), ((1, selected), jnp.int32), ((FEAT, NPATCH), BF16)],
-        [velocity, p2]
+        [velocity]
         + [jnp.asarray(m, BF16) for m in (row_matrix(), lane_matrix(), feature_matrix(), side_matrix())]
         + [patch_index.reshape(1, selected)],
         [],
         flops=1 << 28,
         name="forward_first",
-        sems=7,
+        sems=6,
         hbm_in=True,
     )
     xa, xb, v_in, x = lax.optimization_barrier((xa, xb, v_in, x))
@@ -540,7 +538,7 @@
     a1, d1, a2, d2, a3, d3, pred, *weights = call(
         forward_rest_kernel,
         [ACT, DER, ACT, DER, ACT, DER, ((TGT, NPATCH), F32)] + WEIGHTS,
-        [p_in, feat_mat, x],
+        [p2, feat_mat, x],
         [],
         flops=2 * 819200 * NPATCH,
         name="forward_rest",
@@ -617,7 +615,6 @@
     second_two = jnp.stack([second_moment, moments_other[1]])
     first_two = BETA_ONE * first_two + (1.0 - BETA_ONE) * grad
     second_two = BETA_TWO * second_two + (1.0 - BETA_TWO) * grad * grad
-    first_out, second_out = first_two[0], second_two[0]
     fix_first = 1.0 - BETA_ONE**ADAM_STEP
     fix_second = 1.0 - BETA_TWO**ADAM_STEP
     update = LEARN_RATE * (first_two / fix_first) / (jnp.sqrt(second_two / fix_second) + EPSILON)
@@ -627,7 +624,13 @@
     for step in range(steps - 2, 0, -1):
         if step == 2:
             held[0], fyb = fence((held[0], fyb))
+        if step == 1:
+            held[1], own_grad, own_first, own_second = fence((held[1], grad[0], first_moment, second_moment))
         got = [exchange(part, step) for part in held]
+        if step == 1:
+            first_out = BETA_ONE * own_first + (1.0 - BETA_ONE) * own_grad
+            second_out = BETA_TWO * own_second + (1.0 - BETA_TWO) * own_grad * own_grad
+            got[1], first_out, second_out = fence((got[1], first_out, second_out))
         if step == 2:
             fyb = lax.ppermute(fyb, "tile", tile_swaps[1])
         if step == 1:
@@ -644,7 +647,7 @@
     p_new, velocity_out, sgs_force = call(
         functools.partial(model_kernel, rows, masks, n_tile, in_order),
         [((ROWS, 128), F32)] + [((3, CX, CY, CZ), F32)] * 2,
-        [rank, p_in, *held, *other, flow, x_new, fxa, fxb, fya, fyb, row_mat, lane_mat, feat_mat, side_mat],
+        [rank, p2, *held, *other, flow, x_new, fxa, fxb, fya, fyb, row_mat, lane_mat, feat_mat, side_mat],
         [((ROWS, 128), F32)]
         + WEIGHTS
         + [((FEAT, 17 * 128), BF16), ((6, CX, CY, CZ), F32), ((2, 3, CY, CZ), F32), ((4, 48, 128), F32), ((3, CX, 80, CZ), F32)]

time: 79.4 us -> 79.2 us (level)
  starting transfers between devices: 23 us -> 24 us
  Pallas kernels: 23.1 us -> 22.2 us
    ppermute x1, waiting for transfers between devices: 1.66 us -> 0.01 us  [local(): fxb = lax.ppermute(fxb, 'role', role_swaps[1])]
    ppermute x14, waiting for transfers between devices: 26.2 us -> 27.5 us  [exchange(): return lax.ppermute(x, BOTH, pairs)]
    ppermute x1, starting transfers between devices: 1.03 us -> 1.95 us  [local(): fya = lax.ppermute(fya, 'tile', tile_swaps[0])]
    pallas_call x6, Pallas kernels: 23.1 us -> 22.2 us  [call(): pl.pallas_call(kernel, out_shape=[space[hbm_out](s, t) for s, t in outs],...]
  transfers between devices with their start and end apart: 22 -> 22, of which waited for: 12 -> 13; matrix products, arithmetic and copies ran while one was open for 3% -> 2% of each run, Pallas kernels for 10% -> 10%
where the time goes in v5:
time: 79.2 us; the launch traced here: 79.1 us
  waiting for transfers between devices  28.1 us (35%)
  starting transfers between devices  24 us (30%)
  Pallas kernels  22.2 us (28%)
  other arithmetic  2.79 us (4%)
  between operations  1.74 us (2%)
    ppermute x14, waiting for transfers between devices, exchange(): return lax.ppermute(x, BOTH, pairs)  27.5 us
    pallas_call x6, Pallas kernels, call(): pl.pallas_call(kernel, out_shape=[space[hbm_out](s, t) for s, t in outs],...  22.2 us
    ppermute x14, starting transfers between devices, exchange(): return lax.ppermute(x, BOTH, pairs)  10.3 us
    ppermute x1, starting transfers between devices, local(): yb = lax.ppermute(yb, 'tile', tile_swaps[1])  3.58 us
    ppermute x1, starting transfers between devices, local(): fyb = lax.ppermute(fyb, 'tile', tile_swaps[1])  3.44 us
    ppermute x1, starting transfers between devices, local(): xb = lax.ppermute(jnp.where(role_even, first, last), 'role', role_swaps[1])  2.64 us
    ppermute x1, starting transfers between devices, local(): fya = lax.ppermute(fya, 'tile', tile_swaps[0])  1.95 us
  transfers between devices with their start and end apart: 22, of which 13 were waited for; matrix products, arithmetic and copies ran while one was open for 2% of the time, Pallas kernels for 10%

profile of v5, /device:TPU:0, one launch (start us, length us, event | category | flops | bytes accessed | tf_op | source)
XLA Modules:
  0.0 79.1 jit_solution(7373956446807404232)
XLA Ops:
  0.7 1.3 %convert.4 = bf16[3,8,64,128]{3,2,1,0:T(8,128)(2,1)S(1)} convert(f32[3,8,64,128]{3,2,1,0:T(8,128)} %v_hbm.1) | non-fusion elementwise | flops 196608 | bytes 1179648 | tf_op jit(solution)/shard_map/convert.1
  2.6 2.6 %collective-permute-start.1 = (bf16[3,2,64,128]{3,2,1,0:T(8,128)(2,1)S(1)}, bf16[3,2,64,128]{3,2,1,0:T(8,128)(2,1)S(1)}, u32[]{:S(2)}, u32[]{:S(2)}) collective-permute-start(bf16[3,2,64,128]{3,2,1,0:T(8,128)(2,1)S(1)} %get-tuple-element.143), channel_id=1, source_target_pairs={{0,24},{8,16},{16,8},{24,0},{1,25},{9,17},{17,9},{25,1},{2,26},{10... | collective-permute-start | bytes 294920 | tf_op jit(solution)/shard_map/ppermute | solution.py:518
  5.9 1.9 %forward_first.1 = (f32[3,8,64,128]{3,2,1,0:T(8,128)S(1)}, bf16[256,256]{1,0:T(8,128)(2,1)S(1)}, bf16[512,512]{1,0:T(8,128)(2,1)S(1)}, bf16[128,128]{1,0:T(8,128...) custom-call(f32[3,8,64,128]{3,2,1,0:T(8,128)} %v_hbm.1, ...), custom_call_target="tpu_custom_call" | custom-call | flops 268435456 | bytes 3555328 | tf_op jit(solution)/shard_map/forward_first/pallas_call | solution.py:452
  8.3 1.5 %collective-permute-start.2 = (f32[3,12,2,128]{3,2,1,0:T(2,128)S(1)}, f32[3,12,2,128]{3,2,1,0:T(2,128)S(1)}, u32[]{:S(2)}, u32[]{:S(2)}) collective-permute-start(f32[3,12,2,128]{3,2,1,0:T(2,128)S(1)} %get-tuple-element.78), channel_id=1, source_target_pairs={{0,1},{1,0},{2,3},{3,2},{4,5},{5,4},{6,7},{7,6},{8,9},{9,8},{10,11... | collective-permute-start | bytes 110600 | tf_op jit(solution)/shard_map/ppermute | solution.py:537
  9.8 3.6 %collective-permute-start.3 = (f32[3,12,2,128]{3,2,1,0:T(2,128)S(1)}, f32[3,12,2,128]{3,2,1,0:T(2,128)S(1)}, u32[]{:S(2)}, u32[]{:S(2)}) collective-permute-start(f32[3,12,2,128]{3,2,1,0:T(2,128)S(1)} %get-tuple-element.79), channel_id=1, source_target_pairs={{0,7},{1,2},{2,1},{3,4},{4,3},{5,6},{6,5},{7,0},{8,15},{9,10},{10,... | collective-permute-start | bytes 110600 | tf_op jit(solution)/shard_map/ppermute | solution.py:536
  13.4 3.3 %forward_rest.1 = (bf16[512,1024]{1,0:T(8,128)(2,1)S(1)}, f32[512,1024]{1,0:T(8,128)S(1)}, bf16[512,1024]{1,0:T(8,128)(2,1)S(1)}, f32[512,1024]{1,0:T(8,128)S(1)...) custom-call(f32[6400,128]{1,0:T(8,128)S(1)} %bitcast.12, ...), custom_call_target="tpu_custom_call" | custom-call | flops 1677721600 | bytes 16351232 | tf_op jit(solution)/shard_map/forward_rest/pallas_call | solution.py:452
  16.7 6.7 %backward.1 = (bf16[16,200,128]{2,1,0:T(8,128)(2,1)S(1)}, f32[16,200,128]{2,1,0:T(8,128)S(1)}) custom-call(s32[1]{0:T(128)} %bitcast.rank_ref, s32[1]{0:T(128)S(6)} %copy.18.count_ref, s32[1,2048]{1,0:T(1,128)S(1)} %get-tuple-element.72.index_ref, f32[3,8,64,128]{3,2,1,0:T(8,128)S(1)} %get-tuple-element.97.v_ref, ...), custom_call_target="tpu_custom_call" | custom-call | flops 3355443200 | bytes 17055752 | tf_op jit(solution)/shard_map/backward/pallas_call | solution.py:452
  23.7 2.1 %collective-permute-done.4 = bf16[16,200,128]{2,1,0:T(8,128)(2,1)S(1)} collective-permute-done((bf16[16,200,128]{2,1,0:T(8,128)(2,1)S(1)}, bf16[16,200,128]{2,1,0:T(8,128)(2,1)S(1)}, u32[]{:S(2)}, u32[]{:S(2)}) %collective-permute-start.4) | collective-permute-done | bytes 819232 | tf_op jit(solution)/shard_map/ppermute | solution.py:501
  26.1 2.0 %collective-permute-start.7 = (f32[2,25600]{1,0:T(2,128)S(1)}, f32[2,25600]{1,0:T(2,128)S(1)}, u32[]{:S(2)}, u32[]{:S(2)}) collective-permute-start(f32[2,25600]{1,0:T(2,128)S(1)} %pad_maximum_fusion.1), channel_id=1, source_target_pairs={{0,4},{1,5},{2,6},{3,7},{4,0},{5,1},{6,2},{7,3},{8,12},{9,13},{10,... | collective-permute-start | bytes 614408 | tf_op jit(solution)/shard_map/ppermute | solution.py:501
  28.1 2.4 %flow.1 = (f32[3,8,64,128]{3,2,1,0:T(8,128)S(1)}, bf16[192,1024]{1,0:T(8,128)(2,1)S(1)}, bf16[192,512]{1,0:T(8,128)(2,1)S(1)}, bf16[192,512]{1,0:T(8,128)(2,1)S(...) custom-call(s32[1]{0:T(128)} %bitcast.rank_ref, f32[3,8,64,128]{3,2,1,0:T(8,128)S(1)} %get-tuple-element.97.v_ref, ...), custom_call_target="tpu_custom_call" | custom-call | flops 1073741824 | bytes 3383300 | tf_op jit(solution)/shard_map/flow/pallas_call | solution.py:452
  30.5 3.5 %collective-permute-done.5 = bf16[8,200,128]{2,1,0:T(8,128)(2,1)S(1)} collective-permute-done((bf16[8,200,128]{2,1,0:T(8,128)(2,1)S(1)}, bf16[8,200,128]{2,1,0:T(8,128)(2,1)S(1)}, u32[]{:S(2)}, u32[]{:S(2)}) %collective-permute-start.5) | collective-permute-done | bytes 409632 | tf_op jit(solution)/shard_map/ppermute | solution.py:501
  34.1 1.6 %collective-permute-start.6 = (bf16[4,200,128]{2,1,0:T(8,128)(2,1)S(1)}, bf16[4,200,128]{2,1,0:T(8,128)(2,1)S(1)}, u32[]{:S(2)}, u32[]{:S(2)}) collective-permute-start(bf16[4,200,128]{2,1,0:T(8,128)(2,1)S(1)} %get-tuple-element.142), channel_id=1, source_target_pairs={{0,16},{1,17},{2,18},{3,19},{4,20},{5,21},{6,22},{7,23},{8,9},{9,8... | collective-permute-start | bytes 614408 | tf_op jit(solution)/shard_map/ppermute | solution.py:501
  35.7 2.9 %collective-permute-done.7 = f32[2,25600]{1,0:T(2,128)S(1)} collective-permute-done((f32[2,25600]{1,0:T(2,128)S(1)}, f32[2,25600]{1,0:T(2,128)S(1)}, u32[]{:S(2)}, u32[]{:S(2)}) %collective-permute-start.7) | collective-permute-done | bytes 204832 | tf_op jit(solution)/shard_map/ppermute | solution.py:501
  40.1 4.6 %collective-permute-done.8 = bf16[2,200,128]{2,1,0:T(8,128)(2,1)S(1)} collective-permute-done((bf16[2,200,128]{2,1,0:T(8,128)(2,1)S(1)}, bf16[2,200,128]{2,1,0:T(8,128)(2,1)S(1)}, u32[]{:S(2)}, u32[]{:S(2)}) %collective-permute-start.8) | collective-permute-done | bytes 102432 | tf_op jit(solution)/shard_map/ppermute | solution.py:501
  45.5 2.0 %collective-permute-start.13 = (bf16[192,128]{1,0:T(8,128)(2,1)S(1)}, bf16[192,128]{1,0:T(8,128)(2,1)S(1)}, u32[]{:S(2)}, u32[]{:S(2)}) collective-permute-start(bf16[192,128]{1,0:T(8,128)(2,1)S(1)} %get-tuple-element.116), channel_id=1, source_target_pairs={{0,1},{1,0},{2,3},{3,2},{4,5},{5,4},{6,7},{7,6},{8,9},{9,8},{10,11... | collective-permute-start | bytes 147464 | tf_op jit(solution)/shard_map/ppermute | solution.py:611
  47.5 3.4 %collective-permute-done.9 = bf16[2,200,128]{2,1,0:T(8,128)(2,1)S(1)} collective-permute-done((bf16[2,200,128]{2,1,0:T(8,128)(2,1)S(1)}, bf16[2,200,128]{2,1,0:T(8,128)(2,1)S(1)}, u32[]{:S(2)}, u32[]{:S(2)}) %collective-permute-start.9) | collective-permute-done | bytes 102432 | tf_op jit(solution)/shard_map/ppermute | solution.py:501
  51.2 2.1 %collective-permute-start.11 = (bf16[2,96,128]{2,1,0:T(8,128)(2,1)S(1)}, bf16[2,96,128]{2,1,0:T(8,128)(2,1)S(1)}, u32[]{:S(2)}, u32[]{:S(2)}) collective-permute-start(bf16[2,96,128]{2,1,0:T(8,128)(2,1)S(1)} %slice.87), channel_id=1, source_target_pairs={{0,2},{1,3},{2,0},{3,1},{4,6},{5,7},{6,4},{7,5},{8,10},{9,11},{10,... | collective-permute-start | bytes 147464 | tf_op jit(solution)/shard_map/ppermute | solution.py:501
  53.2 2.0 %collective-permute-done.17 = bf16[2,104,128]{2,1,0:T(8,128)(2,1)S(1)} collective-permute-done((bf16[2,104,128]{2,1,0:T(8,128)(2,1)S(1)}, bf16[2,104,128]{2,1,0:T(8,128)(2,1)S(1)}, u32[]{:S(2)}, u32[]{:S(2)}) %collective-permute-start.17) | collective-permute-done | bytes 53280 | tf_op jit(solution)/shard_map/ppermute | solution.py:501
  55.3 1.6 %collective-permute-start.18 = (bf16[4,104,128]{2,1,0:T(8,128)(2,1)S(1)}, bf16[4,104,128]{2,1,0:T(8,128)(2,1)S(1)}, u32[]{:S(2)}, u32[]{:S(2)}) collective-permute-start(bf16[4,104,128]{2,1,0:T(8,128)(2,1)S(1)} %pad_maximum_fusion.3), channel_id=1, source_target_pairs={{0,16},{1,17},{2,18},{3,19},{4,20},{5,21},{6,22},{7,23},{8,9},{9,8... | collective-permute-start | bytes 319496 | tf_op jit(solution)/shard_map/ppermute | solution.py:501
  57.5 3.4 %collective-permute-start.16 = (bf16[192,128]{1,0:T(8,128)(2,1)S(1)}, bf16[192,128]{1,0:T(8,128)(2,1)S(1)}, u32[]{:S(2)}, u32[]{:S(2)}) collective-permute-start(bf16[192,128]{1,0:T(8,128)(2,1)S(1)} %get-tuple-element.120), channel_id=1, source_target_pairs={{0,7},{1,2},{2,1},{3,4},{4,3},{5,6},{6,5},{7,0},{8,15},{9,10},{10,... | collective-permute-start | bytes 147464 | tf_op jit(solution)/shard_map/ppermute | solution.py:635
  64.2 3.0 %collective-permute-done.19 = bf16[8,104,128]{2,1,0:T(8,128)(2,1)S(1)} collective-permute-done((bf16[8,104,128]{2,1,0:T(8,128)(2,1)S(1)}, bf16[8,104,128]{2,1,0:T(8,128)(2,1)S(1)}, u32[]{:S(2)}, u32[]{:S(2)}) %collective-permute-start.19) | collective-permute-done | bytes 213024 | tf_op jit(solution)/shard_map/ppermute | solution.py:501
  67.3 2.0 %collective-permute-done.15 = bf16[8,96,128]{2,1,0:T(8,128)(2,1)S(1)} collective-permute-done((bf16[8,96,128]{2,1,0:T(8,128)(2,1)S(1)}, bf16[8,96,128]{2,1,0:T(8,128)(2,1)S(1)}, u32[]{:S(2)}, u32[]{:S(2)}) %collective-permute-start.15) | collective-permute-done | bytes 196640 | tf_op jit(solution)/shard_map/ppermute | solution.py:501
  69.3 1.7 %collective-permute-done.20.other_a = bf16[16,96,128]{2,1,0:T(8,128)(2,1)S(1)} collective-permute-done((bf16[16,96,128]{2,1,0:T(8,128)(2,1)S(1)}, bf16[16,96,128]{2,1,0:T(8,128)(2,1)S(1)}, u32[]{:S(2)}, u32[]{:S(2)}) %collective-permute-start.20) | collective-permute-done | bytes 393248 | tf_op jit(solution)/shard_map/ppermute | solution.py:501
  71.1 7.9 %model.1 = (f32[6400,128]{1,0:T(8,128)}, f32[3,8,64,128]{3,2,1,0:T(8,128)}, f32[3,8,64,128]{3,2,1,0:T(8,128)}) custom-call(s32[1]{0:T(128)} %bitcast.rank_ref, f32[6400,128]{1,0:T(8,128)S(1)} %bitcast.13, bf16[16,96,128]{2,1,0:T(8,128)(2,1)S(1)} %constant_dynamic-update-slice_fusion.own_a, ...), custom_call_target="tpu_custom_call" | custom-call | flops 3355443200 | bytes 12222468 | tf_op jit(solution)/shard_map/model/pallas_call | solution.py:452
  (54 shorter events, 8.3 us)
Async XLA Ops:
  0.6 12.7 %copy-start = (f32[819200]{0:T(1024)S(1)}, f32[819200]{0:T(1024)}, u32[]{:S(2)}) copy-start(f32[819200]{0:T(1024)} %param.11) | copy-start | bytes 9830404
  2.1 5.7 %collective-permute-start = (bf16[3,2,64,128]{3,2,1,0:T(8,128)(2,1)S(1)}, bf16[3,2,64,128]{3,2,1,0:T(8,128)(2,1)S(1)}, u32[]{:S(2)}, u32[]{:S(2)}) collective-permute-start(bf16[3,2,64,128]{3,2,1,0:T(8,128)(2,1)S(1)} %get-tuple-element.144), channel_id=1, source_target_pairs={{0,8},{8,0},{16,24},{24,16},{1,9},{9,1},{17,25},{25,17},{2,10},{10... | collective-permute-start | bytes 294920 | tf_op jit(solution)/shard_map/ppermute | solution.py:519
  2.6 5.7 %collective-permute-start.1 = (bf16[3,2,64,128]{3,2,1,0:T(8,128)(2,1)S(1)}, bf16[3,2,64,128]{3,2,1,0:T(8,128)(2,1)S(1)}, u32[]{:S(2)}, u32[]{:S(2)}) collective-permute-start(bf16[3,2,64,128]{3,2,1,0:T(8,128)(2,1)S(1)} %get-tuple-element.143), channel_id=1, source_target_pairs={{0,24},{8,16},{16,8},{24,0},{1,25},{9,17},{17,9},{25,1},{2,26},{10... | collective-permute-start | bytes 294920 | tf_op jit(solution)/shard_map/ppermute | solution.py:518
  8.3 8.4 %collective-permute-start.2 = (f32[3,12,2,128]{3,2,1,0:T(2,128)S(1)}, f32[3,12,2,128]{3,2,1,0:T(2,128)S(1)}, u32[]{:S(2)}, u32[]{:S(2)}) collective-permute-start(f32[3,12,2,128]{3,2,1,0:T(2,128)S(1)} %get-tuple-element.78), channel_id=1, source_target_pairs={{0,1},{1,0},{2,3},{3,2},{4,5},{5,4},{6,7},{7,6},{8,9},{9,8},{10,11... | collective-permute-start | bytes 110600 | tf_op jit(solution)/shard_map/ppermute | solution.py:537
  9.8 6.9 %collective-permute-start.3 = (f32[3,12,2,128]{3,2,1,0:T(2,128)S(1)}, f32[3,12,2,128]{3,2,1,0:T(2,128)S(1)}, u32[]{:S(2)}, u32[]{:S(2)}) collective-permute-start(f32[3,12,2,128]{3,2,1,0:T(2,128)S(1)} %get-tuple-element.79), channel_id=1, source_target_pairs={{0,7},{1,2},{2,1},{3,4},{4,3},{5,6},{6,5},{7,0},{8,15},{9,10},{10,... | collective-permute-start | bytes 110600 | tf_op jit(solution)/shard_map/ppermute | solution.py:536
  16.7 6.8 %copy-start.2 = (f32[25600]{0:T(1024)S(1)}, f32[25600]{0:T(1024)}, u32[]{:S(2)}) copy-start(f32[25600]{0:T(1024)} %param.12) | copy-start | bytes 307204
  23.5 2.4 %collective-permute-start.4 = (bf16[16,200,128]{2,1,0:T(8,128)(2,1)S(1)}, bf16[16,200,128]{2,1,0:T(8,128)(2,1)S(1)}, u32[]{:S(2)}, u32[]{:S(2)}) collective-permute-start(bf16[16,200,128]{2,1,0:T(8,128)(2,1)S(1)} %get-tuple-element.95), channel_id=1, source_target_pairs={{0,8},{1,9},{2,10},{3,11},{4,12},{5,13},{6,14},{7,15},{8,0},{9,1},... | collective-permute-start | bytes 2457608 | tf_op jit(solution)/shard_map/ppermute | solution.py:501
  26.0 8.0 %collective-permute-start.5 = (bf16[8,200,128]{2,1,0:T(8,128)(2,1)S(1)}, bf16[8,200,128]{2,1,0:T(8,128)(2,1)S(1)}, u32[]{:S(2)}, u32[]{:S(2)}) collective-permute-start(bf16[8,200,128]{2,1,0:T(8,128)(2,1)S(1)} %get-tuple-element.96), channel_id=1, source_target_pairs={{0,1},{1,0},{2,3},{3,2},{4,5},{5,4},{6,7},{7,6},{8,24},{9,25},{10,... | collective-permute-start | bytes 1228808 | tf_op jit(solution)/shard_map/ppermute | solution.py:501
  26.1 12.5 %collective-permute-start.7 = (f32[2,25600]{1,0:T(2,128)S(1)}, f32[2,25600]{1,0:T(2,128)S(1)}, u32[]{:S(2)}, u32[]{:S(2)}) collective-permute-start(f32[2,25600]{1,0:T(2,128)S(1)} %pad_maximum_fusion.1), channel_id=1, source_target_pairs={{0,4},{1,5},{2,6},{3,7},{4,0},{5,1},{6,2},{7,3},{8,12},{9,13},{10,... | collective-permute-start | bytes 614408 | tf_op jit(solution)/shard_map/ppermute | solution.py:501
  34.1 5.8 %collective-permute-start.6 = (bf16[4,200,128]{2,1,0:T(8,128)(2,1)S(1)}, bf16[4,200,128]{2,1,0:T(8,128)(2,1)S(1)}, u32[]{:S(2)}, u32[]{:S(2)}) collective-permute-start(bf16[4,200,128]{2,1,0:T(8,128)(2,1)S(1)} %get-tuple-element.142), channel_id=1, source_target_pairs={{0,16},{1,17},{2,18},{3,19},{4,20},{5,21},{6,22},{7,23},{8,9},{9,8... | collective-permute-start | bytes 614408 | tf_op jit(solution)/shard_map/ppermute | solution.py:501
  39.9 4.7 %collective-permute-start.8 = (bf16[2,200,128]{2,1,0:T(8,128)(2,1)S(1)}, bf16[2,200,128]{2,1,0:T(8,128)(2,1)S(1)}, u32[]{:S(2)}, u32[]{:S(2)}) collective-permute-start(bf16[2,200,128]{2,1,0:T(8,128)(2,1)S(1)} %fusion.6), channel_id=1, source_target_pairs={{0,2},{1,3},{2,0},{3,1},{4,6},{5,7},{6,4},{7,5},{8,10},{9,11},{10,... | collective-permute-start | bytes 307208 | tf_op jit(solution)/shard_map/ppermute | solution.py:501
  40.0 7.5 %collective-permute-start.10 = (bf16[192,512]{1,0:T(8,128)(2,1)S(1)}, bf16[192,512]{1,0:T(8,128)(2,1)S(1)}, u32[]{:S(2)}, u32[]{:S(2)}) collective-permute-start(bf16[192,512]{1,0:T(8,128)(2,1)S(1)} %get-tuple-element.113), channel_id=1, source_target_pairs={{0,24},{8,16},{16,8},{24,0},{1,25},{9,17},{17,9},{25,1},{2,26},{10... | collective-permute-start | bytes 589832 | tf_op jit(solution)/shard_map/ppermute | solution.py:608
  44.7 6.2 %collective-permute-start.9 = (bf16[2,200,128]{2,1,0:T(8,128)(2,1)S(1)}, bf16[2,200,128]{2,1,0:T(8,128)(2,1)S(1)}, u32[]{:S(2)}, u32[]{:S(2)}) collective-permute-start(bf16[2,200,128]{2,1,0:T(8,128)(2,1)S(1)} %fusion.8), channel_id=1, source_target_pairs={{0,4},{1,5},{2,6},{3,7},{4,0},{5,1},{6,2},{7,3},{8,12},{9,13},{10,... | collective-permute-start | bytes 307208 | tf_op jit(solution)/shard_map/ppermute | solution.py:501
  45.4 11.4 %collective-permute-start.12 = (bf16[192,512]{1,0:T(8,128)(2,1)S(1)}, bf16[192,512]{1,0:T(8,128)(2,1)S(1)}, u32[]{:S(2)}, u32[]{:S(2)}) collective-permute-start(bf16[192,512]{1,0:T(8,128)(2,1)S(1)} %get-tuple-element.115), channel_id=1, source_target_pairs={{0,8},{8,0},{16,24},{24,16},{1,9},{9,1},{17,25},{25,17},{2,10},{10... | collective-permute-start | bytes 589832 | tf_op jit(solution)/shard_map/ppermute | solution.py:610
  45.5 11.4 %collective-permute-start.13 = (bf16[192,128]{1,0:T(8,128)(2,1)S(1)}, bf16[192,128]{1,0:T(8,128)(2,1)S(1)}, u32[]{:S(2)}, u32[]{:S(2)}) collective-permute-start(bf16[192,128]{1,0:T(8,128)(2,1)S(1)} %get-tuple-element.116), channel_id=1, source_target_pairs={{0,1},{1,0},{2,3},{3,2},{4,5},{5,4},{6,7},{7,6},{8,9},{9,8},{10,11... | collective-permute-start | bytes 147464 | tf_op jit(solution)/shard_map/ppermute | solution.py:611
  51.1 4.2 %collective-permute-start.17 = (bf16[2,104,128]{2,1,0:T(8,128)(2,1)S(1)}, bf16[2,104,128]{2,1,0:T(8,128)(2,1)S(1)}, u32[]{:S(2)}, u32[]{:S(2)}) collective-permute-start(bf16[2,104,128]{2,1,0:T(8,128)(2,1)S(1)} %slice.88), channel_id=1, source_target_pairs={{0,2},{1,3},{2,0},{3,1},{4,6},{5,7},{6,4},{7,5},{8,10},{9,11},{10,... | collective-permute-start | bytes 159752 | tf_op jit(solution)/shard_map/ppermute | solution.py:501
  51.2 5.7 %collective-permute-start.11 = (bf16[2,96,128]{2,1,0:T(8,128)(2,1)S(1)}, bf16[2,96,128]{2,1,0:T(8,128)(2,1)S(1)}, u32[]{:S(2)}, u32[]{:S(2)}) collective-permute-start(bf16[2,96,128]{2,1,0:T(8,128)(2,1)S(1)} %slice.87), channel_id=1, source_target_pairs={{0,2},{1,3},{2,0},{3,1},{4,6},{5,7},{6,4},{7,5},{8,10},{9,11},{10,... | collective-permute-start | bytes 147464 | tf_op jit(solution)/shard_map/ppermute | solution.py:501
  55.3 5.9 %collective-permute-start.18 = (bf16[4,104,128]{2,1,0:T(8,128)(2,1)S(1)}, bf16[4,104,128]{2,1,0:T(8,128)(2,1)S(1)}, u32[]{:S(2)}, u32[]{:S(2)}) collective-permute-start(bf16[4,104,128]{2,1,0:T(8,128)(2,1)S(1)} %pad_maximum_fusion.3), channel_id=1, source_target_pairs={{0,16},{1,17},{2,18},{3,19},{4,20},{5,21},{6,22},{7,23},{8,9},{9,8... | collective-permute-start | bytes 319496 | tf_op jit(solution)/shard_map/ppermute | solution.py:501
  56.9 6.4 %collective-permute-start.14 = (bf16[4,96,128]{2,1,0:T(8,128)(2,1)S(1)}, bf16[4,96,128]{2,1,0:T(8,128)(2,1)S(1)}, u32[]{:S(2)}, u32[]{:S(2)}) collective-permute-start(bf16[4,96,128]{2,1,0:T(8,128)(2,1)S(1)} %pad_maximum_fusion.4), channel_id=1, source_target_pairs={{0,16},{1,17},{2,18},{3,19},{4,20},{5,21},{6,22},{7,23},{8,9},{9,8... | collective-permute-start | bytes 294920 | tf_op jit(solution)/shard_map/ppermute | solution.py:501
  57.5 9.8 %collective-permute-start.16 = (bf16[192,128]{1,0:T(8,128)(2,1)S(1)}, bf16[192,128]{1,0:T(8,128)(2,1)S(1)}, u32[]{:S(2)}, u32[]{:S(2)}) collective-permute-start(bf16[192,128]{1,0:T(8,128)(2,1)S(1)} %get-tuple-element.120), channel_id=1, source_target_pairs={{0,7},{1,2},{2,1},{3,4},{4,3},{5,6},{6,5},{7,0},{8,15},{9,10},{10,... | collective-permute-start | bytes 147464 | tf_op jit(solution)/shard_map/ppermute | solution.py:635
  61.2 5.9 %collective-permute-start.19 = (bf16[8,104,128]{2,1,0:T(8,128)(2,1)S(1)}, bf16[8,104,128]{2,1,0:T(8,128)(2,1)S(1)}, u32[]{:S(2)}, u32[]{:S(2)}) collective-permute-start(bf16[8,104,128]{2,1,0:T(8,128)(2,1)S(1)} %pad_maximum_fusion), channel_id=1, source_target_pairs={{0,1},{1,0},{2,3},{3,2},{4,5},{5,4},{6,7},{7,6},{8,24},{9,25},{10,... | collective-permute-start | bytes 638984 | tf_op jit(solution)/shard_map/ppermute | solution.py:501
  63.3 5.9 %collective-permute-start.15 = (bf16[8,96,128]{2,1,0:T(8,128)(2,1)S(1)}, bf16[8,96,128]{2,1,0:T(8,128)(2,1)S(1)}, u32[]{:S(2)}, u32[]{:S(2)}) collective-permute-start(bf16[8,96,128]{2,1,0:T(8,128)(2,1)S(1)} %pad_maximum_fusion.2), channel_id=1, source_target_pairs={{0,1},{1,0},{2,3},{3,2},{4,5},{5,4},{6,7},{7,6},{8,24},{9,25},{10,... | collective-permute-start | bytes 589832 | tf_op jit(solution)/shard_map/ppermute | solution.py:501
  67.2 3.9 %collective-permute-start.21 = (bf16[16,104,128]{2,1,0:T(8,128)(2,1)S(1)}, bf16[16,104,128]{2,1,0:T(8,128)(2,1)S(1)}, u32[]{:S(2)}, u32[]{:S(2)}) collective-permute-start(bf16[16,104,128]{2,1,0:T(8,128)(2,1)S(1)} %constant_dynamic-update-slice_fusion.3.own_b), channel_id=1, source_target_pairs={{0,8},{1,9},{2,10},{3,11},{4,12},{5,13},{6,14},{7,15},{8,0},{9,1},... | collective-permute-start | bytes 1277960 | tf_op jit(solution)/shard_map/ppermute | solution.py:501
  69.3 1.8 %collective-permute-start.20 = (bf16[16,96,128]{2,1,0:T(8,128)(2,1)S(1)}, bf16[16,96,128]{2,1,0:T(8,128)(2,1)S(1)}, u32[]{:S(2)}, u32[]{:S(2)}) collective-permute-start(bf16[16,96,128]{2,1,0:T(8,128)(2,1)S(1)} %constant_dynamic-update-slice_fusion.own_a), channel_id=1, source_target_pairs={{0,8},{1,9},{2,10},{3,11},{4,12},{5,13},{6,14},{7,15},{8,0},{9,1},... | collective-permute-start | bytes 1179656 | tf_op jit(solution)/shard_map/ppermute | solution.py:501
  (1 other events, 6.8 us)

commit v6 on v5

--- a/solution.py
+++ b/solution.py
@@ -156,8 +156,8 @@
 
 
 def forward_first_kernel(
-    v_hbm, row_hbm, lane_hbm, feat_hbm, side_hbm, index_hbm,
-    v_out, row_out, lane_out, feat_out, side_out, index_out, x_out, sems
+    row_scale, count_ref, v_hbm, row_hbm, lane_hbm, feat_hbm, side_hbm, index_hbm,
+    v_out, row_out, lane_out, feat_out, side_out, index_out, weight_out, x_out, sems
 ):
     copies = [
         pltpu.make_async_copy(src, dst, sems.at[i])
@@ -172,6 +172,8 @@
     x_out[...] = cells_to_patches(velocity_blocks(v_out), row_out[...], lane_out[...], 3)
     for copy in copies[3:]:
         copy.wait()
+    weight = multiplicity(index_out, count_ref) * row_scale
+    weight_out[...] = jnp.concatenate([weight[q : q + 1] for q in range(8)], axis=1)
 
 
 def parity(rank_ref, n_tile):
@@ -271,14 +273,13 @@
     return dot_nt(left, right)
 
 
-def backward_kernel(row_scale, rows, masks, n_tile, in_order, rank_ref, count_ref, index_ref, v_ref, xa_ref, xb_ref, ya_ref, yb_ref, row_ref, lane_ref,
+def backward_kernel(rows, masks, n_tile, in_order, rank_ref, weight_ref, v_ref, xa_ref, xb_ref, ya_ref, yb_ref, row_ref, lane_ref,
                     feat_ref, w1, w2, wo, x_ref, a1_ref, a2_ref, a3_ref, d1_ref, d2_ref, d3_ref, pred_ref, *rest):
     if in_order:
         send_out, keep_out, pad, grads = rest
     else:
         grads, pad = rest
-    weight = multiplicity(index_ref, count_ref) * row_scale
-    weight = jnp.concatenate([weight[q : q + 1] for q in range(8)], axis=1)
+    weight = weight_ref[...]
     fill_padded(pad, rank_ref, n_tile, v_ref, xa_ref, xb_ref, ya_ref, yb_ref)
     target = cells_to_patches(stress_blocks(pad), row_ref[...], lane_ref[...], 6)
     error = ((pred_ref[...] - target.astype(F32)) * weight).astype(BF16)
@@ -517,16 +518,17 @@
     first, last = velocity[:, :2].astype(BF16), velocity[:, CX - 2 :].astype(BF16)
     xb = lax.ppermute(jnp.where(role_even, first, last), "role", role_swaps[1])
     xa = lax.ppermute(jnp.where(role_even, last, first), "role", role_swaps[0])
-    v_in, row_mat, lane_mat, feat_mat, side_mat, index, x = call(
-        forward_first_kernel,
+    v_in, row_mat, lane_mat, feat_mat, side_mat, _, weight, x = call(
+        functools.partial(forward_first_kernel, row_scale),
         [((3, CX, CY, CZ), F32), ((256, 256), BF16), ((512, 512), BF16), ((128, 128), BF16)]
-        + [((TGT, 128), BF16), ((1, selected), jnp.int32), ((FEAT, NPATCH), BF16)],
-        [velocity]
+        + [((TGT, 128), BF16), ((1, selected), jnp.int32), ((1, NPATCH), F32), ((FEAT, NPATCH), BF16)],
+        [patch_count, velocity]
         + [jnp.asarray(m, BF16) for m in (row_matrix(), lane_matrix(), feature_matrix(), side_matrix())]
         + [patch_index.reshape(1, selected)],
         [],
         flops=1 << 28,
         name="forward_first",
+        scalars=1,
         sems=6,
         hbm_in=True,
     )
@@ -547,15 +549,15 @@
 
     grad_outs = [((half, rows, 128), BF16), ((half, rows, 128), F32)] if in_order else [((ROWS, 128), F32)]
     grads = call(
-        functools.partial(backward_kernel, row_scale, rows, masks, n_tile, in_order),
+        functools.partial(backward_kernel, rows, masks, n_tile, in_order),
         grad_outs,
-        [rank, patch_count, index, v_in]
+        [rank, weight, v_in]
         + halos
         + [row_mat, lane_mat, feat_mat]
         + weights[1:]
         + [x, a1, a2, a3, d1, d2, d3, pred],
         [PADDED] + ([((ROWS, 128), F32)] if in_order else []),
-        scalars=2,
+        scalars=1,
         flops=4 * 819200 * NPATCH,
         name="backward",
     )

time: 79.2 us -> 79.3 us (level)
  transfers between devices with their start and end apart: 22 -> 22, of which waited for: 13 -> 12; matrix products, arithmetic and copies ran while one was open for 2% -> 2% of each run, Pallas kernels for 10% -> 10%
where the time goes in v6:
time: 79.3 us; the launch traced here: 79.1 us
  waiting for transfers between devices  28 us (35%)
  starting transfers between devices  23.7 us (30%)
  Pallas kernels  22.6 us (28%)
  other arithmetic  2.79 us (4%)
  between operations  1.75 us (2%)
    ppermute x14, waiting for transfers between devices, exchange(): return lax.ppermute(x, BOTH, pairs)  28 us
    pallas_call x6, Pallas kernels, call(): pl.pallas_call(kernel, out_shape=[space[hbm_out](s, t) for s, t in outs],...  22.6 us
    ppermute x14, starting transfers between devices, exchange(): return lax.ppermute(x, BOTH, pairs)  9.96 us
    ppermute x1, starting transfers between devices, local(): yb = lax.ppermute(yb, 'tile', tile_swaps[1])  3.57 us
    ppermute x1, starting transfers between devices, local(): fyb = lax.ppermute(fyb, 'tile', tile_swaps[1])  3.31 us
    ppermute x1, starting transfers between devices, local(): xb = lax.ppermute(jnp.where(role_even, first, last), 'role', role_swaps[1])  2.64 us
    ppermute x1, starting transfers between devices, local(): fya = lax.ppermute(fya, 'tile', tile_swaps[0])  1.95 us
  transfers between devices with their start and end apart: 22, of which 12 were waited for; matrix products, arithmetic and copies ran while one was open for 2% of the time, Pallas kernels for 10%

profile of v6, /device:TPU:0, one launch (start us, length us, event | category | flops | bytes accessed | tf_op | source)
XLA Modules:
  0.0 79.1 jit_solution(11091347555475857265)
XLA Ops:
  0.7 1.3 %convert.4 = bf16[3,8,64,128]{3,2,1,0:T(8,128)(2,1)S(1)} convert(f32[3,8,64,128]{3,2,1,0:T(8,128)} %v_hbm.1) | non-fusion elementwise | flops 196608 | bytes 1179648 | tf_op jit(solution)/shard_map/convert.1
  2.6 2.6 %collective-permute-start.1 = (bf16[3,2,64,128]{3,2,1,0:T(8,128)(2,1)S(1)}, bf16[3,2,64,128]{3,2,1,0:T(8,128)(2,1)S(1)}, u32[]{:S(2)}, u32[]{:S(2)}) collective-permute-start(bf16[3,2,64,128]{3,2,1,0:T(8,128)(2,1)S(1)} %get-tuple-element.143), channel_id=1, source_target_pairs={{0,24},{8,16},{16,8},{24,0},{1,25},{9,17},{17,9},{25,1},{2,26},{10... | collective-permute-start | bytes 294920 | tf_op jit(solution)/shard_map/ppermute | solution.py:519
  5.9 2.6 %forward_first.1 = (f32[3,8,64,128]{3,2,1,0:T(8,128)S(1)}, bf16[256,256]{1,0:T(8,128)(2,1)S(1)}, bf16[512,512]{1,0:T(8,128)(2,1)S(1)}, bf16[128,128]{1,0:T(8,128...) custom-call(s32[1]{0:T(128)S(6)} %copy.18.count_ref, ...), custom_call_target="tpu_custom_call" | custom-call | flops 268435456 | bytes 3559428 | tf_op jit(solution)/shard_map/forward_first/pallas_call | solution.py:453
  8.6 1.6 %collective-permute-start.2 = (f32[3,12,2,128]{3,2,1,0:T(2,128)S(1)}, f32[3,12,2,128]{3,2,1,0:T(2,128)S(1)}, u32[]{:S(2)}, u32[]{:S(2)}) collective-permute-start(f32[3,12,2,128]{3,2,1,0:T(2,128)S(1)} %get-tuple-element.78), channel_id=1, source_target_pairs={{0,1},{1,0},{2,3},{3,2},{4,5},{5,4},{6,7},{7,6},{8,9},{9,8},{10,11... | collective-permute-start | bytes 110600 | tf_op jit(solution)/shard_map/ppermute | solution.py:539
  10.1 3.6 %collective-permute-start.3 = (f32[3,12,2,128]{3,2,1,0:T(2,128)S(1)}, f32[3,12,2,128]{3,2,1,0:T(2,128)S(1)}, u32[]{:S(2)}, u32[]{:S(2)}) collective-permute-start(f32[3,12,2,128]{3,2,1,0:T(2,128)S(1)} %get-tuple-element.79), channel_id=1, source_target_pairs={{0,7},{1,2},{2,1},{3,4},{4,3},{5,6},{6,5},{7,0},{8,15},{9,10},{10,... | collective-permute-start | bytes 110600 | tf_op jit(solution)/shard_map/ppermute | solution.py:538
  13.7 3.3 %forward_rest.1 = (bf16[512,1024]{1,0:T(8,128)(2,1)S(1)}, f32[512,1024]{1,0:T(8,128)S(1)}, bf16[512,1024]{1,0:T(8,128)(2,1)S(1)}, f32[512,1024]{1,0:T(8,128)S(1)...) custom-call(f32[6400,128]{1,0:T(8,128)S(1)} %bitcast.12, ...), custom_call_target="tpu_custom_call" | custom-call | flops 1677721600 | bytes 16351232 | tf_op jit(solution)/shard_map/forward_rest/pallas_call | solution.py:453
  17.1 6.4 %backward.1 = (bf16[16,200,128]{2,1,0:T(8,128)(2,1)S(1)}, f32[16,200,128]{2,1,0:T(8,128)S(1)}) custom-call(s32[1]{0:T(128)} %bitcast.rank_ref, f32[1,1024]{1,0:T(1,128)S(1)} %get-tuple-element.72.weight_ref, f32[3,8,64,128]{3,2,1,0:T(8,128)S(1)} %get-tuple-element.97.v_ref, bf16[3,2,64,128]{3,2,1,0:T(8,128)(2,1)S(1)} %collective-permute-done.xa_ref, ...), custom_call_target="tpu_custom_call" | custom-call | flops 3355443200 | bytes 17051652 | tf_op jit(solution)/shard_map/backward/pallas_call | solution.py:453
  23.8 2.1 %collective-permute-done.4 = bf16[16,200,128]{2,1,0:T(8,128)(2,1)S(1)} collective-permute-done((bf16[16,200,128]{2,1,0:T(8,128)(2,1)S(1)}, bf16[16,200,128]{2,1,0:T(8,128)(2,1)S(1)}, u32[]{:S(2)}, u32[]{:S(2)}) %collective-permute-start.4) | collective-permute-done | bytes 819232 | tf_op jit(solution)/shard_map/ppermute | solution.py:502
  26.1 2.1 %collective-permute-start.7 = (f32[2,25600]{1,0:T(2,128)S(1)}, f32[2,25600]{1,0:T(2,128)S(1)}, u32[]{:S(2)}, u32[]{:S(2)}) collective-permute-start(f32[2,25600]{1,0:T(2,128)S(1)} %pad_maximum_fusion.1), channel_id=1, source_target_pairs={{0,4},{1,5},{2,6},{3,7},{4,0},{5,1},{6,2},{7,3},{8,12},{9,13},{10,... | collective-permute-start | bytes 614408 | tf_op jit(solution)/shard_map/ppermute | solution.py:502
  28.2 2.4 %flow.1 = (f32[3,8,64,128]{3,2,1,0:T(8,128)S(1)}, bf16[192,1024]{1,0:T(8,128)(2,1)S(1)}, bf16[192,512]{1,0:T(8,128)(2,1)S(1)}, bf16[192,512]{1,0:T(8,128)(2,1)S(...) custom-call(s32[1]{0:T(128)} %bitcast.rank_ref, f32[3,8,64,128]{3,2,1,0:T(8,128)S(1)} %get-tuple-element.97.v_ref, ...), custom_call_target="tpu_custom_call" | custom-call | flops 1073741824 | bytes 3383300 | tf_op jit(solution)/shard_map/flow/pallas_call | solution.py:453
  30.5 3.5 %collective-permute-done.5 = bf16[8,200,128]{2,1,0:T(8,128)(2,1)S(1)} collective-permute-done((bf16[8,200,128]{2,1,0:T(8,128)(2,1)S(1)}, bf16[8,200,128]{2,1,0:T(8,128)(2,1)S(1)}, u32[]{:S(2)}, u32[]{:S(2)}) %collective-permute-start.5) | collective-permute-done | bytes 409632 | tf_op jit(solution)/shard_map/ppermute | solution.py:502
  34.1 1.3 %collective-permute-start.6 = (bf16[4,200,128]{2,1,0:T(8,128)(2,1)S(1)}, bf16[4,200,128]{2,1,0:T(8,128)(2,1)S(1)}, u32[]{:S(2)}, u32[]{:S(2)}) collective-permute-start(bf16[4,200,128]{2,1,0:T(8,128)(2,1)S(1)} %get-tuple-element.142), channel_id=1, source_target_pairs={{0,16},{1,17},{2,18},{3,19},{4,20},{5,21},{6,22},{7,23},{8,9},{9,8... | collective-permute-start | bytes 614408 | tf_op jit(solution)/shard_map/ppermute | solution.py:502
  35.4 2.9 %collective-permute-done.7 = f32[2,25600]{1,0:T(2,128)S(1)} collective-permute-done((f32[2,25600]{1,0:T(2,128)S(1)}, f32[2,25600]{1,0:T(2,128)S(1)}, u32[]{:S(2)}, u32[]{:S(2)}) %collective-permute-start.7) | collective-permute-done | bytes 204832 | tf_op jit(solution)/shard_map/ppermute | solution.py:502
  38.3 1.6 %collective-permute-done.6 = bf16[4,200,128]{2,1,0:T(8,128)(2,1)S(1)} collective-permute-done((bf16[4,200,128]{2,1,0:T(8,128)(2,1)S(1)}, bf16[4,200,128]{2,1,0:T(8,128)(2,1)S(1)}, u32[]{:S(2)}, u32[]{:S(2)}) %collective-permute-start.6) | collective-permute-done | bytes 204832 | tf_op jit(solution)/shard_map/ppermute | solution.py:502
  40.1 4.6 %collective-permute-done.8 = bf16[2,200,128]{2,1,0:T(8,128)(2,1)S(1)} collective-permute-done((bf16[2,200,128]{2,1,0:T(8,128)(2,1)S(1)}, bf16[2,200,128]{2,1,0:T(8,128)(2,1)S(1)}, u32[]{:S(2)}, u32[]{:S(2)}) %collective-permute-start.8) | collective-permute-done | bytes 102432 | tf_op jit(solution)/shard_map/ppermute | solution.py:502
  45.6 2.0 %collective-permute-start.13 = (bf16[192,128]{1,0:T(8,128)(2,1)S(1)}, bf16[192,128]{1,0:T(8,128)(2,1)S(1)}, u32[]{:S(2)}, u32[]{:S(2)}) collective-permute-start(bf16[192,128]{1,0:T(8,128)(2,1)S(1)} %get-tuple-element.116), channel_id=1, source_target_pairs={{0,1},{1,0},{2,3},{3,2},{4,5},{5,4},{6,7},{7,6},{8,9},{9,8},{10,11... | collective-permute-start | bytes 147464 | tf_op jit(solution)/shard_map/ppermute | solution.py:613
  47.5 3.4 %collective-permute-done.9 = bf16[2,200,128]{2,1,0:T(8,128)(2,1)S(1)} collective-permute-done((bf16[2,200,128]{2,1,0:T(8,128)(2,1)S(1)}, bf16[2,200,128]{2,1,0:T(8,128)(2,1)S(1)}, u32[]{:S(2)}, u32[]{:S(2)}) %collective-permute-start.9) | collective-permute-done | bytes 102432 | tf_op jit(solution)/shard_map/ppermute | solution.py:502
  51.2 2.1 %collective-permute-start.11 = (bf16[2,96,128]{2,1,0:T(8,128)(2,1)S(1)}, bf16[2,96,128]{2,1,0:T(8,128)(2,1)S(1)}, u32[]{:S(2)}, u32[]{:S(2)}) collective-permute-start(bf16[2,96,128]{2,1,0:T(8,128)(2,1)S(1)} %slice.87), channel_id=1, source_target_pairs={{0,2},{1,3},{2,0},{3,1},{4,6},{5,7},{6,4},{7,5},{8,10},{9,11},{10,... | collective-permute-start | bytes 147464 | tf_op jit(solution)/shard_map/ppermute | solution.py:502
  53.3 2.0 %collective-permute-done.17 = bf16[2,104,128]{2,1,0:T(8,128)(2,1)S(1)} collective-permute-done((bf16[2,104,128]{2,1,0:T(8,128)(2,1)S(1)}, bf16[2,104,128]{2,1,0:T(8,128)(2,1)S(1)}, u32[]{:S(2)}, u32[]{:S(2)}) %collective-permute-start.17) | collective-permute-done | bytes 53280 | tf_op jit(solution)/shard_map/ppermute | solution.py:502
  57.5 3.3 %collective-permute-start.16 = (bf16[192,128]{1,0:T(8,128)(2,1)S(1)}, bf16[192,128]{1,0:T(8,128)(2,1)S(1)}, u32[]{:S(2)}, u32[]{:S(2)}) collective-permute-start(bf16[192,128]{1,0:T(8,128)(2,1)S(1)} %get-tuple-element.120), channel_id=1, source_target_pairs={{0,7},{1,2},{2,1},{3,4},{4,3},{5,6},{6,5},{7,0},{8,15},{9,10},{10,... | collective-permute-start | bytes 147464 | tf_op jit(solution)/shard_map/ppermute | solution.py:637
  64.2 3.0 %collective-permute-done.19 = bf16[8,104,128]{2,1,0:T(8,128)(2,1)S(1)} collective-permute-done((bf16[8,104,128]{2,1,0:T(8,128)(2,1)S(1)}, bf16[8,104,128]{2,1,0:T(8,128)(2,1)S(1)}, u32[]{:S(2)}, u32[]{:S(2)}) %collective-permute-start.19) | collective-permute-done | bytes 213024 | tf_op jit(solution)/shard_map/ppermute | solution.py:502
  67.3 2.0 %collective-permute-done.15 = bf16[8,96,128]{2,1,0:T(8,128)(2,1)S(1)} collective-permute-done((bf16[8,96,128]{2,1,0:T(8,128)(2,1)S(1)}, bf16[8,96,128]{2,1,0:T(8,128)(2,1)S(1)}, u32[]{:S(2)}, u32[]{:S(2)}) %collective-permute-start.15) | collective-permute-done | bytes 196640 | tf_op jit(solution)/shard_map/ppermute | solution.py:502
  69.4 1.7 %collective-permute-done.20.other_a = bf16[16,96,128]{2,1,0:T(8,128)(2,1)S(1)} collective-permute-done((bf16[16,96,128]{2,1,0:T(8,128)(2,1)S(1)}, bf16[16,96,128]{2,1,0:T(8,128)(2,1)S(1)}, u32[]{:S(2)}, u32[]{:S(2)}) %collective-permute-start.20) | collective-permute-done | bytes 393248 | tf_op jit(solution)/shard_map/ppermute | solution.py:502
  71.1 7.9 %model.1 = (f32[6400,128]{1,0:T(8,128)}, f32[3,8,64,128]{3,2,1,0:T(8,128)}, f32[3,8,64,128]{3,2,1,0:T(8,128)}) custom-call(s32[1]{0:T(128)} %bitcast.rank_ref, f32[6400,128]{1,0:T(8,128)S(1)} %bitcast.13, bf16[16,96,128]{2,1,0:T(8,128)(2,1)S(1)} %constant_dynamic-update-slice_fusion.own_a, ...), custom_call_target="tpu_custom_call" | custom-call | flops 3355443200 | bytes 12222468 | tf_op jit(solution)/shard_map/model/pallas_call | solution.py:453
  (54 shorter events, 8.2 us)
Async XLA Ops:
  0.6 13.1 %copy-start = (f32[819200]{0:T(1024)S(1)}, f32[819200]{0:T(1024)}, u32[]{:S(2)}) copy-start(f32[819200]{0:T(1024)} %param.11) | copy-start | bytes 9830404
  2.1 6.4 %collective-permute-start = (bf16[3,2,64,128]{3,2,1,0:T(8,128)(2,1)S(1)}, bf16[3,2,64,128]{3,2,1,0:T(8,128)(2,1)S(1)}, u32[]{:S(2)}, u32[]{:S(2)}) collective-permute-start(bf16[3,2,64,128]{3,2,1,0:T(8,128)(2,1)S(1)} %get-tuple-element.144), channel_id=1, source_target_pairs={{0,8},{8,0},{16,24},{24,16},{1,9},{9,1},{17,25},{25,17},{2,10},{10... | collective-permute-start | bytes 294920 | tf_op jit(solution)/shard_map/ppermute | solution.py:520
  2.6 5.9 %collective-permute-start.1 = (bf16[3,2,64,128]{3,2,1,0:T(8,128)(2,1)S(1)}, bf16[3,2,64,128]{3,2,1,0:T(8,128)(2,1)S(1)}, u32[]{:S(2)}, u32[]{:S(2)}) collective-permute-start(bf16[3,2,64,128]{3,2,1,0:T(8,128)(2,1)S(1)} %get-tuple-element.143), channel_id=1, source_target_pairs={{0,24},{8,16},{16,8},{24,0},{1,25},{9,17},{17,9},{25,1},{2,26},{10... | collective-permute-start | bytes 294920 | tf_op jit(solution)/shard_map/ppermute | solution.py:519
  8.6 8.5 %collective-permute-start.2 = (f32[3,12,2,128]{3,2,1,0:T(2,128)S(1)}, f32[3,12,2,128]{3,2,1,0:T(2,128)S(1)}, u32[]{:S(2)}, u32[]{:S(2)}) collective-permute-start(f32[3,12,2,128]{3,2,1,0:T(2,128)S(1)} %get-tuple-element.78), channel_id=1, source_target_pairs={{0,1},{1,0},{2,3},{3,2},{4,5},{5,4},{6,7},{7,6},{8,9},{9,8},{10,11... | collective-permute-start | bytes 110600 | tf_op jit(solution)/shard_map/ppermute | solution.py:539
  10.1 6.9 %collective-permute-start.3 = (f32[3,12,2,128]{3,2,1,0:T(2,128)S(1)}, f32[3,12,2,128]{3,2,1,0:T(2,128)S(1)}, u32[]{:S(2)}, u32[]{:S(2)}) collective-permute-start(f32[3,12,2,128]{3,2,1,0:T(2,128)S(1)} %get-tuple-element.79), channel_id=1, source_target_pairs={{0,7},{1,2},{2,1},{3,4},{4,3},{5,6},{6,5},{7,0},{8,15},{9,10},{10,... | collective-permute-start | bytes 110600 | tf_op jit(solution)/shard_map/ppermute | solution.py:538
  17.0 6.5 %copy-start.2 = (f32[25600]{0:T(1024)S(1)}, f32[25600]{0:T(1024)}, u32[]{:S(2)}) copy-start(f32[25600]{0:T(1024)} %param.12) | copy-start | bytes 307204
  23.5 2.4 %collective-permute-start.4 = (bf16[16,200,128]{2,1,0:T(8,128)(2,1)S(1)}, bf16[16,200,128]{2,1,0:T(8,128)(2,1)S(1)}, u32[]{:S(2)}, u32[]{:S(2)}) collective-permute-start(bf16[16,200,128]{2,1,0:T(8,128)(2,1)S(1)} %get-tuple-element.95), channel_id=1, source_target_pairs={{0,8},{1,9},{2,10},{3,11},{4,12},{5,13},{6,14},{7,15},{8,0},{9,1},... | collective-permute-start | bytes 2457608 | tf_op jit(solution)/shard_map/ppermute | solution.py:502
  26.0 8.0 %collective-permute-start.5 = (bf16[8,200,128]{2,1,0:T(8,128)(2,1)S(1)}, bf16[8,200,128]{2,1,0:T(8,128)(2,1)S(1)}, u32[]{:S(2)}, u32[]{:S(2)}) collective-permute-start(bf16[8,200,128]{2,1,0:T(8,128)(2,1)S(1)} %get-tuple-element.96), channel_id=1, source_target_pairs={{0,1},{1,0},{2,3},{3,2},{4,5},{5,4},{6,7},{7,6},{8,24},{9,25},{10,... | collective-permute-start | bytes 1228808 | tf_op jit(solution)/shard_map/ppermute | solution.py:502
  26.1 12.2 %collective-permute-start.7 = (f32[2,25600]{1,0:T(2,128)S(1)}, f32[2,25600]{1,0:T(2,128)S(1)}, u32[]{:S(2)}, u32[]{:S(2)}) collective-permute-start(f32[2,25600]{1,0:T(2,128)S(1)} %pad_maximum_fusion.1), channel_id=1, source_target_pairs={{0,4},{1,5},{2,6},{3,7},{4,0},{5,1},{6,2},{7,3},{8,12},{9,13},{10,... | collective-permute-start | bytes 614408 | tf_op jit(solution)/shard_map/ppermute | solution.py:502
  34.1 5.8 %collective-permute-start.6 = (bf16[4,200,128]{2,1,0:T(8,128)(2,1)S(1)}, bf16[4,200,128]{2,1,0:T(8,128)(2,1)S(1)}, u32[]{:S(2)}, u32[]{:S(2)}) collective-permute-start(bf16[4,200,128]{2,1,0:T(8,128)(2,1)S(1)} %get-tuple-element.142), channel_id=1, source_target_pairs={{0,16},{1,17},{2,18},{3,19},{4,20},{5,21},{6,22},{7,23},{8,9},{9,8... | collective-permute-start | bytes 614408 | tf_op jit(solution)/shard_map/ppermute | solution.py:502
  40.0 4.7 %collective-permute-start.8 = (bf16[2,200,128]{2,1,0:T(8,128)(2,1)S(1)}, bf16[2,200,128]{2,1,0:T(8,128)(2,1)S(1)}, u32[]{:S(2)}, u32[]{:S(2)}) collective-permute-start(bf16[2,200,128]{2,1,0:T(8,128)(2,1)S(1)} %fusion.6), channel_id=1, source_target_pairs={{0,2},{1,3},{2,0},{3,1},{4,6},{5,7},{6,4},{7,5},{8,10},{9,11},{10,... | collective-permute-start | bytes 307208 | tf_op jit(solution)/shard_map/ppermute | solution.py:502
  40.1 7.5 %collective-permute-start.10 = (bf16[192,512]{1,0:T(8,128)(2,1)S(1)}, bf16[192,512]{1,0:T(8,128)(2,1)S(1)}, u32[]{:S(2)}, u32[]{:S(2)}) collective-permute-start(bf16[192,512]{1,0:T(8,128)(2,1)S(1)} %get-tuple-element.113), channel_id=1, source_target_pairs={{0,24},{8,16},{16,8},{24,0},{1,25},{9,17},{17,9},{25,1},{2,26},{10... | collective-permute-start | bytes 589832 | tf_op jit(solution)/shard_map/ppermute | solution.py:610
  44.8 6.2 %collective-permute-start.9 = (bf16[2,200,128]{2,1,0:T(8,128)(2,1)S(1)}, bf16[2,200,128]{2,1,0:T(8,128)(2,1)S(1)}, u32[]{:S(2)}, u32[]{:S(2)}) collective-permute-start(bf16[2,200,128]{2,1,0:T(8,128)(2,1)S(1)} %fusion.8), channel_id=1, source_target_pairs={{0,4},{1,5},{2,6},{3,7},{4,0},{5,1},{6,2},{7,3},{8,12},{9,13},{10,... | collective-permute-start | bytes 307208 | tf_op jit(solution)/shard_map/ppermute | solution.py:502
  45.5 11.1 %collective-permute-start.12 = (bf16[192,512]{1,0:T(8,128)(2,1)S(1)}, bf16[192,512]{1,0:T(8,128)(2,1)S(1)}, u32[]{:S(2)}, u32[]{:S(2)}) collective-permute-start(bf16[192,512]{1,0:T(8,128)(2,1)S(1)} %get-tuple-element.115), channel_id=1, source_target_pairs={{0,8},{8,0},{16,24},{24,16},{1,9},{9,1},{17,25},{25,17},{2,10},{10... | collective-permute-start | bytes 589832 | tf_op jit(solution)/shard_map/ppermute | solution.py:612
  45.6 11.1 %collective-permute-start.13 = (bf16[192,128]{1,0:T(8,128)(2,1)S(1)}, bf16[192,128]{1,0:T(8,128)(2,1)S(1)}, u32[]{:S(2)}, u32[]{:S(2)}) collective-permute-start(bf16[192,128]{1,0:T(8,128)(2,1)S(1)} %get-tuple-element.116), channel_id=1, source_target_pairs={{0,1},{1,0},{2,3},{3,2},{4,5},{5,4},{6,7},{7,6},{8,9},{9,8},{10,11... | collective-permute-start | bytes 147464 | tf_op jit(solution)/shard_map/ppermute | solution.py:613
  51.1 4.2 %collective-permute-start.17 = (bf16[2,104,128]{2,1,0:T(8,128)(2,1)S(1)}, bf16[2,104,128]{2,1,0:T(8,128)(2,1)S(1)}, u32[]{:S(2)}, u32[]{:S(2)}) collective-permute-start(bf16[2,104,128]{2,1,0:T(8,128)(2,1)S(1)} %slice.88), channel_id=1, source_target_pairs={{0,2},{1,3},{2,0},{3,1},{4,6},{5,7},{6,4},{7,5},{8,10},{9,11},{10,... | collective-permute-start | bytes 159752 | tf_op jit(solution)/shard_map/ppermute | solution.py:502
  51.2 5.4 %collective-permute-start.11 = (bf16[2,96,128]{2,1,0:T(8,128)(2,1)S(1)}, bf16[2,96,128]{2,1,0:T(8,128)(2,1)S(1)}, u32[]{:S(2)}, u32[]{:S(2)}) collective-permute-start(bf16[2,96,128]{2,1,0:T(8,128)(2,1)S(1)} %slice.87), channel_id=1, source_target_pairs={{0,2},{1,3},{2,0},{3,1},{4,6},{5,7},{6,4},{7,5},{8,10},{9,11},{10,... | collective-permute-start | bytes 147464 | tf_op jit(solution)/shard_map/ppermute | solution.py:502
  55.3 5.9 %collective-permute-start.18 = (bf16[4,104,128]{2,1,0:T(8,128)(2,1)S(1)}, bf16[4,104,128]{2,1,0:T(8,128)(2,1)S(1)}, u32[]{:S(2)}, u32[]{:S(2)}) collective-permute-start(bf16[4,104,128]{2,1,0:T(8,128)(2,1)S(1)} %pad_maximum_fusion.3), channel_id=1, source_target_pairs={{0,16},{1,17},{2,18},{3,19},{4,20},{5,21},{6,22},{7,23},{8,9},{9,8... | collective-permute-start | bytes 319496 | tf_op jit(solution)/shard_map/ppermute | solution.py:502
  56.6 6.7 %collective-permute-start.14 = (bf16[4,96,128]{2,1,0:T(8,128)(2,1)S(1)}, bf16[4,96,128]{2,1,0:T(8,128)(2,1)S(1)}, u32[]{:S(2)}, u32[]{:S(2)}) collective-permute-start(bf16[4,96,128]{2,1,0:T(8,128)(2,1)S(1)} %pad_maximum_fusion.4), channel_id=1, source_target_pairs={{0,16},{1,17},{2,18},{3,19},{4,20},{5,21},{6,22},{7,23},{8,9},{9,8... | collective-permute-start | bytes 294920 | tf_op jit(solution)/shard_map/ppermute | solution.py:502
  57.5 9.8 %collective-permute-start.16 = (bf16[192,128]{1,0:T(8,128)(2,1)S(1)}, bf16[192,128]{1,0:T(8,128)(2,1)S(1)}, u32[]{:S(2)}, u32[]{:S(2)}) collective-permute-start(bf16[192,128]{1,0:T(8,128)(2,1)S(1)} %get-tuple-element.120), channel_id=1, source_target_pairs={{0,7},{1,2},{2,1},{3,4},{4,3},{5,6},{6,5},{7,0},{8,15},{9,10},{10,... | collective-permute-start | bytes 147464 | tf_op jit(solution)/shard_map/ppermute | solution.py:637
  61.3 5.9 %collective-permute-start.19 = (bf16[8,104,128]{2,1,0:T(8,128)(2,1)S(1)}, bf16[8,104,128]{2,1,0:T(8,128)(2,1)S(1)}, u32[]{:S(2)}, u32[]{:S(2)}) collective-permute-start(bf16[8,104,128]{2,1,0:T(8,128)(2,1)S(1)} %pad_maximum_fusion), channel_id=1, source_target_pairs={{0,1},{1,0},{2,3},{3,2},{4,5},{5,4},{6,7},{7,6},{8,24},{9,25},{10,... | collective-permute-start | bytes 638984 | tf_op jit(solution)/shard_map/ppermute | solution.py:502
  63.4 5.9 %collective-permute-start.15 = (bf16[8,96,128]{2,1,0:T(8,128)(2,1)S(1)}, bf16[8,96,128]{2,1,0:T(8,128)(2,1)S(1)}, u32[]{:S(2)}, u32[]{:S(2)}) collective-permute-start(bf16[8,96,128]{2,1,0:T(8,128)(2,1)S(1)} %pad_maximum_fusion.2), channel_id=1, source_target_pairs={{0,1},{1,0},{2,3},{3,2},{4,5},{5,4},{6,7},{7,6},{8,24},{9,25},{10,... | collective-permute-start | bytes 589832 | tf_op jit(solution)/shard_map/ppermute | solution.py:502
  67.2 3.9 %collective-permute-start.21 = (bf16[16,104,128]{2,1,0:T(8,128)(2,1)S(1)}, bf16[16,104,128]{2,1,0:T(8,128)(2,1)S(1)}, u32[]{:S(2)}, u32[]{:S(2)}) collective-permute-start(bf16[16,104,128]{2,1,0:T(8,128)(2,1)S(1)} %constant_dynamic-update-slice_fusion.3.own_b), channel_id=1, source_target_pairs={{0,8},{1,9},{2,10},{3,11},{4,12},{5,13},{6,14},{7,15},{8,0},{9,1},... | collective-permute-start | bytes 1277960 | tf_op jit(solution)/shard_map/ppermute | solution.py:502
  69.3 1.8 %collective-permute-start.20 = (bf16[16,96,128]{2,1,0:T(8,128)(2,1)S(1)}, bf16[16,96,128]{2,1,0:T(8,128)(2,1)S(1)}, u32[]{:S(2)}, u32[]{:S(2)}) collective-permute-start(bf16[16,96,128]{2,1,0:T(8,128)(2,1)S(1)} %constant_dynamic-update-slice_fusion.own_a), channel_id=1, source_target_pairs={{0,8},{1,9},{2,10},{3,11},{4,12},{5,13},{6,14},{7,15},{8,0},{9,1},... | collective-permute-start | bytes 1179656 | tf_op jit(solution)/shard_map/ppermute | solution.py:502
  (1 other events, 6.5 us)
